TPU v7x, 512 devices: a whole 4x4x16 slice. The times are simulated.
512 devices in a mesh: sa: 32 (over y, x, z_hi), tp: 16 (over z_lo, core).
Axes of the slice: x: 4, y: 4, z: 16 (z_hi: 2, z_lo: 8; z = z_hi * 8 + z_lo), core: 2. Of those that a mesh axis runs over, the one named last changes fastest.
Arguments:
- window: float32 [2, 2, 64, 32, 2048], P(None, None, 'sa', None, 'tp'), may hold values from -4 to 4
- damping: float32 [64, 32], P('sa'), may hold values from 0 to 1
- propagator: float32 [2, 32, 32], replicated, may hold values from -1 to 1, as said below
- coupling: float32 [32], replicated, may hold values from 0.5 to 1.5
Outputs:
- lesser_next: float32 [2, 64, 32, 2048], P(None, 'sa', None, 'tp')
Inputs may be any that keep to these rules, and one draw needn't show every extreme that they name: `propagator`: a unitary matrix.
All inputs are finite; a program needn't handle non-finite values.
Results may differ from a plain program's by a relative error of at most 0.0079.
Values may be sent and summed in bfloat16 or wider, within the bound.
No kernel may reach another device: no remote copies, remote signals or barrier semaphores. Data moves between devices by JAX's collectives and lax.ppermute only.
A program may use at most 64 MiB of HBM per device.

v0:
```python
import math

import jax
import jax.numpy as jnp
from jax import lax
from jax.sharding import Mesh
from jax.sharding import PartitionSpec as P

SA = ("sa_0", "sa_1", "sa_2")


highest = lax.Precision.HIGHEST


def laid_out(blocks, dim):
    dims = list(blocks.shape[1:])
    dims[dim] *= blocks.shape[0]
    return jnp.moveaxis(blocks, 0, dim).reshape(dims)


def from_everyone(shard, axis):
    peers = lax.axis_size(axis)
    return lax.all_to_all(
        jnp.broadcast_to(shard[None], (peers, *shard.shape)), axis, 0, 0, tiled=True
    )


def gather_directly(shard, axis, dim):
    return laid_out(from_everyone(shard, axis), dim)


def all_blocks(shard, axes, turns):
    blocks = shard
    for k in turns:
        blocks = lax.all_gather(blocks, axes[k])
    done = turns[::-1]
    back = [done.index(k) for k in range(len(axes))]
    blocks = blocks.transpose(*back, *range(len(axes), blocks.ndim))
    return blocks.reshape(-1, *shard.shape)


def whole_of(shard, axes, turns, dim):
    return laid_out(all_blocks(shard, axes, turns), dim)


def nothing_yet(shard, identity):
    return jax.tree.map(
        lambda a, e: jnp.broadcast_to(jnp.asarray(e, a.dtype), a.shape), shard, identity
    )


def gathered_once(shard, axis):
    leaves = jax.tree.leaves(shard)
    turns = sorted(range(len(leaves)), key=lambda k: -leaves[k].size)
    width = (1, *leaves[turns[0]].shape)[-1]
    lines = [
        jnp.pad(leaves[k].reshape(-1), (0, -leaves[k].size % width)).reshape(-1, width)
        for k in turns
    ]
    both, at, found = (lax.all_gather(jnp.concatenate(lines), axis), 0, {})
    for k, line in zip(turns, lines):
        share = both[:, at : at + len(line)].reshape(len(both), -1)
        found[k] = share[:, : leaves[k].size].reshape(-1, *leaves[k].shape)
        at += len(line)
    numbers = iter(range(len(leaves)))
    return jax.tree.map(lambda _: found[next(numbers)], shard)


def carried_in(shard, axes, combine, identity):
    before = start = nothing_yet(shard, identity)
    running = shard
    for axis in reversed(axes):
        peers, place = (lax.axis_size(axis), lax.axis_index(axis))
        pieces = gathered_once(running, axis)
        inside, running = (start, start)
        for k in range(peers):
            passed = k < place
            running = combine(running, jax.tree.map(lambda part: part[k], pieces))
            inside = jax.tree.map(lambda new, old: jnp.where(passed, new, old), running, inside)
        before = combine(inside, before)
    return before


def spectral_self_energy(occupied_correlator, greater, coupling, column_tiles):
    factor = jnp.tile(coupling[:, None] * coupling[None, :], (1, column_tiles))
    less_re, less_im = (occupied_correlator[0], occupied_correlator[1])
    great_re, great_im = (greater[0], greater[1])
    lsquare_re = less_re * less_re - less_im * less_im
    lsquare_im = 2.0 * less_re * less_im
    gsquare_re = great_re * great_re - great_im * great_im
    gsquare_im = 2.0 * great_re * great_im
    sless_re = -factor * (lsquare_re * great_re + lsquare_im * great_im)
    sless_im = -factor * (lsquare_im * great_re - lsquare_re * great_im)
    sgreat_re = -factor * (gsquare_re * less_re + gsquare_im * less_im)
    sgreat_im = -factor * (gsquare_im * less_re - gsquare_re * less_im)
    return jnp.stack([sgreat_re - sless_re, sgreat_im - sless_im]).astype(jnp.bfloat16)


def complex_product(left_re, left_im, right_re, right_im):
    cosine_component = jnp.dot(left_re, right_re, precision=highest) - jnp.dot(
        left_im, right_im, precision=highest
    )
    imag_part = jnp.dot(left_re, right_im, precision=highest) + jnp.dot(
        left_im, right_re, precision=highest
    )
    return (cosine_component, imag_part)


def propagate(forcing, damping, propagator, initial):

    def advance(state, inputs):
        damp_row, force_row = inputs
        cosine_component, imag_part = complex_product(
            propagator[0], propagator[1], state[0], state[1]
        )
        advanced = damp_row[None, :, None] * jnp.stack([cosine_component, imag_part]) + force_row
        return (advanced, advanced)

    last_state, produced = lax.scan(advance, initial, (damping, jnp.moveaxis(forcing, 1, 0)))
    return jnp.moveaxis(produced, 0, 1)


def combine(earlier, following):
    carry_re, carry_im = complex_product(following[0], following[1], earlier[0], earlier[1])
    shift_re, shift_im = complex_product(following[0], following[1], earlier[2], earlier[3])
    return (carry_re, carry_im, shift_re + following[2], shift_im + following[3])


def shards(window, damping, propagator, coupling):
    occupied_correlator = window[0]
    greater = window[1]
    orbitals = coupling.shape[0]
    block_rows = occupied_correlator.shape[1]
    column_entries = occupied_correlator.shape[3]
    column_tiles = column_entries // orbitals
    horizon = block_rows * lax.axis_size(SA)
    weight_scale = 1.0 / (horizon * math.sqrt(orbitals))
    position = lax.axis_index(SA)
    initial = occupied_correlator[:, 0]

    def collision(current):
        spectral = spectral_self_energy(current, greater, coupling, column_tiles)
        spectral_rows = gather_directly(spectral, "tp", 3)
        left_re = spectral_rows[0].reshape(block_rows * orbitals, -1)
        left_im = spectral_rows[1].reshape(block_rows * orbitals, -1)
        shard_piece = whole_of(current.astype(jnp.bfloat16), SA, (2, 0, 1), 1)
        span_rows = shard_piece.shape[1] * orbitals
        piece_re = shard_piece[0].reshape(span_rows, column_entries)
        piece_im = shard_piece[1].reshape(span_rows, column_entries)
        cosine_component = jnp.dot(left_re, piece_re, preferred_element_type=jnp.float32) - jnp.dot(
            left_im, piece_im, preferred_element_type=jnp.float32
        )
        imag_part = jnp.dot(left_re, piece_im, preferred_element_type=jnp.float32) + jnp.dot(
            left_im, piece_re, preferred_element_type=jnp.float32
        )
        return weight_scale * jnp.stack([cosine_component, imag_part]).reshape(current.shape)

    def advance_block(forcing):
        start_state = jnp.where(position == 0, initial, jnp.zeros_like(initial))
        unit_real = jnp.eye(orbitals, dtype=jnp.float32)
        unit_imag = jnp.zeros((orbitals, orbitals), jnp.float32)
        resting = jnp.zeros((2, block_rows, orbitals, orbitals), jnp.float32)
        carried = propagate(resting, damping, propagator, jnp.stack([unit_real, unit_imag]))[:, -1]
        offset_rows = propagate(forcing, damping, propagator, start_state)[:, -1]
        active = jnp.where(position == 0, 0.0, 1.0)
        element = (active * carried[0], active * carried[1], offset_rows[0], offset_rows[1])
        blank = jnp.zeros((orbitals, column_entries), jnp.float32)
        identity = (unit_real, unit_imag, blank, blank)
        prefix = carried_in(element, SA, combine, identity)
        incoming = jnp.where(position == 0, initial, jnp.stack([prefix[2], prefix[3]]))
        return propagate(forcing, damping, propagator, incoming)

    first_term = collision(occupied_correlator)
    predicted = advance_block(first_term)
    second_term = collision(predicted)
    return advance_block(0.5 * (first_term + second_term))


def solution(mesh):
    finer = Mesh(mesh.devices.reshape(4, 4, 2, mesh.shape["tp"]), ("sa_0", "sa_1", "sa_2", "tp"))
    placed = (P(None, None, SA, None, "tp"), P(SA, None), P(), P())
    return jax.shard_map(
        shards, mesh=finer, in_specs=placed, out_specs=P(None, SA, None, "tp"), check_vma=False
    )
```

profile of v0, /device:TPU:8, one launch (start us, length us, event | category | flops | bytes accessed | tf_op | source)
XLA Modules:
  0.0 281.0 jit_solution(16813482456472039905)
XLA Ops:
  6.5 0.8 slice-done
  7.4 16.4 %all_gather.70 = bf16[2,2,2,32,128]{4,3,2,1,0:T(8,128)(2,1)S(1)} all-gather(bf16[1,2,2,32,128]{4,3,2,1,0:T(8,128)(2,1)S(1)} %copy.38), channel_id=1, replica_groups=mesh['sa_0'=4,'sa_1'=4,'sa_2'=2,'tp'=16] {'sa_2'}, dimensions={0}, use_global_device_ids=true | all-gather | bytes 98304 | tf_op jit(solution)/shard_map/all_gather | solution.py:35
  23.7 13.5 %all-gather = bf16[8,2,2,32,128]{4,3,2,1,0:T(8,128)(2,1)} all-gather(bf16[2,2,2,32,128]{4,3,2,1,0:T(8,128)(2,1)S(1)} %all_gather.70), channel_id=2, replica_groups=mesh['sa_0'=4,'sa_1'=4,'sa_2'=2,'tp'=16] {'sa_0'}, dimensions={0}, use_global_device_ids=true | all-gather | bytes 327680 | tf_op jit(solution)/shard_map/all_gather | solution.py:35
  37.3 0.6 copy-done.5
  38.1 0.7 copy-done.4
  38.8 0.9 broadcast_in_dim.10
  39.8 9.3 %all-to-all-start = ((bf16[16,2,2,32,128]{4,3,2,1,0:T(8,128)(2,1)}), bf16[16,2,2,32,128]{4,3,2,1,0:T(8,128)(2,1)S(1)}, u32[]{:S(2)}, u32[]{:S(2)}) async-start(bf16[16,2,2,32,128]{4,3,2,1,0:T(8,128)(2,1)} %broadcast_in_dim.10), calls=%async_computation | async-start | bytes 1048576 | tf_op jit(solution)/shard_map/all_to_all | solution.py:23
  49.2 0.7 copy-done
  49.9 1.5 while.66
  51.6 0.6 copy-done.1
  52.2 17.9 %all-gather.14.cloned.1.call-done = bf16[16,2,2,2,32,128]{5,4,3,2,1,0:T(8,128)(2,1)} async-done(((bf16[4,2,2,2,32,128]{5,4,3,2,1,0:T(8,128)(2,1)}), bf16[16,2,2,2,32,128]{5,4,3,2,1,0:T(8,128)(2,1)}) %all-gather.14.cloned.1.call-update) | async-done | bytes 1048592 | tf_op jit(solution)/shard_map/all_gather | solution.py:35
  70.1 1.3 copy.39
  71.5 3.3 %all-to-all-done = bf16[16,2,2,32,128]{4,3,2,1,0:T(8,128)(2,1)S(1)} async-done(((bf16[16,2,2,32,128]{4,3,2,1,0:T(8,128)(2,1)}), bf16[16,2,2,32,128]{4,3,2,1,0:T(8,128)(2,1)S(1)}, u32[]{:S(2)}, u32[]{:S(2)}) %all-to-all-start) | async-done | bytes 524320 | tf_op jit(solution)/shard_map/all_to_all | solution.py:23
  76.1 0.7 copy-done.3
  76.9 1.5 while.65
  78.4 13.9 %all-gather.2 = f32[160,128]{1,0:T(8,128)S(1)} all-gather(f32[80,128]{1,0:T(8,128)S(1)} %pad_maximum_fusion.1), channel_id=4, replica_groups=mesh['sa_0'=4,'sa_1'=4,'sa_2'=2,'tp'=16] {'sa_2'}, dimensions={0}, use_global_device_ids=true | all-gather | bytes 122880 | tf_op jit(solution)/shard_map/all_gather | solution.py:60
  94.8 12.4 %all-gather.3 = f32[320,128]{1,0:T(8,128)S(1)} all-gather(f32[80,128]{1,0:T(8,128)S(1)} %pad_maximum_fusion.4), channel_id=5, replica_groups=mesh['sa_0'=4,'sa_1'=4,'sa_2'=2,'tp'=16] {'sa_1'}, dimensions={0}, use_global_device_ids=true | all-gather | bytes 204800 | tf_op jit(solution)/shard_map/all_gather | solution.py:60
  113.3 12.1 %all-gather.4 = f32[320,128]{1,0:T(8,128)S(1)} all-gather(f32[80,128]{1,0:T(8,128)S(1)} %pad_maximum_fusion.5), channel_id=6, replica_groups=mesh['sa_0'=4,'sa_1'=4,'sa_2'=2,'tp'=16] {'sa_0'}, dimensions={0}, use_global_device_ids=true | all-gather | bytes 204800 | tf_op jit(solution)/shard_map/all_gather | solution.py:60
  130.2 1.5 while.67
  131.8 0.9 broadcast_in_dim.11
  132.8 7.1 %all-to-all-start.1 = ((bf16[16,2,2,32,128]{4,3,2,1,0:T(8,128)(2,1)}), bf16[16,2,2,32,128]{4,3,2,1,0:T(8,128)(2,1)S(1)}, u32[]{:S(2)}, u32[]{:S(2)}) async-start(bf16[16,2,2,32,128]{4,3,2,1,0:T(8,128)(2,1)} %broadcast_in_dim.11), calls=%async_computation.1 | async-start | bytes 1048576 | tf_op jit(solution)/shard_map/all_to_all | solution.py:23
  140.0 20.4 %all-gather.5 = bf16[4,2,32,128]{3,2,0,1:T(8,128)(2,1)S(1)} all-gather(bf16[2,2,32,128]{3,2,0,1:T(8,128)(2,1)S(1)} %bitcast_convert_fusion), channel_id=7, replica_groups=mesh['sa_0'=4,'sa_1'=4,'sa_2'=2,'tp'=16] {'sa_2'}, dimensions={0}, use_global_device_ids=true | all-gather | bytes 98304 | tf_op jit(solution)/shard_map/all_gather | solution.py:35
  160.3 13.0 %all-gather.6 = bf16[8,2,2,32,128]{4,3,2,1,0:T(8,128)(2,1)} all-gather(bf16[2,2,2,32,128]{4,3,2,1,0:T(8,128)(2,1)S(1)} %bitcast.962), channel_id=8, replica_groups=mesh['sa_0'=4,'sa_1'=4,'sa_2'=2,'tp'=16] {'sa_0'}, dimensions={0}, use_global_device_ids=true | all-gather | bytes 327680 | tf_op jit(solution)/shard_map/all_gather | solution.py:35
  173.4 41.4 %all-gather.16.cloned.1.call-done = bf16[16,2,2,2,32,128]{5,4,3,2,1,0:T(8,128)(2,1)} async-done(((bf16[4,2,2,2,32,128]{5,4,3,2,1,0:T(8,128)(2,1)}), bf16[16,2,2,2,32,128]{5,4,3,2,1,0:T(8,128)(2,1)}) %all-gather.16.cloned.1.call-update) | async-done | bytes 1048592 | tf_op jit(solution)/shard_map/all_gather | solution.py:35
  214.9 1.3 copy.47
  217.6 0.7 copy-done.2
  218.4 1.5 while.68
  219.9 14.3 %all-gather.8 = f32[160,128]{1,0:T(8,128)S(1)} all-gather(f32[80,128]{1,0:T(8,128)S(1)} %pad_maximum_fusion), channel_id=10, replica_groups=mesh['sa_0'=4,'sa_1'=4,'sa_2'=2,'tp'=16] {'sa_2'}, dimensions={0}, use_global_device_ids=true | all-gather | bytes 122880 | tf_op jit(solution)/shard_map/all_gather | solution.py:60
  236.9 12.2 %all-gather.9 = f32[320,128]{1,0:T(8,128)S(1)} all-gather(f32[80,128]{1,0:T(8,128)S(1)} %pad_maximum_fusion.6), channel_id=11, replica_groups=mesh['sa_0'=4,'sa_1'=4,'sa_2'=2,'tp'=16] {'sa_1'}, dimensions={0}, use_global_device_ids=true | all-gather | bytes 204800 | tf_op jit(solution)/shard_map/all_gather | solution.py:60
  255.1 12.1 %all-gather.10 = f32[320,128]{1,0:T(8,128)S(1)} all-gather(f32[80,128]{1,0:T(8,128)S(1)} %pad_maximum_fusion.7), channel_id=12, replica_groups=mesh['sa_0'=4,'sa_1'=4,'sa_2'=2,'tp'=16] {'sa_0'}, dimensions={0}, use_global_device_ids=true | all-gather | bytes 204800 | tf_op jit(solution)/shard_map/all_gather | solution.py:60
  272.0 1.5 while.69
  273.5 0.6 copy-done.6
  (347 shorter events, 36.9 us)
Async XLA Ops:
  6.5 0.8 slice-start
  6.5 63.5 %all-gather.14.cloned.1.call-start = ((), (), s32[]{:S(2)}) async-start(), calls=%async_computation.2 | async-start | bytes 1310720 | tf_op jit(solution)/shard_map/all_gather | solution.py:35
  37.2 0.7 copy-start.5
  37.9 0.9 copy-start.4
  39.8 35.0 %all-to-all-start = ((bf16[16,2,2,32,128]{4,3,2,1,0:T(8,128)(2,1)}), bf16[16,2,2,32,128]{4,3,2,1,0:T(8,128)(2,1)S(1)}, u32[]{:S(2)}, u32[]{:S(2)}) async-start(bf16[16,2,2,32,128]{4,3,2,1,0:T(8,128)(2,1)} %broadcast_in_dim.10), calls=%async_computation | async-start | bytes 1048576 | tf_op jit(solution)/shard_map/all_to_all | solution.py:23
  49.1 0.8 copy-start
  49.1 0.7 copy-start.7
  51.5 0.6 copy-start.1
  76.1 0.8 copy-start.3
  132.8 83.5 %all-to-all-start.1 = ((bf16[16,2,2,32,128]{4,3,2,1,0:T(8,128)(2,1)}), bf16[16,2,2,32,128]{4,3,2,1,0:T(8,128)(2,1)S(1)}, u32[]{:S(2)}, u32[]{:S(2)}) async-start(bf16[16,2,2,32,128]{4,3,2,1,0:T(8,128)(2,1)} %broadcast_in_dim.11), calls=%async_computation.1 | async-start | bytes 1048576 | tf_op jit(solution)/shard_map/all_to_all | solution.py:23
  139.9 75.0 %all-gather.16.cloned.1.call-start = ((), (), s32[]{:S(2)}) async-start(), calls=%async_computation.3 | async-start | bytes 1310720 | tf_op jit(solution)/shard_map/all_gather | solution.py:35
  217.6 0.8 copy-start.2
  273.5 0.6 copy-start.6
Sparse Core Ops, SparseCore 0:
  37.4 32.6 all-gather.13
  173.5 41.2 all-gather.15
where the time goes:
time: 282 us; the launch traced here: 281 us
  blocking collectives  140 us (50%)
  waiting for transfers between devices  62.7 us (22%)
  matrix products  30.2 us (11%)
  starting transfers between devices  16.4 us (6%)
  local copies, waits for them, and re-layouts  14.9 us (5%)
  between operations  14.4 us (5%)
    all_gather x6, blocking collectives, gathered_once(): both, at, found = (lax.all_gather(jnp.concatenate(lines), axis), 0, {})  77 us
    all_gather x4, blocking collectives, all_blocks(): blocks = lax.all_gather(blocks, axes[k])  63.2 us
    all_gather x2, waiting for transfers between devices, all_blocks(): blocks = lax.all_gather(blocks, axes[k])  59.4 us
    all_to_all x2, starting transfers between devices, from_everyone(): lax.all_to_all(jnp.broadcast_to(shard[None], (peers, *shard.shape)), axis...  16.4 us
    dot_general x52, matrix products, complex_product(): jnp.dot(left_im, right_im, precision=highest)  7.79 us
    dot_general x52, matrix products, complex_product(): jnp.dot(left_re, right_re, precision=highest)  7.32 us
    dot_general x46, matrix products, complex_product(): jnp.dot(left_im, right_re, precision=highest)  6.95 us
    dot_general x46, matrix products, complex_product(): jnp.dot(left_re, right_im, precision=highest)  6.35 us
  transfers between devices with their start and end apart: 4, of which 3 were waited for; matrix products, arithmetic and copies ran while one was open for 2% of the time, Pallas kernels for 0%

commit v1 on v0

v1 whole, which is shorter than its diff:
```python
import functools
import math

import jax
import jax.numpy as jnp
from jax import lax
from jax.experimental import pallas as pl
from jax.experimental.pallas import tpu as pltpu
from jax.sharding import Mesh
from jax.sharding import PartitionSpec as P

FIRST = ("y", "x", "zh")
SECOND = ("zm", "zq", "c")
PLANE = ("y", "x")
f32, bf16 = jnp.float32, jnp.bfloat16
VMEM = pl.BlockSpec(memory_space=pltpu.VMEM)
SMEM = pl.BlockSpec(memory_space=pltpu.SMEM)


def from_everyone(shard, axis):
    peers = lax.axis_size(axis)
    return lax.all_to_all(
        jnp.broadcast_to(shard[None], (peers, *shard.shape)), axis, 0, 0, tiled=True
    )


def swapped(shard, axis):
    return lax.ppermute(shard, axis, [(0, 1), (1, 0)])


def in_order(own, other, axis):
    first = lax.axis_index(axis) == 0
    return jnp.stack([jnp.where(first, own, other), jnp.where(first, other, own)])


def spectral(less_re, less_im, great_re, great_im, factor):
    lsquare_re = less_re * less_re - less_im * less_im
    lsquare_im = 2.0 * less_re * less_im
    gsquare_re = great_re * great_re - great_im * great_im
    gsquare_im = 2.0 * great_re * great_im
    real = (lsquare_re * great_re + lsquare_im * great_im) - (
        gsquare_re * less_re + gsquare_im * less_im
    )
    imag = (lsquare_im * great_re - lsquare_re * great_im) - (
        gsquare_im * less_re - gsquare_re * less_im
    )
    return factor * real, factor * imag


def dot(left, right):
    return jnp.dot(left, right, preferred_element_type=f32)


def row_times_column(core, own_ref, other_ref, y_ref, heights, acc_ref):
    acc_ref[...] = jnp.zeros_like(acc_ref)

    def step(q, carry):
        for s_ref, side in ((own_ref, core), (other_ref, 1 - core)):
            left, right = [], []
            for m in range(2):
                if heights == 2:
                    left.append(s_ref[q, :, m].reshape(256, 128))
                else:
                    left.append(s_ref[q, m])
                j = 8 * m + 2 * q + side
                right.append(
                    jnp.concatenate(
                        [
                            y_ref[j, :, 0:64].reshape(128, 128),
                            y_ref[j, :, 64:128].reshape(128, 128),
                        ],
                        axis=1,
                    )
                )
            acc_ref[...] += dot(jnp.concatenate(left, axis=1), jnp.concatenate(right, axis=0))
        return carry

    lax.fori_loop(0, 4, step, 0)


def first_collision(scale, where_ref, own_ref, other_ref, y_ref, out_ref, acc_ref):
    row_times_column(where_ref[2], own_ref, other_ref, y_ref, 2, acc_ref)
    for h in range(2):
        top, low = acc_ref[h * 128 : h * 128 + 64], acc_ref[h * 128 + 64 : h * 128 + 128]
        out_ref[h, 0:64] = (scale * (top[:, :128] - low[:, 128:])).astype(bf16)
        out_ref[h, 64:128] = (scale * (top[:, 128:] + low[:, :128])).astype(bf16)


def last_collision(scale, where_ref, own_ref, other_ref, y_ref, base_ref, out_ref, acc_ref):
    row_times_column(where_ref[2], own_ref, other_ref, y_ref, 1, acc_ref)
    top, low = acc_ref[0:64], acc_ref[64:128]
    out_ref[0] = base_ref[0:64] + (0.5 * scale) * (top[:, :128] - low[:, 128:])
    out_ref[1] = base_ref[64:128] + (0.5 * scale) * (top[:, 128:] + low[:, :128])


def halves(x):
    high = x.astype(bf16)
    return high, (x - high.astype(f32)).astype(bf16)


def long_product(left, right):
    lh, ll = left
    rh, rl = halves(right)
    return dot(
        jnp.concatenate([lh, lh, ll, ll], axis=1), jnp.concatenate([rh, rl, rh, rl], axis=0)
    )


def embedded(z):
    return jnp.concatenate([z, jnp.concatenate([-z[32:], z[:32]], axis=0)], axis=1)


def put_unit(z, at):
    row = lax.broadcasted_iota(jnp.int32, z.shape, 0)
    lane = lax.broadcasted_iota(jnp.int32, z.shape, 1)
    unit = jnp.where((row == lane - 32 * at) & (row < 32), 1.0, 0.0)
    return jnp.where(lane >= 32 * at, unit, z)


def lanes_from_zero(z, last):
    moved = jnp.concatenate([z[:, 32:], z[:, :32]], axis=1)
    row = lax.broadcasted_iota(jnp.int32, z.shape, 0)
    lane = lax.broadcasted_iota(jnp.int32, z.shape, 1)
    tail = jnp.where(row == lane - 224, 1.0, 0.0) if last else jnp.zeros_like(z)
    return jnp.where(lane >= 224, tail, moved)


def build_steps(damp_ref, u_ref, p_ref, q_ref, pc_ref, hc_ref, z_ref):
    unitary = embedded(u_ref[...])
    high, low = halves(unitary)

    def store(k, i, z):
        wide = lanes_from_zero(z, i == 7).astype(bf16)
        top, under = wide[:32], wide[32:]
        p_ref[k, i * 32 : i * 32 + 32, 0:256] = top
        p_ref[k, i * 32 : i * 32 + 32, 256:512] = -under
        p_ref[k, 256 + i * 32 : 288 + i * 32, 0:256] = under
        p_ref[k, 256 + i * 32 : 288 + i * 32, 256:512] = top
        first = embedded(z[:, :32]).astype(bf16)
        q_ref[k, i * 32 : i * 32 + 32] = first[:32]
        q_ref[k, 256 + i * 32 : 288 + i * 32] = first[32:]

    for k in range(8):
        start = jnp.concatenate([u_ref[...], jnp.zeros((64, 224), f32)], axis=1)
        z = put_unit(damp_ref[:, 8 * k : 8 * k + 1] * start, 1)
        z_ref[k] = z
        store(k, 0, z)
    for i in range(1, 8):
        for k in range(8):
            t = 8 * k + i
            z = damp_ref[:, t : t + 1] * long_product((high, low), z_ref[k])
            if i < 7:
                z = put_unit(z, i + 1)
            z_ref[k] = z
            store(k, i, z)

    w = None
    for k in range(8):
        whole = z_ref[k][:, :32]
        if k == 0:
            w = put_unit(jnp.concatenate([whole, jnp.zeros((64, 224), f32)], axis=1), 1)
        else:
            w = long_product(halves(embedded(whole)), w)
            if k < 7:
                w = put_unit(w, k + 1)
        wide = lanes_from_zero(w, k == 7).astype(bf16)
        top, under = wide[:32], wide[32:]
        pc_ref[k * 64 : k * 64 + 32, 0:256] = top
        pc_ref[k * 64 : k * 64 + 32, 256:512] = -under
        pc_ref[k * 64 + 32 : k * 64 + 64, 0:256] = under
        pc_ref[k * 64 + 32 : k * 64 + 64, 256:512] = top
        hc_ref[k * 64 : k * 64 + 64] = embedded(w[:, :32]).astype(bf16)


def predict(
    where_ref, force_ref, lg_ref, factor_ref, p_ref, q_ref, pc_ref, hc_ref,
    y_ref, t_ref, base_ref,
    loc_ref, s_ref, ends_ref, carry_ref, hom_ref,
):
    j, h = where_ref[0], where_ref[1]
    own_block, own_start = j // 2, pl.multiple_of((j % 2) * 128 + h * 64, 64)

    def block_of(ref, k, start):
        return jnp.concatenate(
            [
                ref[2 * k + u // 2, u % 2, start + 64 * part : start + 64 * part + 64]
                for part in range(2)
                for u in range(4)
            ],
            axis=0,
        )

    def local(k, _):
        x = dot(p_ref[k], block_of(force_ref, k, 0))
        loc_ref[k] = x
        ends_ref[0, k] = x[224:256].astype(bf16)
        ends_ref[1, k] = x[480:512].astype(bf16)
        return 0

    lax.fori_loop(0, 8, local, 0)
    initial = jnp.concatenate([lg_ref[0, 0, 0:32], lg_ref[0, 0, 64:96]], axis=0)
    hom = dot(hc_ref[...], initial)
    carry = dot(pc_ref[...], ends_ref[...].reshape(512, 128)) + hom
    hom_ref[0] = initial
    carry_ref[0] = initial
    for k in range(7):
        hom_ref[k + 1] = hom[k * 64 : k * 64 + 64].astype(bf16)
        carry_ref[k + 1] = carry[k * 64 : k * 64 + 64].astype(bf16)
    factor = factor_ref[...]

    def whole(k, _):
        x = loc_ref[k] + dot(q_ref[k], carry_ref[k])
        loc_ref[k] = x
        g = block_of(lg_ref, k, 128).astype(f32)
        real, imag = spectral(x[:256], x[256:], g[:256], g[256:], factor)
        s = jnp.concatenate([real, imag], axis=0).astype(bf16)
        s_ref[k] = s
        y = x.astype(bf16)
        for u in range(4):
            for part in range(2):
                y_ref[2 * k + u // 2, u % 2, 64 * part : 64 * part + 64] = y[
                    256 * part + 64 * u : 256 * part + 64 * u + 64
                ]
        last = jnp.concatenate([p_ref[k, 224:256], p_ref[k, 480:512]], axis=0)
        end = dot(last, s).astype(bf16)
        ends_ref[0, k] = end[:32]
        ends_ref[1, k] = end[32:]
        return 0

    lax.fori_loop(0, 8, whole, 0)
    carry = dot(pc_ref[...], ends_ref[...].reshape(512, 128))
    carry_ref[0] = jnp.zeros((64, 128), bf16)
    for k in range(7):
        carry_ref[k + 1] = carry[k * 64 : k * 64 + 64].astype(bf16)

    low = pl.multiple_of(own_start + 256, 64)

    def own(ref):
        return jnp.concatenate(
            [ref[own_block, pl.ds(own_start, 64)], ref[own_block, pl.ds(low, 64)]], axis=0
        )

    q_own = own(q_ref)
    t_ref[...] = (
        dot(own(p_ref), s_ref[own_block]) + dot(q_own, carry_ref[own_block])
    ).astype(bf16)
    base_ref[...] = 0.5 * (own(loc_ref) + dot(q_own, hom_ref[own_block]))


def call(kernel, outs, scratch, ins, flops, moved):
    return pl.pallas_call(
        kernel,
        out_shape=outs,
        in_specs=ins,
        out_specs=jax.tree.map(lambda _: VMEM, outs),
        scratch_shapes=scratch,
        cost_estimate=pl.CostEstimate(flops=flops, bytes_accessed=moved, transcendentals=0),
    )


def shape(*dims, kind=bf16):
    return jax.ShapeDtypeStruct(dims, kind)


def shards(window, damping, propagator, coupling):
    orbitals = coupling.shape[0]
    horizon = damping.shape[0] * lax.axis_size(FIRST)
    scale = 1.0 / (horizon * math.sqrt(orbitals))
    factor = jnp.tile(coupling[:, None] * coupling[None, :], (8, 4))
    window = window.reshape(2, 2, 64, 128)
    less, great = window[0], window[1]
    where = jnp.stack(
        [lax.axis_index(PLANE), lax.axis_index("zh"), lax.axis_index("c")]
    ).astype(jnp.int32)

    real, imag = spectral(less[0], less[1], great[0], great[1], factor[:64])
    s1 = jnp.concatenate([real, imag]).astype(bf16)

    d0 = damping.reshape(1, 64)
    high = lax.reduce_precision(d0, 8, 7)
    rest = d0 - high
    mid = lax.reduce_precision(rest, 8, 7)
    tail = rest - mid
    rows = jnp.concatenate([high, mid, tail, jnp.zeros_like(d0)], axis=1).reshape(2, 128)
    message = jnp.concatenate(
        [less.reshape(128, 128), great.reshape(128, 128), jnp.pad(rows, ((0, 14), (0, 0)))]
    ).astype(bf16)
    pair = in_order(message, swapped(message, "zh"), "zh")
    lg = from_everyone(pair, PLANE)

    s_rows = from_everyone(s1, ("zh", "zm"))
    s_rows = from_everyone(s_rows, "zq")
    s_other = swapped(s_rows, "c")
    s_rows = s_rows.reshape(4, 2, 2, 128, 128)
    s_other = s_other.reshape(4, 2, 2, 128, 128)

    c1 = call(
        functools.partial(first_collision, scale),
        shape(2, 128, 128),
        [pltpu.VMEM((256, 256), f32)],
        [SMEM, VMEM, VMEM, VMEM],
        2 * 256 * 256 * 2048,
        4 << 20,
    )(where, s_rows, s_other, lg)
    force = from_everyone(c1, PLANE)

    parts = lg[:, :, 256:258].astype(f32).reshape(32, 4, 64)
    damp = (parts[:, 0] + (parts[:, 1] + parts[:, 2])).reshape(64, 32)
    damp = jnp.tile(damp.T, (2, 1))
    steps, inflow, coarse, start = call(
        build_steps,
        (shape(8, 512, 512), shape(8, 512, 64), shape(512, 512), shape(512, 64)),
        [pltpu.VMEM((8, 64, 256), f32)],
        [VMEM, VMEM],
        64 * 2 * 64 * 256 * 256,
        6 << 20,
    )(damp, propagator.reshape(64, 32))

    y2, t2, base = call(
        predict,
        (shape(16, 2, 128, 128), shape(128, 128), shape(128, 128, kind=f32)),
        [
            pltpu.VMEM((8, 512, 128), f32),
            pltpu.VMEM((8, 512, 128), bf16),
            pltpu.VMEM((2, 8, 32, 128), bf16),
            pltpu.VMEM((8, 64, 128), bf16),
            pltpu.VMEM((8, 64, 128), bf16),
        ],
        [SMEM] + [VMEM] * 7,
        2 * 8 * 512 * 512 * 128 * 2,
        10 << 20,
    )(where, force, lg, factor, steps, inflow, coarse, start)

    t_rows = from_everyone(t2, "zm")
    t_rows = from_everyone(t_rows, "zq")
    t_other = swapped(t_rows, "c")
    out = call(
        functools.partial(last_collision, scale),
        shape(2, 64, 128, kind=f32),
        [pltpu.VMEM((128, 256), f32)],
        [SMEM, VMEM, VMEM, VMEM, VMEM],
        2 * 128 * 256 * 2048,
        2 << 20,
    )(where, t_rows, t_other, y2, base)
    return out.reshape(2, 2, orbitals, 128)


def solution(mesh):
    finer = Mesh(mesh.devices.reshape(4, 4, 2, 2, 4, 2), (*FIRST, *SECOND))
    placed = (P(None, None, FIRST, None, SECOND), P(FIRST, None), P(), P())
    return jax.shard_map(
        shards, mesh=finer, in_specs=placed, out_specs=P(None, FIRST, None, SECOND), check_vma=False
    )
```

time: 282 us -> 166 us (0.59)
  the two profiles are of different devices: /device:TPU:8 before, /device:TPU:1 now
where the time goes in v1:
time: 166 us; the launch traced here: 165 us
  blocking collectives  49.3 us (30%)
  waiting for transfers between devices  43 us (26%)
  starting transfers between devices  33.7 us (20%)
  Pallas kernels  24.5 us (15%)
  local copies, waits for them, and re-layouts  11.8 us (7%)
  other arithmetic  2.51 us (2%)
    all_to_all x3, blocking collectives, from_everyone(): lax.all_to_all(jnp.broadcast_to(shard[None], (peers, *shard.shape)), axis...  49.3 us
    all_to_all x3, waiting for transfers between devices, from_everyone(): lax.all_to_all(jnp.broadcast_to(shard[None], (peers, *shard.shape)), axis...  30.3 us
    all_to_all x3, starting transfers between devices, from_everyone(): lax.all_to_all(jnp.broadcast_to(shard[None], (peers, *shard.shape)), axis...  18.7 us
    ppermute x3, starting transfers between devices, swapped(): return lax.ppermute(shard, axis, [(0, 1), (1, 0)])  15 us
    ppermute x3, waiting for transfers between devices, swapped(): return lax.ppermute(shard, axis, [(0, 1), (1, 0)])  12.7 us
    pallas_call x1, Pallas kernels, shards(): call(predict, (shape(16, 2, 128, 128), shape(128, 128), shape(128, 128, k...  10.6 us
    pallas_call x1, Pallas kernels, shards(): call(build_steps, (shape(8, 512, 512), shape(8, 512, 64), shape(512, 512)...  7.42 us
    broadcast_in_dim x6, local copies, waits for them, and re-layouts, from_everyone(): jnp.broadcast_to(shard[None], (peers, *shard.shape))  5.44 us
  transfers between devices with their start and end apart: 6, of which 5 were waited for; matrix products, arithmetic and copies ran while one was open for 2% of the time, Pallas kernels for 4%

profile of v1, /device:TPU:1, one launch (start us, length us, event | category | flops | bytes accessed | tf_op | source)
XLA Modules:
  0.0 165.0 jit_solution(17162623125724078687)
XLA Ops:
  0.0 0.8 broadcast_multiply_fusion
  0.9 0.8 fusion.16
  1.9 28.1 %all_to_all.30 = bf16[4,128,128]{2,1,0:T(8,128)(2,1)S(1)} all-to-all(bf16[4,128,128]{2,1,0:T(8,128)(2,1)S(1)} %broadcast_in_dim.14), channel_id=1, replica_groups=mesh['y'=4,'x'=4,'zh'=2,'zm'=2,'zq'=4,'c'=2] {'zh','zm'}, dimensions={0} | all-to-all | bytes 262144 | tf_op jit(solution)/shard_map/all_to_all | solution.py:22
  29.9 0.9 broadcast_in_dim.15
  30.9 3.9 %all-to-all-start.1 = ((bf16[4,4,128,128]{3,2,1,0:T(8,128)(2,1)}), bf16[4,4,128,128]{3,2,1,0:T(8,128)(2,1)S(1)}, u32[]{:S(2)}, u32[]{:S(2)}) async-start(bf16[4,4,128,128]{3,2,1,0:T(8,128)(2,1)} %broadcast_in_dim.15), calls=%async_computation.1 | async-start | bytes 1048576 | tf_op jit(solution)/shard_map/all_to_all | solution.py:22
  35.1 2.4 %collective-permute-start.1 = (bf16[272,128]{1,0:T(8,128)(2,1)S(1)}, bf16[272,128]{1,0:T(8,128)(2,1)S(1)}, u32[]{:S(2)}, u32[]{:S(2)}) collective-permute-start(bf16[272,128]{1,0:T(8,128)(2,1)S(1)} %fusion.1), channel_id=1, source_target_pairs={{0,16},{16,0},{1,17},{17,1},{2,18},{18,2},{3,19},{19,3},{4,20},{20... | collective-permute-start | bytes 208904 | tf_op jit(solution)/shard_map/ppermute | solution.py:28
  37.5 11.6 %collective-permute-done.1 = bf16[272,128]{1,0:T(8,128)(2,1)S(1)} collective-permute-done((bf16[272,128]{1,0:T(8,128)(2,1)S(1)}, bf16[272,128]{1,0:T(8,128)(2,1)S(1)}, u32[]{:S(2)}, u32[]{:S(2)}) %collective-permute-start.1) | collective-permute-done | bytes 69664 | tf_op jit(solution)/shard_map/ppermute | solution.py:28
  49.1 4.3 %all-to-all-done.1 = bf16[4,4,128,128]{3,2,1,0:T(8,128)(2,1)S(1)} async-done(((bf16[4,4,128,128]{3,2,1,0:T(8,128)(2,1)}), bf16[4,4,128,128]{3,2,1,0:T(8,128)(2,1)S(1)}, u32[]{:S(2)}, u32[]{:S(2)}) %all-to-all-start.1) | async-done | bytes 524320 | tf_op jit(solution)/shard_map/all_to_all | solution.py:22
  53.4 1.7 %broadcast_in_dim.17 = bf16[16,2,272,128]{3,2,1,0:T(8,128)(2,1)} broadcast(bf16[2,272,128]{2,1,0:T(8,128)(2,1)S(1)} %pad_maximum_fusion), dimensions={1,2,3} | broadcast | bytes 2367488 | tf_op jit(solution)/shard_map/broadcast_in_dim | solution.py:23
  55.1 6.8 %all-to-all-start.2 = ((bf16[16,2,272,128]{3,2,1,0:T(8,128)(2,1)}), bf16[16,2,272,128]{3,2,1,0:T(8,128)(2,1)S(1)}, u32[]{:S(2)}, u32[]{:S(2)}) async-start(bf16[16,2,272,128]{3,2,1,0:T(8,128)(2,1)} %broadcast_in_dim.17), calls=%async_computation.2 | async-start | bytes 4456448 | tf_op jit(solution)/shard_map/all_to_all | solution.py:22
  61.8 5.0 %collective-permute-start = (bf16[4,4,128,128]{3,2,1,0:T(8,128)(2,1)S(1)}, bf16[4,4,128,128]{3,2,1,0:T(8,128)(2,1)S(1)}, u32[]{:S(2)}, u32[]{:S(2)}) collective-permute-start(bf16[4,4,128,128]{3,2,1,0:T(8,128)(2,1)S(1)} %all-to-all-done.1), channel_id=1, source_target_pairs={{0,1},{1,0},{2,3},{3,2},{4,5},{5,4},{6,7},{7,6},{8,9},{9,8},{10,11... | collective-permute-start | bytes 1572872 | tf_op jit(solution)/shard_map/ppermute | solution.py:28
  66.8 0.6 pad_add_fusion.where_ref
  67.5 21.0 %all-to-all-done.2.y_ref.lg_ref = bf16[16,2,272,128]{3,2,1,0:T(8,128)(2,1)S(1)} async-done(((bf16[16,2,272,128]{3,2,1,0:T(8,128)(2,1)}), bf16[16,2,272,128]{3,2,1,0:T(8,128)(2,1)S(1)}, u32[]{:S(2)}, u32[]{:S(2)}) %all-to-all-start.2) | async-done | bytes 2228256 | tf_op jit(solution)/shard_map/all_to_all | solution.py:22
  88.4 1.4 copy-done
  89.8 0.2 copy-done.5
  90.0 3.6 %shard_map.46 = bf16[2,128,128]{2,1,0:T(8,128)(2,1)} custom-call(s32[3]{0:T(128)} %pad_add_fusion.where_ref, bf16[4,2,2,128,128]{4,3,2,1,0:T(8,128)(2,1)} %bitcast.117, bf16[4,2,2,128,128]{4,3,2,1,0:T(8,128)(2,1)} %bitcast.118, bf16[16,2,272,128]{3,2,1,0:T(8,128)(2,1)} %copy-done), custom_call_target="tpu_custom_call" | custom-call | flops 268435456 | bytes 4194304 | tf_op jit(solution)/shard_map/pallas_call | solution.py:297
  93.6 2.0 %broadcast_in_dim.18 = bf16[16,2,128,128]{3,2,1,0:T(8,128)(2,1)} broadcast(bf16[2,128,128]{2,1,0:T(8,128)(2,1)} %shard_map.46), dimensions={1,2,3} | broadcast | bytes 1114112 | tf_op jit(solution)/shard_map/broadcast_in_dim | solution.py:23
  95.6 8.1 %all-to-all-start.3 = ((bf16[16,2,128,128]{3,2,1,0:T(8,128)(2,1)}), bf16[16,2,128,128]{3,2,1,0:T(8,128)(2,1)S(1)}, u32[]{:S(2)}, u32[]{:S(2)}) async-start(bf16[16,2,128,128]{3,2,1,0:T(8,128)(2,1)} %broadcast_in_dim.18), calls=%async_computation.3 | async-start | bytes 2097152 | tf_op jit(solution)/shard_map/all_to_all | solution.py:22
  103.8 0.9 tile.9.factor_ref
  104.7 0.8 slice_convert_fusion
  105.8 0.6 tile.20
  106.5 7.4 %shard_map.47 = (bf16[8,512,512]{2,1,0:T(8,128)(2,1)}, bf16[8,512,64]{2,1,0:T(8,128)(2,1)}, bf16[512,512]{1,0:T(8,128)(2,1)}, bf16[512,64]{1,0:T(8,128)(2,1)}) custom-call(f32[64,64]{1,0:T(8,128)} %bitcast.127, f32[64,32]{1,0:T(8,128)} %bitcast.130), custom_call_target="tpu_custom_call" | custom-call | flops 536870912 | bytes 6291456 | tf_op jit(solution)/shard_map/pallas_call | solution.py:310
  113.9 5.1 %all-to-all-done.3.force_ref = bf16[16,2,128,128]{3,2,1,0:T(8,128)(2,1)S(1)} async-done(((bf16[16,2,128,128]{3,2,1,0:T(8,128)(2,1)}), bf16[16,2,128,128]{3,2,1,0:T(8,128)(2,1)S(1)}, u32[]{:S(2)}, u32[]{:S(2)}) %all-to-all-start.3) | async-done | bytes 1048608 | tf_op jit(solution)/shard_map/all_to_all | solution.py:22
  119.0 1.0 copy-done.1
  120.0 10.6 %shard_map.48 = (bf16[16,2,128,128]{3,2,1,0:T(8,128)(2,1)}, bf16[128,128]{1,0:T(8,128)(2,1)}, f32[128,128]{1,0:T(8,128)}) custom-call(s32[3]{0:T(128)} %pad_add_fusion.where_ref, bf16[16,2,128,128]{3,2,1,0:T(8,128)(2,1)} %copy-done.1, bf16[16,2,272,128]{3,2,1,0:T(8,128)(2,1)} %copy-done, f32[256,128]{1,0:T(8,128)} %tile.9.factor_ref, ...), custom_call_target="tpu_custom_call" | custom-call | flops 1073741824 | bytes 10485760 | tf_op jit(solution)/shard_map/pallas_call | solution.py:319
  130.6 0.8 broadcast_in_dim.19
  131.4 11.8 %all_to_all.31 = bf16[2,128,128]{2,1,0:T(8,128)(2,1)S(1)} all-to-all(bf16[2,128,128]{2,1,0:T(8,128)(2,1)S(1)} %broadcast_in_dim.19), channel_id=1, replica_groups=mesh['y'=4,'x'=4,'zh'=2,'zm'=2,'zq'=4,'c'=2] {'zm'}, dimensions={0} | all-to-all | bytes 131072 | tf_op jit(solution)/shard_map/all_to_all | solution.py:22
  143.3 9.4 %all_to_all.32.own_ref = bf16[4,2,128,128]{3,2,1,0:T(8,128)(2,1)S(1)} all-to-all(bf16[4,2,128,128]{3,2,1,0:T(8,128)(2,1)S(1)} %broadcast_in_dim.20), channel_id=1, replica_groups=mesh['y'=4,'x'=4,'zh'=2,'zm'=2,'zq'=4,'c'=2] {'zq'}, dimensions={0} | all-to-all | bytes 524288 | tf_op jit(solution)/shard_map/all_to_all | solution.py:22
  152.7 7.7 %collective-permute-start.2 = (bf16[4,2,128,128]{3,2,1,0:T(8,128)(2,1)S(1)}, bf16[4,2,128,128]{3,2,1,0:T(8,128)(2,1)S(1)}, u32[]{:S(2)}, u32[]{:S(2)}) collective-permute-start(bf16[4,2,128,128]{3,2,1,0:T(8,128)(2,1)S(1)} %all_to_all.32.own_ref), channel_id=1, source_target_pairs={{0,1},{1,0},{2,3},{3,2},{4,5},{5,4},{6,7},{7,6},{8,9},{9,8},{10,11... | collective-permute-start | bytes 786440 | tf_op jit(solution)/shard_map/ppermute | solution.py:28
  160.4 1.1 collective-permute-done.2.other_ref
  161.5 0.7 copy-done.6
  162.2 2.8 %shard_map.49 = f32[2,64,128]{2,1,0:T(8,128)} custom-call(s32[3]{0:T(128)} %pad_add_fusion.where_ref, bf16[4,2,128,128]{3,2,1,0:T(8,128)(2,1)} %copy-done.3, bf16[4,2,128,128]{3,2,1,0:T(8,128)(2,1)} %copy-done.6, bf16[16,2,128,128]{3,2,1,0:T(8,128)(2,1)} %get-tuple-element.17.y_ref, f32[128,128]{1,0:T(8,128)} %get-tuple-element.18.base_ref), custom_call_target="tpu_custom_call" | custom-call | flops 134217728 | bytes 2097152 | tf_op jit(solution)/shard_map/pallas_call | solution.py:337
  (35 shorter events, 1.0 us)
Async XLA Ops:
  0.0 34.7 %copy-start.4 = (f32[2,2,2,32,128]{4,3,2,1,0:T(8,128)S(1)}, f32[2,2,2,32,128]{4,3,2,1,0:T(8,128)}, u32[]{:S(2)}) copy-start(f32[2,2,2,32,128]{4,3,2,1,0:T(8,128)} %param.4) | copy-start | bytes 393220
  0.0 34.8 %copy-start.7 = (f32[2,32]{1,0:T(2,128)S(1)}, f32[2,32]{1,0:T(2,128)}, u32[]{:S(2)}) copy-start(f32[2,32]{1,0:T(2,128)} %param.5) | copy-start | bytes 772
  30.9 22.5 %all-to-all-start.1 = ((bf16[4,4,128,128]{3,2,1,0:T(8,128)(2,1)}), bf16[4,4,128,128]{3,2,1,0:T(8,128)(2,1)S(1)}, u32[]{:S(2)}, u32[]{:S(2)}) async-start(bf16[4,4,128,128]{3,2,1,0:T(8,128)(2,1)} %broadcast_in_dim.15), calls=%async_computation.1 | async-start | bytes 1048576 | tf_op jit(solution)/shard_map/all_to_all | solution.py:22
  35.1 14.0 %collective-permute-start.1 = (bf16[272,128]{1,0:T(8,128)(2,1)S(1)}, bf16[272,128]{1,0:T(8,128)(2,1)S(1)}, u32[]{:S(2)}, u32[]{:S(2)}) collective-permute-start(bf16[272,128]{1,0:T(8,128)(2,1)S(1)} %fusion.1), channel_id=1, source_target_pairs={{0,16},{16,0},{1,17},{17,1},{2,18},{18,2},{3,19},{19,3},{4,20},{20... | collective-permute-start | bytes 208904 | tf_op jit(solution)/shard_map/ppermute | solution.py:28
  53.4 8.4 %copy-start.2 = (bf16[4,4,128,128]{3,2,1,0:T(8,128)(2,1)}, bf16[4,4,128,128]{3,2,1,0:T(8,128)(2,1)S(1)}, u32[]{:S(2)}) copy-start(bf16[4,4,128,128]{3,2,1,0:T(8,128)(2,1)S(1)} %all-to-all-done.1) | copy-start | bytes 1572868
  55.1 33.4 %all-to-all-start.2 = ((bf16[16,2,272,128]{3,2,1,0:T(8,128)(2,1)}), bf16[16,2,272,128]{3,2,1,0:T(8,128)(2,1)S(1)}, u32[]{:S(2)}, u32[]{:S(2)}) async-start(bf16[16,2,272,128]{3,2,1,0:T(8,128)(2,1)} %broadcast_in_dim.17), calls=%async_computation.2 | async-start | bytes 4456448 | tf_op jit(solution)/shard_map/all_to_all | solution.py:22
  61.8 26.6 %collective-permute-start = (bf16[4,4,128,128]{3,2,1,0:T(8,128)(2,1)S(1)}, bf16[4,4,128,128]{3,2,1,0:T(8,128)(2,1)S(1)}, u32[]{:S(2)}, u32[]{:S(2)}) collective-permute-start(bf16[4,4,128,128]{3,2,1,0:T(8,128)(2,1)S(1)} %all-to-all-done.1), channel_id=1, source_target_pairs={{0,1},{1,0},{2,3},{3,2},{4,5},{5,4},{6,7},{7,6},{8,9},{9,8},{10,11... | collective-permute-start | bytes 1572872 | tf_op jit(solution)/shard_map/ppermute | solution.py:28
  88.4 1.4 copy-start
  88.4 1.6 copy-start.5
  95.6 23.3 %all-to-all-start.3 = ((bf16[16,2,128,128]{3,2,1,0:T(8,128)(2,1)}), bf16[16,2,128,128]{3,2,1,0:T(8,128)(2,1)S(1)}, u32[]{:S(2)}, u32[]{:S(2)}) async-start(bf16[16,2,128,128]{3,2,1,0:T(8,128)(2,1)} %broadcast_in_dim.18), calls=%async_computation.3 | async-start | bytes 2097152 | tf_op jit(solution)/shard_map/all_to_all | solution.py:22
  119.0 1.0 copy-start.1
  152.7 8.8 %copy-start.3 = (bf16[4,2,128,128]{3,2,1,0:T(8,128)(2,1)}, bf16[4,2,128,128]{3,2,1,0:T(8,128)(2,1)S(1)}, u32[]{:S(2)}) copy-start(bf16[4,2,128,128]{3,2,1,0:T(8,128)(2,1)S(1)} %all_to_all.32.own_ref) | copy-start | bytes 786436
  152.7 8.8 %collective-permute-start.2 = (bf16[4,2,128,128]{3,2,1,0:T(8,128)(2,1)S(1)}, bf16[4,2,128,128]{3,2,1,0:T(8,128)(2,1)S(1)}, u32[]{:S(2)}, u32[]{:S(2)}) collective-permute-start(bf16[4,2,128,128]{3,2,1,0:T(8,128)(2,1)S(1)} %all_to_all.32.own_ref), channel_id=1, source_target_pairs={{0,1},{1,0},{2,3},{3,2},{4,5},{5,4},{6,7},{7,6},{8,9},{9,8},{10,11... | collective-permute-start | bytes 786440 | tf_op jit(solution)/shard_map/ppermute | solution.py:28
  161.5 0.7 copy-start.6

commit v2 on v1

v2 whole, which is shorter than its diff:
```python
import functools
import math

import jax
import jax.numpy as jnp
from jax import lax
from jax.experimental import pallas as pl
from jax.experimental.pallas import tpu as pltpu
from jax.sharding import Mesh
from jax.sharding import PartitionSpec as P

FIRST = ("y", "x", "zh")
SECOND = ("zm", "zq", "c")
PLANE = ("y", "x")
f32, bf16 = jnp.float32, jnp.bfloat16
VMEM = pl.BlockSpec(memory_space=pltpu.VMEM)
SMEM = pl.BlockSpec(memory_space=pltpu.SMEM)


def from_everyone(shard, axis):
    peers = lax.axis_size(axis)
    return lax.all_to_all(
        jnp.broadcast_to(shard[None], (peers, *shard.shape)), axis, 0, 0, tiled=True
    )


def crossed(shard, axis, other):
    peers = lax.axis_size(axis)
    return lax.ppermute(shard, axis, [(k, k ^ other) for k in range(peers)])


def swapped(shard, axis):
    return crossed(shard, axis, 1)


def in_order(own, other, axis):
    first = lax.axis_index(axis) == 0
    return jnp.stack([jnp.where(first, own, other), jnp.where(first, other, own)])


def spectral(less_re, less_im, great_re, great_im, factor):
    lsquare_re = less_re * less_re - less_im * less_im
    lsquare_im = 2.0 * less_re * less_im
    gsquare_re = great_re * great_re - great_im * great_im
    gsquare_im = 2.0 * great_re * great_im
    real = (lsquare_re * great_re + lsquare_im * great_im) - (
        gsquare_re * less_re + gsquare_im * less_im
    )
    imag = (lsquare_im * great_re - lsquare_re * great_im) - (
        gsquare_im * less_re - gsquare_re * less_im
    )
    return factor * real, factor * imag


def dot(left, right):
    return jnp.dot(left, right, preferred_element_type=f32)


def row_times_column(pieces, y_ref, acc_ref):
    for n, (left, blocks) in enumerate(pieces):
        right = [
            jnp.concatenate(
                [y_ref[j, :, 0:64].reshape(128, 128), y_ref[j, :, 64:128].reshape(128, 128)],
                axis=1,
            )
            for j in blocks
        ]
        part = dot(jnp.concatenate(left, axis=1), jnp.concatenate(right, axis=0))
        if n == 0:
            acc_ref[...] = part
        else:
            acc_ref[...] += part


def first_collision(scale, where_ref, own_ref, other_ref, y_ref, out_ref, acc_ref):
    zm, zq, core = where_ref[2], where_ref[3], where_ref[4]
    pieces = [
        (
            [s_ref[d, e].reshape(256, 128) for e in range(2)],
            [8 * (zm ^ e) + 2 * (zq ^ d) + side for e in range(2)],
        )
        for s_ref, side in ((own_ref, core), (other_ref, 1 - core))
        for d in range(4)
    ]
    row_times_column(pieces, y_ref, acc_ref)
    for h in range(2):
        top, low = acc_ref[h * 128 : h * 128 + 64], acc_ref[h * 128 + 64 : h * 128 + 128]
        real = (scale * (top[:, :128] - low[:, 128:])).astype(bf16)
        imag = (scale * (top[:, 128:] + low[:, :128])).astype(bf16)
        for peer in range(16):
            out_ref[peer, h, 0:64] = real
            out_ref[peer, h, 64:128] = imag


def last_collision(scale, where_ref, own_ref, other_ref, y_ref, base_ref, out_ref, acc_ref):
    core = where_ref[4]
    pieces = [
        ([s_ref[2 * p + e] for e in range(2)], [4 * p + 2 * e + side for e in range(2)])
        for s_ref, side in ((own_ref, core), (other_ref, 1 - core))
        for p in range(4)
    ]
    row_times_column(pieces, y_ref, acc_ref)
    top, low = acc_ref[0:64], acc_ref[64:128]
    out_ref[0] = base_ref[0:64] + (0.5 * scale) * (top[:, :128] - low[:, 128:])
    out_ref[1] = base_ref[64:128] + (0.5 * scale) * (top[:, 128:] + low[:, :128])


def halves(x):
    high = x.astype(bf16)
    return high, (x - high.astype(f32)).astype(bf16)


def long_product(left, right):
    lh, ll = left
    rh, rl = halves(right)
    return dot(
        jnp.concatenate([lh, lh, ll, ll], axis=1), jnp.concatenate([rh, rl, rh, rl], axis=0)
    )


def embedded(z):
    return jnp.concatenate([z, jnp.concatenate([-z[32:], z[:32]], axis=0)], axis=1)


def put_unit(z, at):
    row = lax.broadcasted_iota(jnp.int32, z.shape, 0)
    lane = lax.broadcasted_iota(jnp.int32, z.shape, 1)
    unit = jnp.where((row == lane - 32 * at) & (row < 32), 1.0, 0.0)
    return jnp.where(lane >= 32 * at, unit, z)


def lanes_from_zero(z, last):
    moved = jnp.concatenate([z[:, 32:], z[:, :32]], axis=1)
    row = lax.broadcasted_iota(jnp.int32, z.shape, 0)
    lane = lax.broadcasted_iota(jnp.int32, z.shape, 1)
    tail = jnp.where(row == lane - 224, 1.0, 0.0) if last else jnp.zeros_like(z)
    return jnp.where(lane >= 224, tail, moved)


def build_steps(damp_ref, u_ref, p_ref, q_ref, pc_ref, hc_ref, z_ref):
    left = halves(embedded(u_ref[...]))

    def store(k, i, z):
        high, low = halves(lanes_from_zero(z, i == 7))
        first_high, first_low = halves(z[:, :32])
        first = jnp.concatenate([first_high, first_high, first_low], axis=1)
        for part in range(2):
            start = 256 * part + 32 * i
            rows, to = slice(32 * part, 32 * part + 32), slice(start, start + 32)
            p_ref[k, to, 0:256] = high[rows]
            p_ref[k, to, 256:512] = low[rows]
            q_ref[k, to] = first[rows]

    for k in range(8):
        start = jnp.concatenate([u_ref[...], jnp.zeros((64, 224), f32)], axis=1)
        z = put_unit(damp_ref[:, 8 * k : 8 * k + 1] * start, 1)
        z_ref[k] = z
        store(k, 0, z)
    for i in range(1, 8):
        for k in range(8):
            t = 8 * k + i
            z = damp_ref[:, t : t + 1] * long_product(left, z_ref[k])
            if i < 7:
                z = put_unit(z, i + 1)
            z_ref[k] = z
            store(k, i, z)

    w = None
    for k in range(8):
        whole = z_ref[k][:, :32]
        if k == 0:
            w = put_unit(jnp.concatenate([whole, jnp.zeros((64, 224), f32)], axis=1), 1)
        else:
            w = long_product(halves(embedded(whole)), w)
            if k < 7:
                w = put_unit(w, k + 1)
        high, low = halves(lanes_from_zero(w, k == 7))
        rows = slice(k * 64, k * 64 + 64)
        pc_ref[rows, 0:256] = high
        pc_ref[rows, 256:512] = high
        pc_ref[rows, 512:768] = low
        hc_ref[rows] = jnp.concatenate(halves(w[:, :32]), axis=1)


def predict(
    where_ref, force_ref, lg_ref, factor_ref, p_ref, q_ref, pc_ref, hc_ref,
    y_ref, t_ref, base_ref,
    f_ref, s_ref, ends_ref, carry_ref, hom_ref, x_ref,
):
    j, h = where_ref[0], where_ref[1]
    own_block, own_start = j // 2, pl.multiple_of((j % 2) * 128 + h * 64, 64)
    own_low = pl.multiple_of(own_start + 256, 64)

    def block_of(ref, k, start):
        return jnp.concatenate(
            [
                jnp.concatenate(
                    [
                        ref[2 * k + u // 2, u % 2, start + 64 * part : start + 64 * part + 64]
                        for u in range(4)
                    ],
                    axis=0,
                )
                for part in range(2)
            ],
            axis=1,
        )

    def parts(product):
        rows = product.shape[0] // 2
        top, low = product[:rows], product[rows:]
        return top[:, :128] - low[:, 128:], top[:, 128:] + low[:, :128]

    def twice(x):
        return jnp.concatenate([x, x], axis=0)

    def last_rows(k):
        return jnp.concatenate([p_ref[k, 224:256], p_ref[k, 480:512]], axis=0)

    def put_end(k, source):
        real, imag = parts(dot(last_rows(k), twice(source)))
        high, low = halves(jnp.concatenate([real, imag], axis=1))
        ends_ref[0, k], ends_ref[1, k], ends_ref[2, k] = high, low, high

    def coarse():
        return dot(pc_ref[...], ends_ref[...].reshape(768, 256))

    def rows_of(product, k):
        part = product[k * 64 : k * 64 + 64]
        return jnp.concatenate(parts(part), axis=1)

    def triple(x):
        high, low = halves(x)
        return jnp.concatenate([high, low, high], axis=0)

    for k in range(8):
        source = block_of(force_ref, k, 0)
        f_ref[k] = source
        put_end(k, source)
    initial = jnp.concatenate([lg_ref[0, 0, 0:32], lg_ref[0, 0, 64:96]], axis=1)
    hom = dot(hc_ref[...], twice(initial))
    carry = coarse() + hom
    hom_ref[0] = carry_ref[0] = triple(initial.astype(f32))
    for k in range(7):
        hom_ref[k + 1] = triple(rows_of(hom, k))
        carry_ref[k + 1] = triple(rows_of(carry, k))
    factor = factor_ref[...]

    def whole(k, _):
        real, imag = parts(dot(p_ref[k], twice(f_ref[k])) + dot(q_ref[k], carry_ref[k]))
        x_ref[k, 0:256], x_ref[k, 256:512] = real, imag
        g = block_of(lg_ref, k, 128).astype(f32)
        spectral_re, spectral_im = spectral(real, imag, g[:, :128], g[:, 128:], factor)
        s = jnp.concatenate([spectral_re, spectral_im], axis=1).astype(bf16)
        s_ref[k] = s
        for part, y in enumerate((real.astype(bf16), imag.astype(bf16))):
            for u in range(4):
                y_ref[2 * k + u // 2, u % 2, 64 * part : 64 * part + 64] = y[64 * u : 64 * u + 64]
        put_end(k, s)
        return 0

    lax.fori_loop(0, 8, whole, 0)
    carry = coarse()
    carry_ref[0] = jnp.zeros((96, 256), bf16)
    for k in range(7):
        carry_ref[k + 1] = triple(rows_of(carry, k))

    def own(ref):
        return jnp.concatenate(
            [ref[own_block, pl.ds(own_start, 64)], ref[own_block, pl.ds(own_low, 64)]], axis=0
        )

    q_own = own(q_ref)
    real, imag = parts(dot(own(p_ref), twice(s_ref[own_block])) + dot(q_own, carry_ref[own_block]))
    t_ref[0:64], t_ref[64:128] = real.astype(bf16), imag.astype(bf16)
    real, imag = parts(dot(q_own, hom_ref[own_block]))
    base = own(x_ref)
    base_ref[0:64] = 0.5 * (base[0:64] + real)
    base_ref[64:128] = 0.5 * (base[64:128] + imag)


def call(kernel, outs, scratch, ins, flops, moved):
    return pl.pallas_call(
        kernel,
        out_shape=outs,
        in_specs=ins,
        out_specs=jax.tree.map(lambda _: VMEM, outs),
        scratch_shapes=scratch,
        compiler_params=pltpu.CompilerParams(vmem_limit_bytes=24 << 20),
        cost_estimate=pl.CostEstimate(flops=flops, bytes_accessed=moved, transcendentals=0),
    )


def shape(*dims, kind=bf16):
    return jax.ShapeDtypeStruct(dims, kind)


def shards(window, damping, propagator, coupling):
    orbitals = coupling.shape[0]
    horizon = damping.shape[0] * lax.axis_size(FIRST)
    scale = 1.0 / (horizon * math.sqrt(orbitals))
    factor = jnp.tile(coupling[:, None] * coupling[None, :], (8, 4))
    window = window.reshape(2, 2, 64, 128)
    less, great = window[0], window[1]
    where = jnp.stack(
        [lax.axis_index(axis) for axis in (PLANE, "zh", "zm", "zq", "c")]
    ).astype(jnp.int32)

    real, imag = spectral(less[0], less[1], great[0], great[1], factor[:64])
    s1 = jnp.concatenate([real, imag]).astype(bf16)

    d0 = damping.reshape(1, 64)
    high = lax.reduce_precision(d0, 8, 7)
    rest = d0 - high
    mid = lax.reduce_precision(rest, 8, 7)
    tail = rest - mid
    rows = jnp.concatenate([high, mid, tail, jnp.zeros_like(d0)], axis=1).reshape(2, 128)
    message = jnp.concatenate(
        [
            less.reshape(128, 128).astype(bf16),
            great.reshape(128, 128).astype(bf16),
            jnp.pad(rows.astype(bf16), ((0, 14), (0, 0))),
            s1,
        ]
    )
    pair = in_order(message, swapped(message, "zh"), "zh")
    lg = from_everyone(pair[:, :272], PLANE)

    s_rows = pair[:, 272:]
    s_rows = jnp.stack([s_rows, swapped(s_rows, "zm")])
    s_rows = jnp.stack([s_rows] + [crossed(s_rows, "zq", d) for d in (1, 2, 3)])
    s_other = swapped(s_rows, "c")

    c1 = call(
        functools.partial(first_collision, scale),
        shape(16, 2, 128, 128),
        [pltpu.VMEM((256, 256), f32)],
        [SMEM, VMEM, VMEM, VMEM],
        2 * 256 * 256 * 2048,
        4 << 20,
    )(where, s_rows, s_other, lg)
    force = lax.all_to_all(c1, PLANE, 0, 0, tiled=True)

    parts = lg[:, :, 256:258].astype(f32).reshape(32, 4, 64)
    damp = (parts[:, 0] + (parts[:, 1] + parts[:, 2])).reshape(64, 32)
    damp = jnp.tile(damp.T, (2, 1))
    steps, inflow, coarse, start = call(
        build_steps,
        (shape(8, 512, 512), shape(8, 512, 96), shape(512, 768), shape(512, 64)),
        [pltpu.VMEM((8, 64, 256), f32)],
        [VMEM, VMEM],
        64 * 2 * 64 * 256 * 256,
        6 << 20,
    )(damp, propagator.reshape(64, 32))

    y2, t2, base = call(
        predict,
        (shape(16, 2, 128, 128), shape(128, 128), shape(128, 128, kind=f32)),
        [
            pltpu.VMEM((8, 256, 256), bf16),
            pltpu.VMEM((8, 256, 256), bf16),
            pltpu.VMEM((3, 8, 32, 256), bf16),
            pltpu.VMEM((8, 96, 256), bf16),
            pltpu.VMEM((8, 96, 256), bf16),
            pltpu.VMEM((8, 512, 128), f32),
        ],
        [SMEM] + [VMEM] * 7,
        2 * 8 * 512 * 512 * 128 * 2,
        10 << 20,
    )(where, force, lg, factor, steps, inflow, coarse, start)

    t_rows = from_everyone(t2, ("zm", "zq"))
    t_other = swapped(t_rows, "c")
    out = call(
        functools.partial(last_collision, scale),
        shape(2, 64, 128, kind=f32),
        [pltpu.VMEM((128, 256), f32)],
        [SMEM, VMEM, VMEM, VMEM, VMEM],
        2 * 128 * 256 * 2048,
        2 << 20,
    )(where, t_rows, t_other, y2, base)
    return out.reshape(2, 2, orbitals, 128)


def solution(mesh):
    finer = Mesh(mesh.devices.reshape(4, 4, 2, 2, 4, 2), (*FIRST, *SECOND))
    placed = (P(None, None, FIRST, None, SECOND), P(FIRST, None), P(), P())
    return jax.shard_map(
        shards, mesh=finer, in_specs=placed, out_specs=P(None, FIRST, None, SECOND), check_vma=False
    )
```

time: 166 us -> 136 us (0.82)
  starting transfers between devices: 33.7 us -> 62.9 us
  blocking collectives: 49.3 us -> 21.2 us
  waiting for transfers between devices: 43 us -> 17.1 us
  Pallas kernels: 24.5 us -> 15 us
  local copies, waits for them, and re-layouts: 11.8 us -> 16.2 us
    ppermute x3 -> x7, starting transfers between devices: 15 us -> 49 us  [crossed(): return lax.ppermute(shard, axis, [(k, k ^ other) for k in range(peers)])]
    all_to_all x3 -> x1, waiting for transfers between devices: 30.3 us -> 0.01 us  [from_everyone(): lax.all_to_all(jnp.broadcast_to(shard[None], (peers, *shard.shape)), axis...]
    all_to_all x3 -> x1, blocking collectives: 49.3 us -> 21.2 us  [from_everyone(): lax.all_to_all(jnp.broadcast_to(shard[None], (peers, *shard.shape)), axis...]
    all_to_all x3 -> x1, starting transfers between devices: 18.7 us -> 7 us  [from_everyone(): lax.all_to_all(jnp.broadcast_to(shard[None], (peers, *shard.shape)), axis...]
    all_to_all x0 -> x1, starting transfers between devices: none -> 6.93 us  [shards(): force = lax.all_to_all(c1, PLANE, 0, 0, tiled=True)]
    unnamed x16 -> x20, local copies, waits for them, and re-layouts: 3.34 us -> 10.2 us
    pallas_call x2, Pallas kernels: 11 us -> 6.41 us  [the longest x1 5.35 us: shards(): call(build_steps, (shape(8, 512, 512), shape(8, 512, 96), shape(512, 768)...]
    all_to_all x0 -> x1, waiting for transfers between devices: none -> 3.87 us  [shards(): force = lax.all_to_all(c1, PLANE, 0, 0, tiled=True)]
  transfers between devices with their start and end apart: 6 -> 9, of which waited for: 5 -> 7; matrix products, arithmetic and copies ran while one was open for 2% -> 2% of each run, Pallas kernels for 4% -> 4%
where the time goes in v2:
time: 136 us; the launch traced here: 135 us
  starting transfers between devices  62.9 us (46%)
  blocking collectives  21.2 us (16%)
  waiting for transfers between devices  17.1 us (13%)
  local copies, waits for them, and re-layouts  16.2 us (12%)
  Pallas kernels  15 us (11%)
  other arithmetic  2.01 us (1%)
    ppermute x7, starting transfers between devices, crossed(): return lax.ppermute(shard, axis, [(k, k ^ other) for k in range(peers)])  49 us
    all_to_all x1, blocking collectives, from_everyone(): lax.all_to_all(jnp.broadcast_to(shard[None], (peers, *shard.shape)), axis...  21.2 us
    ppermute x7, waiting for transfers between devices, crossed(): return lax.ppermute(shard, axis, [(k, k ^ other) for k in range(peers)])  13.2 us
    unnamed x20, local copies, waits for them, and re-layouts  10.2 us
    pallas_call x1, Pallas kernels, shards(): call(predict, (shape(16, 2, 128, 128), shape(128, 128), shape(128, 128, k...  7.12 us
    all_to_all x1, starting transfers between devices, from_everyone(): lax.all_to_all(jnp.broadcast_to(shard[None], (peers, *shard.shape)), axis...  7 us
    all_to_all x1, starting transfers between devices, shards(): force = lax.all_to_all(c1, PLANE, 0, 0, tiled=True)  6.93 us
    pallas_call x1, Pallas kernels, shards(): call(build_steps, (shape(8, 512, 512), shape(8, 512, 96), shape(512, 768)...  5.35 us
  transfers between devices with their start and end apart: 9, of which 7 were waited for; matrix products, arithmetic and copies ran while one was open for 2% of the time, Pallas kernels for 4%

profile of v2, /device:TPU:1, one launch (start us, length us, event | category | flops | bytes accessed | tf_op | source)
XLA Modules:
  0.0 134.8 jit_solution(9583636429432990966)
XLA Ops:
  0.0 0.9 convert.22
  3.8 16.3 %collective-permute-start = (bf16[400,128]{1,0:T(8,128)(2,1)S(1)}, bf16[400,128]{1,0:T(8,128)(2,1)S(1)}, u32[]{:S(2)}, u32[]{:S(2)}) collective-permute-start(bf16[400,128]{1,0:T(8,128)(2,1)S(1)} %constant_dynamic-update-slice_fusion), channel_id=1, source_target_pairs={{0,16},{16,0},{1,17},{17,1},{2,18},{18,2},{3,19},{19,3},{4,20},{20... | collective-permute-start | bytes 307208 | tf_op jit(solution)/shard_map/ppermute | solution.py:29
  20.0 2.3 %collective-permute-done = bf16[400,128]{1,0:T(8,128)(2,1)S(1)} collective-permute-done((bf16[400,128]{1,0:T(8,128)(2,1)S(1)}, bf16[400,128]{1,0:T(8,128)(2,1)S(1)}, u32[]{:S(2)}, u32[]{:S(2)}) %collective-permute-start) | collective-permute-done | bytes 102432 | tf_op jit(solution)/shard_map/ppermute | solution.py:29
  22.4 1.7 %broadcast_in_dim.7 = bf16[16,2,272,128]{3,2,1,0:T(8,128)(2,1)} broadcast(bf16[2,272,128]{2,1,0:T(8,128)(2,1)S(1)} %pad_maximum_fusion.1), dimensions={1,2,3} | broadcast | bytes 2367488 | tf_op jit(solution)/shard_map/broadcast_in_dim | solution.py:23
  24.1 7.0 %all-to-all-start = ((bf16[16,2,272,128]{3,2,1,0:T(8,128)(2,1)}), bf16[16,2,272,128]{3,2,1,0:T(8,128)(2,1)S(1)}, u32[]{:S(2)}, u32[]{:S(2)}) async-start(bf16[16,2,272,128]{3,2,1,0:T(8,128)(2,1)} %broadcast_in_dim.7), calls=%async_computation | async-start | bytes 4456448 | tf_op jit(solution)/shard_map/all_to_all | solution.py:22
  31.1 9.9 %collective-permute-start.1 = (bf16[2,128,128]{2,1,0:T(8,128)(2,1)S(1)}, bf16[2,128,128]{2,1,0:T(8,128)(2,1)S(1)}, u32[]{:S(2)}, u32[]{:S(2)}) collective-permute-start(bf16[2,128,128]{2,1,0:T(8,128)(2,1)S(1)} %pad_maximum_fusion.3), channel_id=1, source_target_pairs={{0,8},{8,0},{1,9},{9,1},{2,10},{10,2},{3,11},{11,3},{4,12},{12,4},... | collective-permute-start | bytes 196616 | tf_op jit(solution)/shard_map/ppermute | solution.py:29
  41.1 3.4 %collective-permute-done.1 = bf16[2,128,128]{2,1,0:T(8,128)(2,1)S(1)} collective-permute-done((bf16[2,128,128]{2,1,0:T(8,128)(2,1)S(1)}, bf16[2,128,128]{2,1,0:T(8,128)(2,1)S(1)}, u32[]{:S(2)}, u32[]{:S(2)}) %collective-permute-start.1) | collective-permute-done | bytes 65568 | tf_op jit(solution)/shard_map/ppermute | solution.py:29
  44.4 6.7 %collective-permute-start.3 = (bf16[2,2,128,128]{3,2,1,0:T(8,128)(2,1)S(1)}, bf16[2,2,128,128]{3,2,1,0:T(8,128)(2,1)S(1)}, u32[]{:S(2)}, u32[]{:S(2)}) collective-permute-start(bf16[2,2,128,128]{3,2,1,0:T(8,128)(2,1)S(1)} %get-tuple-element.24), channel_id=1, source_target_pairs={{0,4},{2,6},{4,0},{6,2},{1,5},{3,7},{5,1},{7,3},{8,12},{10,14},{12... | collective-permute-start | bytes 393224 | tf_op jit(solution)/shard_map/ppermute | solution.py:29
  51.1 1.9 %collective-permute-start.2 = (bf16[2,2,128,128]{3,2,1,0:T(8,128)(2,1)S(1)}, bf16[2,2,128,128]{3,2,1,0:T(8,128)(2,1)S(1)}, u32[]{:S(2)}, u32[]{:S(2)}) collective-permute-start(bf16[2,2,128,128]{3,2,1,0:T(8,128)(2,1)S(1)} %get-tuple-element.24), channel_id=1, source_target_pairs={{0,2},{2,0},{4,6},{6,4},{1,3},{3,1},{5,7},{7,5},{8,10},{10,8},{12,... | collective-permute-start | bytes 393224 | tf_op jit(solution)/shard_map/ppermute | solution.py:29
  53.1 3.1 %collective-permute-start.4 = (bf16[2,2,128,128]{3,2,1,0:T(8,128)(2,1)S(1)}, bf16[2,2,128,128]{3,2,1,0:T(8,128)(2,1)S(1)}, u32[]{:S(2)}, u32[]{:S(2)}) collective-permute-start(bf16[2,2,128,128]{3,2,1,0:T(8,128)(2,1)S(1)} %get-tuple-element.24), channel_id=1, source_target_pairs={{0,6},{2,4},{4,2},{6,0},{1,7},{3,5},{5,3},{7,1},{8,14},{10,12},{12... | collective-permute-start | bytes 393224 | tf_op jit(solution)/shard_map/ppermute | solution.py:29
  56.2 2.3 %collective-permute-done.2 = bf16[2,2,128,128]{3,2,1,0:T(8,128)(2,1)S(1)} collective-permute-done((bf16[2,2,128,128]{3,2,1,0:T(8,128)(2,1)S(1)}, bf16[2,2,128,128]{3,2,1,0:T(8,128)(2,1)S(1)}, u32[]{:S(2)}, u32[]{:S(2)}) %collective-permute-start.2) | collective-permute-done | bytes 131104 | tf_op jit(solution)/shard_map/ppermute | solution.py:29
  58.5 2.7 %collective-permute-done.4 = bf16[2,2,128,128]{3,2,1,0:T(8,128)(2,1)S(1)} collective-permute-done((bf16[2,2,128,128]{3,2,1,0:T(8,128)(2,1)S(1)}, bf16[2,2,128,128]{3,2,1,0:T(8,128)(2,1)S(1)}, u32[]{:S(2)}, u32[]{:S(2)}) %collective-permute-start.4) | collective-permute-done | bytes 131104 | tf_op jit(solution)/shard_map/ppermute | solution.py:29
  61.2 3.5 %collective-permute-start.5 = (bf16[4,2,2,128,128]{4,3,2,1,0:T(8,128)(2,1)S(1)}, bf16[4,2,2,128,128]{4,3,2,1,0:T(8,128)(2,1)S(1)}, u32[]{:S(2)}, u32[]{:S(2)}) collective-permute-start(bf16[4,2,2,128,128]{4,3,2,1,0:T(8,128)(2,1)S(1)} %pad_maximum_fusion.own_ref), channel_id=1, source_target_pairs={{0,1},{1,0},{2,3},{3,2},{4,5},{5,4},{6,7},{7,6},{8,9},{9,8},{10,11... | collective-permute-start | bytes 1572872 | tf_op jit(solution)/shard_map/ppermute | solution.py:29
  64.9 1.4 %collective-permute-done.5.other_ref = bf16[4,2,2,128,128]{4,3,2,1,0:T(8,128)(2,1)S(1)} collective-permute-done((bf16[4,2,2,128,128]{4,3,2,1,0:T(8,128)(2,1)S(1)}, bf16[4,2,2,128,128]{4,3,2,1,0:T(8,128)(2,1)S(1)}, u32[]{:S(2)}, u32[]{:S(2)}) %collective-permute-start.5) | collective-permute-done | bytes 524320 | tf_op jit(solution)/shard_map/ppermute | solution.py:29
  66.3 1.1 shard_map.46
  67.4 1.0 copy-done.2
  68.4 6.9 %all-to-all-start.1 = ((bf16[16,2,128,128]{3,2,1,0:T(8,128)(2,1)}), bf16[16,2,128,128]{3,2,1,0:T(8,128)(2,1)S(1)}, u32[]{:S(2)}, u32[]{:S(2)}) async-start(bf16[16,2,128,128]{3,2,1,0:T(8,128)(2,1)} %copy-done.2), calls=%async_computation.1 | async-start | bytes 2097152 | tf_op jit(solution)/shard_map/all_to_all | solution.py:342
  75.3 0.9 tile.8
  76.2 1.3 tile.9.factor_ref
  78.6 5.4 %shard_map.47 = (bf16[8,512,512]{2,1,0:T(8,128)(2,1)S(1)}, bf16[8,512,96]{2,1,0:T(8,128)(2,1)S(1)}, bf16[512,768]{1,0:T(8,128)(2,1)S(1)}, bf16[512,64]{1,0:T(8,128)(2,1)S(1)}) custom-call(f32[64,64]{1,0:T(8,128)S(1)} %bitcast.125, f32[64,32]{1,0:T(8,128)S(1)} %bitcast.126), custom_call_target="tpu_custom_call" | custom-call | flops 536870912 | bytes 6291456 | tf_op jit(solution)/shard_map/pallas_call | solution.py:347
  84.0 1.9 %copy-done = bf16[8,512,512]{2,1,0:T(8,128)(2,1)} copy-done((bf16[8,512,512]{2,1,0:T(8,128)(2,1)}, bf16[8,512,512]{2,1,0:T(8,128)(2,1)S(1)}, u32[]{:S(2)}) %copy-start) | copy-done | bytes 4194328
  85.9 1.0 copy-done.3
  86.9 0.9 copy-done.5
  87.8 3.9 %all-to-all-done.1.force_ref = bf16[16,2,128,128]{3,2,1,0:T(8,128)(2,1)S(1)} async-done(((bf16[16,2,128,128]{3,2,1,0:T(8,128)(2,1)}), bf16[16,2,128,128]{3,2,1,0:T(8,128)(2,1)S(1)}, u32[]{:S(2)}, u32[]{:S(2)}) %all-to-all-start.1) | async-done | bytes 1048608 | tf_op jit(solution)/shard_map/all_to_all | solution.py:342
  91.7 2.2 %copy-done.1 = bf16[8,512,512]{2,1,0:T(8,128)(2,1)S(1)} copy-done((bf16[8,512,512]{2,1,0:T(8,128)(2,1)S(1)}, bf16[8,512,512]{2,1,0:T(8,128)(2,1)}, u32[]{:S(2)}) %copy-start.1) | copy-done | bytes 4194328
  93.8 1.2 copy-done.4
  95.1 1.1 copy-done.6
  96.2 7.1 %shard_map.48 = (bf16[16,2,128,128]{3,2,1,0:T(8,128)(2,1)S(1)}, bf16[128,128]{1,0:T(8,128)(2,1)S(1)}, f32[128,128]{1,0:T(8,128)S(1)}) custom-call(s32[5]{0:T(128)S(1)} %stack.56.where_ref, bf16[16,2,128,128]{3,2,1,0:T(8,128)(2,1)S(1)} %all-to-all-done.1.force_ref, bf16[16,2,272,128]{3,2,1,0:T(8,128)(2,1)S(1)} %all-to-all-done.y_ref.lg_ref, ...), custom_call_target="tpu_custom_call" | custom-call | flops 1073741824 | bytes 10485760 | tf_op jit(solution)/shard_map/pallas_call | solution.py:356
  103.4 21.2 %all_to_all.15.own_ref = bf16[8,128,128]{2,1,0:T(8,128)(2,1)S(1)} all-to-all(bf16[8,128,128]{2,1,0:T(8,128)(2,1)S(1)} %broadcast_in_dim.8), channel_id=1, replica_groups=mesh['y'=4,'x'=4,'zh'=2,'zm'=2,'zq'=4,'c'=2] {'zm','zq'}, dimensions={0} | all-to-all | bytes 524288 | tf_op jit(solution)/shard_map/all_to_all | solution.py:22
  124.6 7.6 %collective-permute-start.6 = (bf16[8,128,128]{2,1,0:T(8,128)(2,1)S(1)}, bf16[8,128,128]{2,1,0:T(8,128)(2,1)S(1)}, u32[]{:S(2)}, u32[]{:S(2)}) collective-permute-start(bf16[8,128,128]{2,1,0:T(8,128)(2,1)S(1)} %all_to_all.15.own_ref), channel_id=1, source_target_pairs={{0,1},{1,0},{2,3},{3,2},{4,5},{5,4},{6,7},{7,6},{8,9},{9,8},{10,11... | collective-permute-start | bytes 786440 | tf_op jit(solution)/shard_map/ppermute | solution.py:29
  132.2 1.1 collective-permute-done.6.other_ref
  133.3 1.5 %shard_map.49 = f32[2,64,128]{2,1,0:T(8,128)} custom-call(s32[5]{0:T(128)S(1)} %stack.56.where_ref, bf16[8,128,128]{2,1,0:T(8,128)(2,1)S(1)} %all_to_all.15.own_ref, bf16[8,128,128]{2,1,0:T(8,128)(2,1)S(1)} %collective-permute-done.6.other_ref, bf16[16,2,128,128]{3,2,1,0:T(8,128)(2,1)S(1)} %get-tuple-element.17.y_ref, f32[128,128]{1,0:T(8,128)S(1)} %get-tuple-element.18.base_ref), custom_call_target="tpu_custom_call" | custom-call | flops 134217728 | bytes 2097152 | tf_op jit(solution)/shard_map/pallas_call | solution.py:374
  (42 shorter events, 4.1 us)
Async XLA Ops:
  3.8 18.6 %collective-permute-start = (bf16[400,128]{1,0:T(8,128)(2,1)S(1)}, bf16[400,128]{1,0:T(8,128)(2,1)S(1)}, u32[]{:S(2)}, u32[]{:S(2)}) collective-permute-start(bf16[400,128]{1,0:T(8,128)(2,1)S(1)} %constant_dynamic-update-slice_fusion), channel_id=1, source_target_pairs={{0,16},{16,0},{1,17},{17,1},{2,18},{18,2},{3,19},{19,3},{4,20},{20... | collective-permute-start | bytes 307208 | tf_op jit(solution)/shard_map/ppermute | solution.py:29
  24.1 42.2 %all-to-all-start = ((bf16[16,2,272,128]{3,2,1,0:T(8,128)(2,1)}), bf16[16,2,272,128]{3,2,1,0:T(8,128)(2,1)S(1)}, u32[]{:S(2)}, u32[]{:S(2)}) async-start(bf16[16,2,272,128]{3,2,1,0:T(8,128)(2,1)} %broadcast_in_dim.7), calls=%async_computation | async-start | bytes 4456448 | tf_op jit(solution)/shard_map/all_to_all | solution.py:22
  31.1 13.3 %collective-permute-start.1 = (bf16[2,128,128]{2,1,0:T(8,128)(2,1)S(1)}, bf16[2,128,128]{2,1,0:T(8,128)(2,1)S(1)}, u32[]{:S(2)}, u32[]{:S(2)}) collective-permute-start(bf16[2,128,128]{2,1,0:T(8,128)(2,1)S(1)} %pad_maximum_fusion.3), channel_id=1, source_target_pairs={{0,8},{8,0},{1,9},{9,1},{2,10},{10,2},{3,11},{11,3},{4,12},{12,4},... | collective-permute-start | bytes 196616 | tf_op jit(solution)/shard_map/ppermute | solution.py:29
  44.4 11.7 %collective-permute-start.3 = (bf16[2,2,128,128]{3,2,1,0:T(8,128)(2,1)S(1)}, bf16[2,2,128,128]{3,2,1,0:T(8,128)(2,1)S(1)}, u32[]{:S(2)}, u32[]{:S(2)}) collective-permute-start(bf16[2,2,128,128]{3,2,1,0:T(8,128)(2,1)S(1)} %get-tuple-element.24), channel_id=1, source_target_pairs={{0,4},{2,6},{4,0},{6,2},{1,5},{3,7},{5,1},{7,3},{8,12},{10,14},{12... | collective-permute-start | bytes 393224 | tf_op jit(solution)/shard_map/ppermute | solution.py:29
  51.1 7.3 %collective-permute-start.2 = (bf16[2,2,128,128]{3,2,1,0:T(8,128)(2,1)S(1)}, bf16[2,2,128,128]{3,2,1,0:T(8,128)(2,1)S(1)}, u32[]{:S(2)}, u32[]{:S(2)}) collective-permute-start(bf16[2,2,128,128]{3,2,1,0:T(8,128)(2,1)S(1)} %get-tuple-element.24), channel_id=1, source_target_pairs={{0,2},{2,0},{4,6},{6,4},{1,3},{3,1},{5,7},{7,5},{8,10},{10,8},{12,... | collective-permute-start | bytes 393224 | tf_op jit(solution)/shard_map/ppermute | solution.py:29
  53.1 8.1 %collective-permute-start.4 = (bf16[2,2,128,128]{3,2,1,0:T(8,128)(2,1)S(1)}, bf16[2,2,128,128]{3,2,1,0:T(8,128)(2,1)S(1)}, u32[]{:S(2)}, u32[]{:S(2)}) collective-permute-start(bf16[2,2,128,128]{3,2,1,0:T(8,128)(2,1)S(1)} %get-tuple-element.24), channel_id=1, source_target_pairs={{0,6},{2,4},{4,2},{6,0},{1,7},{3,5},{5,3},{7,1},{8,14},{10,12},{12... | collective-permute-start | bytes 393224 | tf_op jit(solution)/shard_map/ppermute | solution.py:29
  61.2 5.1 %collective-permute-start.5 = (bf16[4,2,2,128,128]{4,3,2,1,0:T(8,128)(2,1)S(1)}, bf16[4,2,2,128,128]{4,3,2,1,0:T(8,128)(2,1)S(1)}, u32[]{:S(2)}, u32[]{:S(2)}) collective-permute-start(bf16[4,2,2,128,128]{4,3,2,1,0:T(8,128)(2,1)S(1)} %pad_maximum_fusion.own_ref), channel_id=1, source_target_pairs={{0,1},{1,0},{2,3},{3,2},{4,5},{5,4},{6,7},{7,6},{8,9},{9,8},{10,11... | collective-permute-start | bytes 1572872 | tf_op jit(solution)/shard_map/ppermute | solution.py:29
  67.4 1.0 copy-start.2
  68.4 23.3 %all-to-all-start.1 = ((bf16[16,2,128,128]{3,2,1,0:T(8,128)(2,1)}), bf16[16,2,128,128]{3,2,1,0:T(8,128)(2,1)S(1)}, u32[]{:S(2)}, u32[]{:S(2)}) async-start(bf16[16,2,128,128]{3,2,1,0:T(8,128)(2,1)} %copy-done.2), calls=%async_computation.1 | async-start | bytes 2097152 | tf_op jit(solution)/shard_map/all_to_all | solution.py:342
  77.8 0.8 copy-start.7
  84.0 1.9 %copy-start = (bf16[8,512,512]{2,1,0:T(8,128)(2,1)}, bf16[8,512,512]{2,1,0:T(8,128)(2,1)S(1)}, u32[]{:S(2)}) copy-start(bf16[8,512,512]{2,1,0:T(8,128)(2,1)S(1)} %get-tuple-element.12.p_ref) | copy-start | bytes 12582916
  85.9 1.0 copy-start.3
  86.9 0.9 copy-start.5
  91.7 2.2 %copy-start.1 = (bf16[8,512,512]{2,1,0:T(8,128)(2,1)S(1)}, bf16[8,512,512]{2,1,0:T(8,128)(2,1)}, u32[]{:S(2)}) copy-start(bf16[8,512,512]{2,1,0:T(8,128)(2,1)} %copy-done) | copy-start | bytes 12582916
  93.8 1.2 copy-start.4
  95.1 1.1 copy-start.6
  124.6 8.7 %collective-permute-start.6 = (bf16[8,128,128]{2,1,0:T(8,128)(2,1)S(1)}, bf16[8,128,128]{2,1,0:T(8,128)(2,1)S(1)}, u32[]{:S(2)}, u32[]{:S(2)}) collective-permute-start(bf16[8,128,128]{2,1,0:T(8,128)(2,1)S(1)} %all_to_all.15.own_ref), channel_id=1, source_target_pairs={{0,1},{1,0},{2,3},{3,2},{4,5},{5,4},{6,7},{7,6},{8,9},{9,8},{10,11... | collective-permute-start | bytes 786440 | tf_op jit(solution)/shard_map/ppermute | solution.py:29

commit v3 on v2

--- a/solution.py
+++ b/solution.py
@@ -15,6 +15,7 @@
 f32, bf16 = jnp.float32, jnp.bfloat16
 VMEM = pl.BlockSpec(memory_space=pltpu.VMEM)
 SMEM = pl.BlockSpec(memory_space=pltpu.SMEM)
+HBM = pl.BlockSpec(memory_space=pltpu.HBM)
 
 
 def from_everyone(shard, axis):
@@ -36,6 +37,15 @@
 def in_order(own, other, axis):
     first = lax.axis_index(axis) == 0
     return jnp.stack([jnp.where(first, own, other), jnp.where(first, other, own)])
+
+
+def couplings(row, times):
+    wide = jnp.broadcast_to(row, (32, 32))
+    at_row = lax.broadcasted_iota(jnp.int32, (32, 32), 0)
+    at_lane = lax.broadcasted_iota(jnp.int32, (32, 32), 1)
+    column = jnp.sum(jnp.where(at_row == at_lane, wide, 0.0), axis=1, keepdims=True)
+    tile = jnp.concatenate([column * wide] * 4, axis=1)
+    return jnp.concatenate([tile] * times, axis=0)
 
 
 def spectral(less_re, less_im, great_re, great_im, factor):
@@ -54,6 +64,22 @@
 
 def dot(left, right):
     return jnp.dot(left, right, preferred_element_type=f32)
+
+
+def compose(window_ref, damp_ref, coupling_ref, out_ref):
+    fields = [[window_ref[which, part] for part in range(2)] for which in range(2)]
+    for which in range(2):
+        for part in range(2):
+            start = 128 * which + 64 * part
+            out_ref[start : start + 64] = fields[which][part].astype(bf16)
+    damp = damp_ref[...]
+    high = damp.astype(bf16).astype(f32)
+    mid = (damp - high).astype(bf16).astype(f32)
+    low = damp - high - mid
+    rows = jnp.concatenate([high, mid, low, jnp.zeros_like(low)], axis=1)
+    out_ref[256:272] = jnp.concatenate([rows, jnp.zeros((14, 128), f32)], axis=0).astype(bf16)
+    real, imag = spectral(*fields[0], *fields[1], couplings(coupling_ref[...], 2))
+    out_ref[272:336], out_ref[336:400] = real.astype(bf16), imag.astype(bf16)
 
 
 def row_times_column(pieces, y_ref, acc_ref):
@@ -93,11 +119,11 @@
 
 
 def last_collision(scale, where_ref, own_ref, other_ref, y_ref, base_ref, out_ref, acc_ref):
-    core = where_ref[4]
+    zm, core = where_ref[2], where_ref[4]
     pieces = [
-        ([s_ref[2 * p + e] for e in range(2)], [4 * p + 2 * e + side for e in range(2)])
+        ([s_ref[q, e] for e in range(2)], [8 * (zm ^ e) + 2 * q + side for e in range(2)])
         for s_ref, side in ((own_ref, core), (other_ref, 1 - core))
-        for p in range(4)
+        for q in range(4)
     ]
     row_times_column(pieces, y_ref, acc_ref)
     top, low = acc_ref[0:64], acc_ref[64:128]
@@ -137,7 +163,13 @@
     return jnp.where(lane >= 224, tail, moved)
 
 
-def build_steps(damp_ref, u_ref, p_ref, q_ref, pc_ref, hc_ref, z_ref):
+def build_steps(damp_ref, u_ref, out_hbm, p_ref, last_ref, pc_ref, z_ref, sems):
+    copies = [
+        pltpu.make_async_copy(p_ref.at[k], out_hbm.at[k, 0:512, 0:640], sems.at[k])
+        for k in range(8)
+    ]
+    copies.append(pltpu.make_async_copy(last_ref, out_hbm.at[:, 512:576, 0:512], sems.at[8]))
+    copies.append(pltpu.make_async_copy(pc_ref, out_hbm.at[:, 576:640, 0:896], sems.at[9]))
     left = halves(embedded(u_ref[...]))
 
     def store(k, i, z):
@@ -149,7 +181,10 @@
             rows, to = slice(32 * part, 32 * part + 32), slice(start, start + 32)
             p_ref[k, to, 0:256] = high[rows]
             p_ref[k, to, 256:512] = low[rows]
-            q_ref[k, to] = first[rows]
+            p_ref[k, to, 512:608] = first[rows]
+            if i == 7:
+                last_ref[k, rows, 0:256] = high[rows]
+                last_ref[k, rows, 256:512] = low[rows]
 
     for k in range(8):
         start = jnp.concatenate([u_ref[...], jnp.zeros((64, 224), f32)], axis=1)
@@ -164,6 +199,9 @@
                 z = put_unit(z, i + 1)
             z_ref[k] = z
             store(k, i, z)
+            if i == 7:
+                copies[k].start()
+    copies[8].start()
 
     w = None
     for k in range(8):
@@ -175,18 +213,33 @@
             if k < 7:
                 w = put_unit(w, k + 1)
         high, low = halves(lanes_from_zero(w, k == 7))
-        rows = slice(k * 64, k * 64 + 64)
-        pc_ref[rows, 0:256] = high
-        pc_ref[rows, 256:512] = high
-        pc_ref[rows, 512:768] = low
-        hc_ref[rows] = jnp.concatenate(halves(w[:, :32]), axis=1)
+        pc_ref[k, :, 0:256] = high
+        pc_ref[k, :, 256:512] = high
+        pc_ref[k, :, 512:768] = low
+        pc_ref[k, :, 768:832] = jnp.concatenate(halves(w[:, :32]), axis=1)
+    copies[9].start()
+    for copy in copies:
+        copy.wait()
 
 
 def predict(
-    where_ref, force_ref, lg_ref, factor_ref, p_ref, q_ref, pc_ref, hc_ref,
+    where_ref, force_ref, lg_ref, coupling_ref, plan_hbm,
     y_ref, t_ref, base_ref,
-    f_ref, s_ref, ends_ref, carry_ref, hom_ref, x_ref,
+    p_ref, last_ref, pc_ref, f_ref, s_ref, ends_ref, carry_ref, hom_ref, x_ref, sems,
 ):
+    copies = [
+        pltpu.make_async_copy(plan_hbm.at[:, 512:576, 0:512], last_ref, sems.at[8]),
+        pltpu.make_async_copy(plan_hbm.at[:, 576:640, 0:896], pc_ref, sems.at[9]),
+    ]
+
+    def fetch(k):
+        return pltpu.make_async_copy(
+            plan_hbm.at[k, 0:512, 0:640], p_ref.at[k], sems.at[k]
+        )
+
+    for copy in copies + [fetch(k) for k in range(8)]:
+        copy.start()
+
     j, h = where_ref[0], where_ref[1]
     own_block, own_start = j // 2, pl.multiple_of((j % 2) * 128 + h * 64, 64)
     own_low = pl.multiple_of(own_start + 256, 64)
@@ -214,16 +267,13 @@
     def twice(x):
         return jnp.concatenate([x, x], axis=0)
 
-    def last_rows(k):
-        return jnp.concatenate([p_ref[k, 224:256], p_ref[k, 480:512]], axis=0)
-
     def put_end(k, source):
-        real, imag = parts(dot(last_rows(k), twice(source)))
+        real, imag = parts(dot(last_ref[k], twice(source)))
         high, low = halves(jnp.concatenate([real, imag], axis=1))
         ends_ref[0, k], ends_ref[1, k], ends_ref[2, k] = high, low, high
 
     def coarse():
-        return dot(pc_ref[...], ends_ref[...].reshape(768, 256))
+        return dot(pc_ref[:, :, 0:768].reshape(512, 768), ends_ref[...].reshape(768, 256))
 
     def rows_of(product, k):
         part = product[k * 64 : k * 64 + 64]
@@ -234,20 +284,24 @@
         return jnp.concatenate([high, low, high], axis=0)
 
     for k in range(8):
-        source = block_of(force_ref, k, 0)
-        f_ref[k] = source
-        put_end(k, source)
+        f_ref[k] = block_of(force_ref, k, 0)
+    copies[0].wait()
+    for k in range(8):
+        put_end(k, f_ref[k])
+    copies[1].wait()
     initial = jnp.concatenate([lg_ref[0, 0, 0:32], lg_ref[0, 0, 64:96]], axis=1)
-    hom = dot(hc_ref[...], twice(initial))
+    hom = dot(pc_ref[:, :, 768:832].reshape(512, 64), twice(initial))
     carry = coarse() + hom
     hom_ref[0] = carry_ref[0] = triple(initial.astype(f32))
     for k in range(7):
         hom_ref[k + 1] = triple(rows_of(hom, k))
         carry_ref[k + 1] = triple(rows_of(carry, k))
-    factor = factor_ref[...]
+    factor = couplings(coupling_ref[...], 8)
 
     def whole(k, _):
-        real, imag = parts(dot(p_ref[k], twice(f_ref[k])) + dot(q_ref[k], carry_ref[k]))
+        fetch(k).wait()
+        source = jnp.concatenate([f_ref[k], f_ref[k], carry_ref[k]], axis=0)
+        real, imag = parts(dot(p_ref[k, :, 0:608], source))
         x_ref[k, 0:256], x_ref[k, 256:512] = real, imag
         g = block_of(lg_ref, k, 128).astype(f32)
         spectral_re, spectral_im = spectral(real, imag, g[:, :128], g[:, 128:], factor)
@@ -270,23 +324,24 @@
             [ref[own_block, pl.ds(own_start, 64)], ref[own_block, pl.ds(own_low, 64)]], axis=0
         )
 
-    q_own = own(q_ref)
-    real, imag = parts(dot(own(p_ref), twice(s_ref[own_block])) + dot(q_own, carry_ref[own_block]))
+    p_own, s_own = own(p_ref), s_ref[own_block]
+    source = jnp.concatenate([s_own, s_own, carry_ref[own_block]], axis=0)
+    real, imag = parts(dot(p_own[:, 0:608], source))
     t_ref[0:64], t_ref[64:128] = real.astype(bf16), imag.astype(bf16)
-    real, imag = parts(dot(q_own, hom_ref[own_block]))
+    real, imag = parts(dot(p_own[:, 512:608], hom_ref[own_block]))
     base = own(x_ref)
     base_ref[0:64] = 0.5 * (base[0:64] + real)
     base_ref[64:128] = 0.5 * (base[64:128] + imag)
 
 
-def call(kernel, outs, scratch, ins, flops, moved):
+def call(kernel, outs, scratch, ins, flops, moved, grant=24, place=VMEM):
     return pl.pallas_call(
         kernel,
         out_shape=outs,
         in_specs=ins,
-        out_specs=jax.tree.map(lambda _: VMEM, outs),
+        out_specs=jax.tree.map(lambda _: place, outs),
         scratch_shapes=scratch,
-        compiler_params=pltpu.CompilerParams(vmem_limit_bytes=24 << 20),
+        compiler_params=pltpu.CompilerParams(vmem_limit_bytes=grant << 20),
         cost_estimate=pl.CostEstimate(flops=flops, bytes_accessed=moved, transcendentals=0),
     )
 
@@ -299,30 +354,19 @@
     orbitals = coupling.shape[0]
     horizon = damping.shape[0] * lax.axis_size(FIRST)
     scale = 1.0 / (horizon * math.sqrt(orbitals))
-    factor = jnp.tile(coupling[:, None] * coupling[None, :], (8, 4))
-    window = window.reshape(2, 2, 64, 128)
-    less, great = window[0], window[1]
     where = jnp.stack(
         [lax.axis_index(axis) for axis in (PLANE, "zh", "zm", "zq", "c")]
     ).astype(jnp.int32)
 
-    real, imag = spectral(less[0], less[1], great[0], great[1], factor[:64])
-    s1 = jnp.concatenate([real, imag]).astype(bf16)
-
-    d0 = damping.reshape(1, 64)
-    high = lax.reduce_precision(d0, 8, 7)
-    rest = d0 - high
-    mid = lax.reduce_precision(rest, 8, 7)
-    tail = rest - mid
-    rows = jnp.concatenate([high, mid, tail, jnp.zeros_like(d0)], axis=1).reshape(2, 128)
-    message = jnp.concatenate(
-        [
-            less.reshape(128, 128).astype(bf16),
-            great.reshape(128, 128).astype(bf16),
-            jnp.pad(rows.astype(bf16), ((0, 14), (0, 0))),
-            s1,
-        ]
-    )
+    strength = coupling.reshape(1, 32)
+    message = call(
+        compose,
+        shape(400, 128),
+        [],
+        [VMEM, VMEM, VMEM],
+        40 * 64 * 128,
+        400 << 10,
+    )(window.reshape(2, 2, 64, 128), damping, strength)
     pair = in_order(message, swapped(message, "zh"), "zh")
     lg = from_everyone(pair[:, :272], PLANE)
 
@@ -341,35 +385,48 @@
     )(where, s_rows, s_other, lg)
     force = lax.all_to_all(c1, PLANE, 0, 0, tiled=True)
 
-    parts = lg[:, :, 256:258].astype(f32).reshape(32, 4, 64)
-    damp = (parts[:, 0] + (parts[:, 1] + parts[:, 2])).reshape(64, 32)
+    parts = lg[:, :, 256:258].reshape(64, 128).astype(f32)
+    damp = parts[:, 0:32] + (parts[:, 32:64] + parts[:, 64:96])
     damp = jnp.tile(damp.T, (2, 1))
-    steps, inflow, coarse, start = call(
+    plan = call(
         build_steps,
-        (shape(8, 512, 512), shape(8, 512, 96), shape(512, 768), shape(512, 64)),
-        [pltpu.VMEM((8, 64, 256), f32)],
+        shape(8, 640, 1024),
+        [
+            pltpu.VMEM((8, 512, 640), bf16),
+            pltpu.VMEM((8, 64, 512), bf16),
+            pltpu.VMEM((8, 64, 896), bf16),
+            pltpu.VMEM((8, 64, 256), f32),
+            pltpu.SemaphoreType.DMA((10,)),
+        ],
         [VMEM, VMEM],
         64 * 2 * 64 * 256 * 256,
         6 << 20,
+        54,
+        HBM,
     )(damp, propagator.reshape(64, 32))
 
     y2, t2, base = call(
         predict,
         (shape(16, 2, 128, 128), shape(128, 128), shape(128, 128, kind=f32)),
         [
+            pltpu.VMEM((8, 512, 640), bf16),
+            pltpu.VMEM((8, 64, 512), bf16),
+            pltpu.VMEM((8, 64, 896), bf16),
             pltpu.VMEM((8, 256, 256), bf16),
             pltpu.VMEM((8, 256, 256), bf16),
             pltpu.VMEM((3, 8, 32, 256), bf16),
             pltpu.VMEM((8, 96, 256), bf16),
             pltpu.VMEM((8, 96, 256), bf16),
             pltpu.VMEM((8, 512, 128), f32),
+            pltpu.SemaphoreType.DMA((10,)),
         ],
-        [SMEM] + [VMEM] * 7,
+        [SMEM] + [VMEM] * 3 + [HBM],
         2 * 8 * 512 * 512 * 128 * 2,
         10 << 20,
-    )(where, force, lg, factor, steps, inflow, coarse, start)
-
-    t_rows = from_everyone(t2, ("zm", "zq"))
+        44,
+    )(where, force, lg, strength, plan)
+
+    t_rows = from_everyone(jnp.stack([t2, swapped(t2, "zm")]), "zq")
     t_other = swapped(t_rows, "c")
     out = call(
         functools.partial(last_collision, scale),

time: 136 us -> 127 us (0.934)
  blocking collectives: 21.2 us -> 9.54 us
  local copies, waits for them, and re-layouts: 16.2 us -> 4.73 us
  starting transfers between devices: 62.9 us -> 69.8 us
  Pallas kernels: 15 us -> 20.6 us
  waiting for transfers between devices: 17.1 us -> 21.5 us
  other arithmetic: 2.01 us -> 0.24 us
    all_to_all x1, blocking collectives: 21.2 us -> 9.54 us  [from_everyone(): lax.all_to_all(jnp.broadcast_to(shard[None], (peers, *shard.shape)), axis...]
    unnamed x20 -> x8, local copies, waits for them, and re-layouts: 10.2 us -> 2.24 us
    ppermute x7 -> x8, starting transfers between devices: 49 us -> 55.9 us  [crossed(): return lax.ppermute(shard, axis, [(k, k ^ other) for k in range(peers)])]
    pallas_call x1 -> x2, Pallas kernels: 5.35 us -> 8.69 us  [the longest x1 8.53 us: shards(): call(build_steps, shape(8, 640, 1024), [pltpu.VMEM((8, 512, 640), bf16),...]
    all_to_all x1, waiting for transfers between devices: 3.87 us -> 6.98 us  [shards(): force = lax.all_to_all(c1, PLANE, 0, 0, tiled=True)]
    another operation x2 -> x0, local copies, waits for them, and re-layouts: 2.17 us -> none  [shards(): factor = jnp.tile(coupling[:, None] * coupling[None, :], (8, 4))]
    ppermute x7 -> x8, waiting for transfers between devices: 13.2 us -> 14.5 us  [crossed(): return lax.ppermute(shard, axis, [(k, k ^ other) for k in range(peers)])]
  transfers between devices with their start and end apart: 9 -> 10, of which waited for: 7 -> 8; matrix products, arithmetic and copies ran while one was open for 2% -> 1% of each run, Pallas kernels for 4% -> 7%
where the time goes in v3:
time: 127 us
  starting transfers between devices  69.8 us (55%)
  waiting for transfers between devices  21.5 us (17%)
  Pallas kernels  20.6 us (16%)
  blocking collectives  9.54 us (8%)
  local copies, waits for them, and re-layouts  4.73 us (4%)
    ppermute x8, starting transfers between devices, crossed(): return lax.ppermute(shard, axis, [(k, k ^ other) for k in range(peers)])  55.9 us
    ppermute x8, waiting for transfers between devices, crossed(): return lax.ppermute(shard, axis, [(k, k ^ other) for k in range(peers)])  14.5 us
    all_to_all x1, blocking collectives, from_everyone(): lax.all_to_all(jnp.broadcast_to(shard[None], (peers, *shard.shape)), axis...  9.54 us
    pallas_call x1, Pallas kernels, shards(): call(build_steps, shape(8, 640, 1024), [pltpu.VMEM((8, 512, 640), bf16),...  8.53 us
    pallas_call x1, Pallas kernels, shards(): call(predict, (shape(16, 2, 128, 128), shape(128, 128), shape(128, 128, k...  8.36 us
    all_to_all x1, starting transfers between devices, from_everyone(): lax.all_to_all(jnp.broadcast_to(shard[None], (peers, *shard.shape)), axis...  7 us
    all_to_all x1, waiting for transfers between devices, shards(): force = lax.all_to_all(c1, PLANE, 0, 0, tiled=True)  6.98 us
    all_to_all x1, starting transfers between devices, shards(): force = lax.all_to_all(c1, PLANE, 0, 0, tiled=True)  6.92 us
  transfers between devices with their start and end apart: 10, of which 8 were waited for; matrix products, arithmetic and copies ran while one was open for 1% of the time, Pallas kernels for 7%

profile of v3, /device:TPU:1, one launch (start us, length us, event | category | flops | bytes accessed | tf_op | source)
XLA Modules:
  0.0 126.6 jit_solution(16618572220413264482)
XLA Ops:
  0.0 0.9 copy-done
  0.9 0.7 copy-done.1
  1.6 0.7 copy-done.3
  2.2 0.2 shard_map.46
  2.4 16.3 %collective-permute-start = (bf16[400,128]{1,0:T(8,128)(2,1)S(1)}, bf16[400,128]{1,0:T(8,128)(2,1)S(1)}, u32[]{:S(2)}, u32[]{:S(2)}) collective-permute-start(bf16[400,128]{1,0:T(8,128)(2,1)S(1)} %shard_map.46), channel_id=1, source_target_pairs={{0,16},{16,0},{1,17},{17,1},{2,18},{18,2},{3,19},{19,3},{4,20},{20... | collective-permute-start | bytes 307208 | tf_op jit(solution)/shard_map/ppermute | solution.py:30
  18.7 2.3 %collective-permute-done = bf16[400,128]{1,0:T(8,128)(2,1)S(1)} collective-permute-done((bf16[400,128]{1,0:T(8,128)(2,1)S(1)}, bf16[400,128]{1,0:T(8,128)(2,1)S(1)}, u32[]{:S(2)}, u32[]{:S(2)}) %collective-permute-start) | collective-permute-done | bytes 102432 | tf_op jit(solution)/shard_map/ppermute | solution.py:30
  21.1 1.7 %broadcast_in_dim.4 = bf16[16,2,272,128]{3,2,1,0:T(8,128)(2,1)} broadcast(bf16[2,272,128]{2,1,0:T(8,128)(2,1)S(1)} %pad_maximum_fusion.1), dimensions={1,2,3} | broadcast | bytes 2367488 | tf_op jit(solution)/shard_map/broadcast_in_dim | solution.py:24
  22.7 7.0 %all-to-all-start = ((bf16[16,2,272,128]{3,2,1,0:T(8,128)(2,1)}), bf16[16,2,272,128]{3,2,1,0:T(8,128)(2,1)S(1)}, u32[]{:S(2)}, u32[]{:S(2)}) async-start(bf16[16,2,272,128]{3,2,1,0:T(8,128)(2,1)} %broadcast_in_dim.4), calls=%async_computation | async-start | bytes 4456448 | tf_op jit(solution)/shard_map/all_to_all | solution.py:23
  29.7 9.9 %collective-permute-start.1 = (bf16[2,128,128]{2,1,0:T(8,128)(2,1)S(1)}, bf16[2,128,128]{2,1,0:T(8,128)(2,1)S(1)}, u32[]{:S(2)}, u32[]{:S(2)}) collective-permute-start(bf16[2,128,128]{2,1,0:T(8,128)(2,1)S(1)} %pad_maximum_fusion.3), channel_id=1, source_target_pairs={{0,8},{8,0},{1,9},{9,1},{2,10},{10,2},{3,11},{11,3},{4,12},{12,4},... | collective-permute-start | bytes 196616 | tf_op jit(solution)/shard_map/ppermute | solution.py:30
  39.7 3.4 %collective-permute-done.1 = bf16[2,128,128]{2,1,0:T(8,128)(2,1)S(1)} collective-permute-done((bf16[2,128,128]{2,1,0:T(8,128)(2,1)S(1)}, bf16[2,128,128]{2,1,0:T(8,128)(2,1)S(1)}, u32[]{:S(2)}, u32[]{:S(2)}) %collective-permute-start.1) | collective-permute-done | bytes 65568 | tf_op jit(solution)/shard_map/ppermute | solution.py:30
  43.1 6.7 %collective-permute-start.3 = (bf16[2,2,128,128]{3,2,1,0:T(8,128)(2,1)S(1)}, bf16[2,2,128,128]{3,2,1,0:T(8,128)(2,1)S(1)}, u32[]{:S(2)}, u32[]{:S(2)}) collective-permute-start(bf16[2,2,128,128]{3,2,1,0:T(8,128)(2,1)S(1)} %get-tuple-element.14), channel_id=1, source_target_pairs={{0,4},{2,6},{4,0},{6,2},{1,5},{3,7},{5,1},{7,3},{8,12},{10,14},{12... | collective-permute-start | bytes 393224 | tf_op jit(solution)/shard_map/ppermute | solution.py:30
  49.8 1.9 %collective-permute-start.2 = (bf16[2,2,128,128]{3,2,1,0:T(8,128)(2,1)S(1)}, bf16[2,2,128,128]{3,2,1,0:T(8,128)(2,1)S(1)}, u32[]{:S(2)}, u32[]{:S(2)}) collective-permute-start(bf16[2,2,128,128]{3,2,1,0:T(8,128)(2,1)S(1)} %get-tuple-element.14), channel_id=1, source_target_pairs={{0,2},{2,0},{4,6},{6,4},{1,3},{3,1},{5,7},{7,5},{8,10},{10,8},{12,... | collective-permute-start | bytes 393224 | tf_op jit(solution)/shard_map/ppermute | solution.py:30
  51.7 3.1 %collective-permute-start.4 = (bf16[2,2,128,128]{3,2,1,0:T(8,128)(2,1)S(1)}, bf16[2,2,128,128]{3,2,1,0:T(8,128)(2,1)S(1)}, u32[]{:S(2)}, u32[]{:S(2)}) collective-permute-start(bf16[2,2,128,128]{3,2,1,0:T(8,128)(2,1)S(1)} %get-tuple-element.14), channel_id=1, source_target_pairs={{0,6},{2,4},{4,2},{6,0},{1,7},{3,5},{5,3},{7,1},{8,14},{10,12},{12... | collective-permute-start | bytes 393224 | tf_op jit(solution)/shard_map/ppermute | solution.py:30
  54.8 2.3 %collective-permute-done.2 = bf16[2,2,128,128]{3,2,1,0:T(8,128)(2,1)S(1)} collective-permute-done((bf16[2,2,128,128]{3,2,1,0:T(8,128)(2,1)S(1)}, bf16[2,2,128,128]{3,2,1,0:T(8,128)(2,1)S(1)}, u32[]{:S(2)}, u32[]{:S(2)}) %collective-permute-start.2) | collective-permute-done | bytes 131104 | tf_op jit(solution)/shard_map/ppermute | solution.py:30
  57.1 2.7 %collective-permute-done.4 = bf16[2,2,128,128]{3,2,1,0:T(8,128)(2,1)S(1)} collective-permute-done((bf16[2,2,128,128]{3,2,1,0:T(8,128)(2,1)S(1)}, bf16[2,2,128,128]{3,2,1,0:T(8,128)(2,1)S(1)}, u32[]{:S(2)}, u32[]{:S(2)}) %collective-permute-start.4) | collective-permute-done | bytes 131104 | tf_op jit(solution)/shard_map/ppermute | solution.py:30
  59.8 0.1 pad_maximum_fusion.own_ref
  59.8 3.5 %collective-permute-start.5 = (bf16[4,2,2,128,128]{4,3,2,1,0:T(8,128)(2,1)S(1)}, bf16[4,2,2,128,128]{4,3,2,1,0:T(8,128)(2,1)S(1)}, u32[]{:S(2)}, u32[]{:S(2)}) collective-permute-start(bf16[4,2,2,128,128]{4,3,2,1,0:T(8,128)(2,1)S(1)} %pad_maximum_fusion.own_ref), channel_id=1, source_target_pairs={{0,1},{1,0},{2,3},{3,2},{4,5},{5,4},{6,7},{7,6},{8,9},{9,8},{10,11... | collective-permute-start | bytes 1572872 | tf_op jit(solution)/shard_map/ppermute | solution.py:30
  63.4 0.1 stack.65.where_ref
  63.5 1.4 %collective-permute-done.5.other_ref = bf16[4,2,2,128,128]{4,3,2,1,0:T(8,128)(2,1)S(1)} collective-permute-done((bf16[4,2,2,128,128]{4,3,2,1,0:T(8,128)(2,1)S(1)}, bf16[4,2,2,128,128]{4,3,2,1,0:T(8,128)(2,1)S(1)}, u32[]{:S(2)}, u32[]{:S(2)}) %collective-permute-start.5) | collective-permute-done | bytes 524320 | tf_op jit(solution)/shard_map/ppermute | solution.py:30
  64.9 2.1 %shard_map.47 = bf16[16,2,128,128]{3,2,1,0:T(8,128)(2,1)} custom-call(s32[5]{0:T(128)S(1)} %stack.65.where_ref, bf16[4,2,2,128,128]{4,3,2,1,0:T(8,128)(2,1)S(1)} %pad_maximum_fusion.own_ref, bf16[4,2,2,128,128]{4,3,2,1,0:T(8,128)(2,1)S(1)} %collective-permute-done.5.other_ref, bf16[16,2,272,128]{3,2,1,0:T(8,128)(2,1)S(1)} %all-to-all-done.y_ref.lg_ref), custom_call_target="tpu_custom_call" | custom-call | flops 268435456 | bytes 4194304 | tf_op jit(solution)/shard_map/pallas_call | solution.py:378
  67.0 6.9 %all-to-all-start.1 = ((bf16[16,2,128,128]{3,2,1,0:T(8,128)(2,1)}), bf16[16,2,128,128]{3,2,1,0:T(8,128)(2,1)S(1)}, u32[]{:S(2)}, u32[]{:S(2)}) async-start(bf16[16,2,128,128]{3,2,1,0:T(8,128)(2,1)} %shard_map.47), calls=%async_computation.1 | async-start | bytes 2097152 | tf_op jit(solution)/shard_map/all_to_all | solution.py:386
  73.9 0.1 fusion.1
  74.1 0.6 tile.4
  74.7 8.5 %shard_map.48.plan_hbm = bf16[8,640,1024]{2,1,0:T(8,128)(2,1)} custom-call(f32[64,64]{1,0:T(8,128)} %bitcast.32, f32[64,32]{1,0:T(8,128)} %bitcast.38), custom_call_target="tpu_custom_call" | custom-call | flops 536870912 | bytes 6291456 | tf_op jit(solution)/shard_map/pallas_call | solution.py:391
  83.3 7.0 %all-to-all-done.1.force_ref = bf16[16,2,128,128]{3,2,1,0:T(8,128)(2,1)S(1)} async-done(((bf16[16,2,128,128]{3,2,1,0:T(8,128)(2,1)}), bf16[16,2,128,128]{3,2,1,0:T(8,128)(2,1)S(1)}, u32[]{:S(2)}, u32[]{:S(2)}) %all-to-all-start.1) | async-done | bytes 1048608 | tf_op jit(solution)/shard_map/all_to_all | solution.py:386
  90.3 8.4 %shard_map.49 = (bf16[16,2,128,128]{3,2,1,0:T(8,128)(2,1)S(1)}, bf16[128,128]{1,0:T(8,128)(2,1)S(1)}, f32[128,128]{1,0:T(8,128)S(1)}) custom-call(s32[5]{0:T(128)S(1)} %stack.65.where_ref, bf16[16,2,128,128]{3,2,1,0:T(8,128)(2,1)S(1)} %all-to-all-done.1.force_ref, bf16[16,2,272,128]{3,2,1,0:T(8,128)(2,1)S(1)} %all-to-all-done.y_ref.lg_ref, ...), custom_call_target="tpu_custom_call" | custom-call | flops 1073741824 | bytes 10485760 | tf_op jit(solution)/shard_map/pallas_call | solution.py:408
  98.6 8.0 %collective-permute-start.6 = (bf16[128,128]{1,0:T(8,128)(2,1)S(1)}, bf16[128,128]{1,0:T(8,128)(2,1)S(1)}, u32[]{:S(2)}, u32[]{:S(2)}) collective-permute-start(bf16[128,128]{1,0:T(8,128)(2,1)S(1)} %get-tuple-element.8), channel_id=1, source_target_pairs={{0,8},{8,0},{1,9},{9,1},{2,10},{10,2},{3,11},{11,3},{4,12},{12,4},... | collective-permute-start | bytes 98312 | tf_op jit(solution)/shard_map/ppermute | solution.py:30
  106.6 1.3 %collective-permute-done.6 = bf16[128,128]{1,0:T(8,128)(2,1)S(1)} collective-permute-done((bf16[128,128]{1,0:T(8,128)(2,1)S(1)}, bf16[128,128]{1,0:T(8,128)(2,1)S(1)}, u32[]{:S(2)}, u32[]{:S(2)}) %collective-permute-start.6) | collective-permute-done | bytes 32800 | tf_op jit(solution)/shard_map/ppermute | solution.py:30
  108.0 9.5 %all_to_all.15.own_ref = bf16[4,2,128,128]{3,2,1,0:T(8,128)(2,1)S(1)} all-to-all(bf16[4,2,128,128]{3,2,1,0:T(8,128)(2,1)S(1)} %broadcast_in_dim.5), channel_id=1, replica_groups=mesh['y'=4,'x'=4,'zh'=2,'zm'=2,'zq'=4,'c'=2] {'zq'}, dimensions={0} | all-to-all | bytes 524288 | tf_op jit(solution)/shard_map/all_to_all | solution.py:23
  117.5 6.4 %collective-permute-start.7 = (bf16[4,2,128,128]{3,2,1,0:T(8,128)(2,1)S(1)}, bf16[4,2,128,128]{3,2,1,0:T(8,128)(2,1)S(1)}, u32[]{:S(2)}, u32[]{:S(2)}) collective-permute-start(bf16[4,2,128,128]{3,2,1,0:T(8,128)(2,1)S(1)} %all_to_all.15.own_ref), channel_id=1, source_target_pairs={{0,1},{1,0},{2,3},{3,2},{4,5},{5,4},{6,7},{7,6},{8,9},{9,8},{10,11... | collective-permute-start | bytes 786440 | tf_op jit(solution)/shard_map/ppermute | solution.py:30
  124.0 1.1 collective-permute-done.7.other_ref
  125.1 1.5 %shard_map.50 = f32[2,64,128]{2,1,0:T(8,128)} custom-call(s32[5]{0:T(128)S(1)} %stack.65.where_ref, bf16[4,2,128,128]{3,2,1,0:T(8,128)(2,1)S(1)} %all_to_all.15.own_ref, bf16[4,2,128,128]{3,2,1,0:T(8,128)(2,1)S(1)} %collective-permute-done.7.other_ref, bf16[16,2,128,128]{3,2,1,0:T(8,128)(2,1)S(1)} %get-tuple-element.9.y_ref, ...), custom_call_target="tpu_custom_call" | custom-call | flops 134217728 | bytes 2097152 | tf_op jit(solution)/shard_map/pallas_call | solution.py:431
  (17 shorter events, 0.2 us)
Async XLA Ops:
  0.0 0.9 copy-start
  0.9 0.7 copy-start.1
  1.6 0.7 copy-start.3
  2.4 18.6 %collective-permute-start = (bf16[400,128]{1,0:T(8,128)(2,1)S(1)}, bf16[400,128]{1,0:T(8,128)(2,1)S(1)}, u32[]{:S(2)}, u32[]{:S(2)}) collective-permute-start(bf16[400,128]{1,0:T(8,128)(2,1)S(1)} %shard_map.46), channel_id=1, source_target_pairs={{0,16},{16,0},{1,17},{17,1},{2,18},{18,2},{3,19},{19,3},{4,20},{20... | collective-permute-start | bytes 307208 | tf_op jit(solution)/shard_map/ppermute | solution.py:30
  22.7 42.2 %all-to-all-start = ((bf16[16,2,272,128]{3,2,1,0:T(8,128)(2,1)}), bf16[16,2,272,128]{3,2,1,0:T(8,128)(2,1)S(1)}, u32[]{:S(2)}, u32[]{:S(2)}) async-start(bf16[16,2,272,128]{3,2,1,0:T(8,128)(2,1)} %broadcast_in_dim.4), calls=%async_computation | async-start | bytes 4456448 | tf_op jit(solution)/shard_map/all_to_all | solution.py:23
  29.7 13.3 %collective-permute-start.1 = (bf16[2,128,128]{2,1,0:T(8,128)(2,1)S(1)}, bf16[2,128,128]{2,1,0:T(8,128)(2,1)S(1)}, u32[]{:S(2)}, u32[]{:S(2)}) collective-permute-start(bf16[2,128,128]{2,1,0:T(8,128)(2,1)S(1)} %pad_maximum_fusion.3), channel_id=1, source_target_pairs={{0,8},{8,0},{1,9},{9,1},{2,10},{10,2},{3,11},{11,3},{4,12},{12,4},... | collective-permute-start | bytes 196616 | tf_op jit(solution)/shard_map/ppermute | solution.py:30
  43.1 11.7 %collective-permute-start.3 = (bf16[2,2,128,128]{3,2,1,0:T(8,128)(2,1)S(1)}, bf16[2,2,128,128]{3,2,1,0:T(8,128)(2,1)S(1)}, u32[]{:S(2)}, u32[]{:S(2)}) collective-permute-start(bf16[2,2,128,128]{3,2,1,0:T(8,128)(2,1)S(1)} %get-tuple-element.14), channel_id=1, source_target_pairs={{0,4},{2,6},{4,0},{6,2},{1,5},{3,7},{5,1},{7,3},{8,12},{10,14},{12... | collective-permute-start | bytes 393224 | tf_op jit(solution)/shard_map/ppermute | solution.py:30
  49.8 7.3 %collective-permute-start.2 = (bf16[2,2,128,128]{3,2,1,0:T(8,128)(2,1)S(1)}, bf16[2,2,128,128]{3,2,1,0:T(8,128)(2,1)S(1)}, u32[]{:S(2)}, u32[]{:S(2)}) collective-permute-start(bf16[2,2,128,128]{3,2,1,0:T(8,128)(2,1)S(1)} %get-tuple-element.14), channel_id=1, source_target_pairs={{0,2},{2,0},{4,6},{6,4},{1,3},{3,1},{5,7},{7,5},{8,10},{10,8},{12,... | collective-permute-start | bytes 393224 | tf_op jit(solution)/shard_map/ppermute | solution.py:30
  51.7 8.1 %collective-permute-start.4 = (bf16[2,2,128,128]{3,2,1,0:T(8,128)(2,1)S(1)}, bf16[2,2,128,128]{3,2,1,0:T(8,128)(2,1)S(1)}, u32[]{:S(2)}, u32[]{:S(2)}) collective-permute-start(bf16[2,2,128,128]{3,2,1,0:T(8,128)(2,1)S(1)} %get-tuple-element.14), channel_id=1, source_target_pairs={{0,6},{2,4},{4,2},{6,0},{1,7},{3,5},{5,3},{7,1},{8,14},{10,12},{12... | collective-permute-start | bytes 393224 | tf_op jit(solution)/shard_map/ppermute | solution.py:30
  59.8 5.1 %collective-permute-start.5 = (bf16[4,2,2,128,128]{4,3,2,1,0:T(8,128)(2,1)S(1)}, bf16[4,2,2,128,128]{4,3,2,1,0:T(8,128)(2,1)S(1)}, u32[]{:S(2)}, u32[]{:S(2)}) collective-permute-start(bf16[4,2,2,128,128]{4,3,2,1,0:T(8,128)(2,1)S(1)} %pad_maximum_fusion.own_ref), channel_id=1, source_target_pairs={{0,1},{1,0},{2,3},{3,2},{4,5},{5,4},{6,7},{7,6},{8,9},{9,8},{10,11... | collective-permute-start | bytes 1572872 | tf_op jit(solution)/shard_map/ppermute | solution.py:30
  67.0 23.3 %all-to-all-start.1 = ((bf16[16,2,128,128]{3,2,1,0:T(8,128)(2,1)}), bf16[16,2,128,128]{3,2,1,0:T(8,128)(2,1)S(1)}, u32[]{:S(2)}, u32[]{:S(2)}) async-start(bf16[16,2,128,128]{3,2,1,0:T(8,128)(2,1)} %shard_map.47), calls=%async_computation.1 | async-start | bytes 2097152 | tf_op jit(solution)/shard_map/all_to_all | solution.py:386
  74.7 15.5 %copy-start.2 = (f32[32]{0:T(128)S(1)}, f32[32]{0:T(128)}, u32[]{:S(2)}) copy-start(f32[32]{0:T(128)} %param.7) | copy-start | bytes 388
  98.6 9.3 %collective-permute-start.6 = (bf16[128,128]{1,0:T(8,128)(2,1)S(1)}, bf16[128,128]{1,0:T(8,128)(2,1)S(1)}, u32[]{:S(2)}, u32[]{:S(2)}) collective-permute-start(bf16[128,128]{1,0:T(8,128)(2,1)S(1)} %get-tuple-element.8), channel_id=1, source_target_pairs={{0,8},{8,0},{1,9},{9,1},{2,10},{10,2},{3,11},{11,3},{4,12},{12,4},... | collective-permute-start | bytes 98312 | tf_op jit(solution)/shard_map/ppermute | solution.py:30
  117.5 7.6 %collective-permute-start.7 = (bf16[4,2,128,128]{3,2,1,0:T(8,128)(2,1)S(1)}, bf16[4,2,128,128]{3,2,1,0:T(8,128)(2,1)S(1)}, u32[]{:S(2)}, u32[]{:S(2)}) collective-permute-start(bf16[4,2,128,128]{3,2,1,0:T(8,128)(2,1)S(1)} %all_to_all.15.own_ref), channel_id=1, source_target_pairs={{0,1},{1,0},{2,3},{3,2},{4,5},{5,4},{6,7},{7,6},{8,9},{9,8},{10,11... | collective-permute-start | bytes 786440 | tf_op jit(solution)/shard_map/ppermute | solution.py:30

commit v4 on v3

--- a/solution.py
+++ b/solution.py
@@ -25,18 +25,8 @@
     )
 
 
-def crossed(shard, axis, other):
-    peers = lax.axis_size(axis)
-    return lax.ppermute(shard, axis, [(k, k ^ other) for k in range(peers)])
-
-
 def swapped(shard, axis):
-    return crossed(shard, axis, 1)
-
-
-def in_order(own, other, axis):
-    first = lax.axis_index(axis) == 0
-    return jnp.stack([jnp.where(first, own, other), jnp.where(first, other, own)])
+    return lax.ppermute(shard, axis, [(0, 1), (1, 0)])
 
 
 def couplings(row, times):
@@ -99,14 +89,14 @@
 
 
 def first_collision(scale, where_ref, own_ref, other_ref, y_ref, out_ref, acc_ref):
-    zm, zq, core = where_ref[2], where_ref[3], where_ref[4]
+    core = where_ref[2]
     pieces = [
         (
-            [s_ref[d, e].reshape(256, 128) for e in range(2)],
-            [8 * (zm ^ e) + 2 * (zq ^ d) + side for e in range(2)],
+            [s_ref[q, m].reshape(256, 128) for m in range(2)],
+            [8 * m + 2 * q + side for m in range(2)],
         )
         for s_ref, side in ((own_ref, core), (other_ref, 1 - core))
-        for d in range(4)
+        for q in range(4)
     ]
     row_times_column(pieces, y_ref, acc_ref)
     for h in range(2):
@@ -119,9 +109,9 @@
 
 
 def last_collision(scale, where_ref, own_ref, other_ref, y_ref, base_ref, out_ref, acc_ref):
-    zm, core = where_ref[2], where_ref[4]
+    core = where_ref[2]
     pieces = [
-        ([s_ref[q, e] for e in range(2)], [8 * (zm ^ e) + 2 * q + side for e in range(2)])
+        ([s_ref[q, m] for m in range(2)], [8 * m + 2 * q + side for m in range(2)])
         for s_ref, side in ((own_ref, core), (other_ref, 1 - core))
         for q in range(4)
     ]
@@ -354,9 +344,7 @@
     orbitals = coupling.shape[0]
     horizon = damping.shape[0] * lax.axis_size(FIRST)
     scale = 1.0 / (horizon * math.sqrt(orbitals))
-    where = jnp.stack(
-        [lax.axis_index(axis) for axis in (PLANE, "zh", "zm", "zq", "c")]
-    ).astype(jnp.int32)
+    where = jnp.stack([lax.axis_index(axis) for axis in (PLANE, "zh", "c")]).astype(jnp.int32)
 
     strength = coupling.reshape(1, 32)
     message = call(
@@ -367,12 +355,11 @@
         40 * 64 * 128,
         400 << 10,
     )(window.reshape(2, 2, 64, 128), damping, strength)
-    pair = in_order(message, swapped(message, "zh"), "zh")
+    pair = lax.all_gather(message, "zh")
     lg = from_everyone(pair[:, :272], PLANE)
 
-    s_rows = pair[:, 272:]
-    s_rows = jnp.stack([s_rows, swapped(s_rows, "zm")])
-    s_rows = jnp.stack([s_rows] + [crossed(s_rows, "zq", d) for d in (1, 2, 3)])
+    s_rows = lax.all_gather(pair[:, 272:], "zm")
+    s_rows = lax.all_gather(s_rows, "zq")
     s_other = swapped(s_rows, "c")
 
     c1 = call(
@@ -426,7 +413,7 @@
         44,
     )(where, force, lg, strength, plan)
 
-    t_rows = from_everyone(jnp.stack([t2, swapped(t2, "zm")]), "zq")
+    t_rows = lax.all_gather(lax.all_gather(t2, "zm"), "zq")
     t_other = swapped(t_rows, "c")
     out = call(
         functools.partial(last_collision, scale),

time: 127 us -> 126 us (level)
  blocking collectives: 9.54 us -> 63.6 us
  starting transfers between devices: 69.8 us -> 27.1 us
  waiting for transfers between devices: 21.5 us -> 9.54 us
    all_gather x0 -> x5, blocking collectives: none -> 63.6 us  [the longest x2 19.6 us: shards(): t_rows = lax.all_gather(lax.all_gather(t2, 'zm'), 'zq')]
    ppermute x8 -> x2, starting transfers between devices: 55.9 us -> 13.6 us  [swapped(): return lax.ppermute(shard, axis, [(0, 1), (1, 0)])]
    ppermute x8 -> x2, waiting for transfers between devices: 14.5 us -> 2.57 us  [swapped(): return lax.ppermute(shard, axis, [(0, 1), (1, 0)])]
    all_to_all x1 -> x0, blocking collectives: 9.54 us -> none  [from_everyone(): lax.all_to_all(jnp.broadcast_to(shard[None], (peers, *shard.shape)), axis...]
  transfers between devices with their start and end apart: 10 -> 4, of which waited for: 8 -> 3; matrix products, arithmetic and copies ran while one was open for 1% -> 1% of each run, Pallas kernels for 7% -> 7%
where the time goes in v4:
time: 126 us
  blocking collectives  63.6 us (50%)
  starting transfers between devices  27.1 us (22%)
  Pallas kernels  20.6 us (16%)
  waiting for transfers between devices  9.54 us (8%)
  local copies, waits for them, and re-layouts  4.63 us (4%)
    all_gather x2, blocking collectives, shards(): t_rows = lax.all_gather(lax.all_gather(t2, 'zm'), 'zq')  19.6 us
    all_gather x1, blocking collectives, shards(): pair = lax.all_gather(message, 'zh')  17.4 us
    all_gather x1, blocking collectives, shards(): s_rows = lax.all_gather(s_rows, 'zq')  14.6 us
    ppermute x2, starting transfers between devices, swapped(): return lax.ppermute(shard, axis, [(0, 1), (1, 0)])  13.6 us
    all_gather x1, blocking collectives, shards(): s_rows = lax.all_gather(pair[:, 272:], 'zm')  12.1 us
    pallas_call x1, Pallas kernels, shards(): call(build_steps, shape(8, 640, 1024), [pltpu.VMEM((8, 512, 640), bf16),...  8.55 us
    pallas_call x1, Pallas kernels, shards(): call(predict, (shape(16, 2, 128, 128), shape(128, 128), shape(128, 128, k...  8.36 us
    all_to_all x1, starting transfers between devices, from_everyone(): lax.all_to_all(jnp.broadcast_to(shard[None], (peers, *shard.shape)), axis...  7 us
  transfers between devices with their start and end apart: 4, of which 3 were waited for; matrix products, arithmetic and copies ran while one was open for 1% of the time, Pallas kernels for 7%

profile of v4, /device:TPU:1, one launch (start us, length us, event | category | flops | bytes accessed | tf_op | source)
XLA Modules:
  0.0 125.7 jit_solution(9381954409143127984)
XLA Ops:
  0.0 0.0 copy-start
  0.0 0.9 copy-done
  0.9 0.0 copy-start.1
  0.9 0.7 copy-done.1
  1.6 0.0 copy-start.3
  1.6 0.7 copy-done.3
  2.2 0.2 shard_map.46
  2.4 17.4 %all-gather = bf16[800,128]{1,0:T(8,128)(2,1)S(1)} all-gather(bf16[400,128]{1,0:T(8,128)(2,1)S(1)} %shard_map.46), channel_id=2, replica_groups=mesh['y'=4,'x'=4,'zh'=2,'zm'=2,'zq'=4,'c'=2] {'zh'}, dimensions={0}, use_global_device_ids=true | all-gather | bytes 307200 | tf_op jit(solution)/shard_map/all_gather | solution.py:358
  19.8 1.7 %broadcast_in_dim.2 = bf16[16,2,272,128]{3,2,1,0:T(8,128)(2,1)} broadcast(bf16[2,272,128]{2,1,0:T(8,128)(2,1)S(1)} %slice.25), dimensions={1,2,3} | broadcast | bytes 2367488 | tf_op jit(solution)/shard_map/broadcast_in_dim | solution.py:24
  21.4 7.0 %all-to-all-start = ((bf16[16,2,272,128]{3,2,1,0:T(8,128)(2,1)}), bf16[16,2,272,128]{3,2,1,0:T(8,128)(2,1)S(1)}, u32[]{:S(2)}, u32[]{:S(2)}) async-start(bf16[16,2,272,128]{3,2,1,0:T(8,128)(2,1)} %broadcast_in_dim.2), calls=%async_computation | async-start | bytes 4456448 | tf_op jit(solution)/shard_map/all_to_all | solution.py:23
  28.5 12.1 %all-gather.1 = bf16[4,128,128]{2,1,0:T(8,128)(2,1)S(1)} all-gather(bf16[2,128,128]{2,1,0:T(8,128)(2,1)S(1)} %slice.24), channel_id=3, replica_groups=mesh['y'=4,'x'=4,'zh'=2,'zm'=2,'zq'=4,'c'=2] {'zm'}, dimensions={0}, use_global_device_ids=true | all-gather | bytes 196608 | tf_op jit(solution)/shard_map/all_gather | solution.py:361
  40.6 14.6 %all-gather.2 = bf16[8,2,128,128]{3,2,1,0:T(8,128)(2,1)S(1)} all-gather(bf16[2,2,128,128]{3,2,1,0:T(8,128)(2,1)S(1)} %bitcast.26), channel_id=4, replica_groups=mesh['y'=4,'x'=4,'zh'=2,'zm'=2,'zq'=4,'c'=2] {'zq'}, dimensions={0}, use_global_device_ids=true | all-gather | bytes 655360 | tf_op jit(solution)/shard_map/all_gather | solution.py:362
  55.2 5.9 %collective-permute-start = (bf16[4,2,2,128,128]{4,3,2,1,0:T(8,128)(2,1)S(1)}, bf16[4,2,2,128,128]{4,3,2,1,0:T(8,128)(2,1)S(1)}, u32[]{:S(2)}, u32[]{:S(2)}) collective-permute-start(bf16[4,2,2,128,128]{4,3,2,1,0:T(8,128)(2,1)S(1)} %bitcast.17), channel_id=1, source_target_pairs={{0,1},{1,0},{2,3},{3,2},{4,5},{5,4},{6,7},{7,6},{8,9},{9,8},{10,11... | collective-permute-start | bytes 1572872 | tf_op jit(solution)/shard_map/ppermute | solution.py:29
  61.1 0.1 pad_add_fusion.where_ref
  61.1 1.4 %collective-permute-done.other_ref = bf16[4,2,2,128,128]{4,3,2,1,0:T(8,128)(2,1)S(1)} collective-permute-done((bf16[4,2,2,128,128]{4,3,2,1,0:T(8,128)(2,1)S(1)}, bf16[4,2,2,128,128]{4,3,2,1,0:T(8,128)(2,1)S(1)}, u32[]{:S(2)}, u32[]{:S(2)}) %collective-permute-start) | collective-permute-done | bytes 524320 | tf_op jit(solution)/shard_map/ppermute | solution.py:29
  62.6 0.0 all-to-all-done.y_ref.lg_ref
  62.6 2.1 %shard_map.47 = bf16[16,2,128,128]{3,2,1,0:T(8,128)(2,1)} custom-call(s32[3]{0:T(128)S(1)} %pad_add_fusion.where_ref, bf16[4,2,2,128,128]{4,3,2,1,0:T(8,128)(2,1)S(1)} %bitcast.18, bf16[4,2,2,128,128]{4,3,2,1,0:T(8,128)(2,1)S(1)} %collective-permute-done.other_ref, bf16[16,2,272,128]{3,2,1,0:T(8,128)(2,1)S(1)} %all-to-all-done.y_ref.lg_ref), custom_call_target="tpu_custom_call" | custom-call | flops 268435456 | bytes 4194304 | tf_op jit(solution)/shard_map/pallas_call | solution.py:365
  64.6 6.5 %all-to-all-start.1 = ((bf16[16,2,128,128]{3,2,1,0:T(8,128)(2,1)}), bf16[16,2,128,128]{3,2,1,0:T(8,128)(2,1)S(1)}, u32[]{:S(2)}, u32[]{:S(2)}) async-start(bf16[16,2,128,128]{3,2,1,0:T(8,128)(2,1)} %shard_map.47), calls=%async_computation.1 | async-start | bytes 2097152 | tf_op jit(solution)/shard_map/all_to_all | solution.py:373
  71.2 0.1 fusion.1
  71.2 0.1 copy.6
  71.3 0.6 tile.4
  71.9 0.0 copy-start.2
  71.9 8.5 %shard_map.48.plan_hbm = bf16[8,640,1024]{2,1,0:T(8,128)(2,1)} custom-call(f32[64,64]{1,0:T(8,128)} %bitcast.28, f32[64,32]{1,0:T(8,128)} %bitcast.30), custom_call_target="tpu_custom_call" | custom-call | flops 536870912 | bytes 6291456 | tf_op jit(solution)/shard_map/pallas_call | solution.py:378
  80.5 7.0 %all-to-all-done.1.force_ref = bf16[16,2,128,128]{3,2,1,0:T(8,128)(2,1)S(1)} async-done(((bf16[16,2,128,128]{3,2,1,0:T(8,128)(2,1)}), bf16[16,2,128,128]{3,2,1,0:T(8,128)(2,1)S(1)}, u32[]{:S(2)}, u32[]{:S(2)}) %all-to-all-start.1) | async-done | bytes 1048608 | tf_op jit(solution)/shard_map/all_to_all | solution.py:373
  87.5 0.0 copy-done.2
  87.5 8.4 %shard_map.49 = (bf16[16,2,128,128]{3,2,1,0:T(8,128)(2,1)S(1)}, bf16[128,128]{1,0:T(8,128)(2,1)S(1)}, f32[128,128]{1,0:T(8,128)S(1)}) custom-call(s32[3]{0:T(128)S(1)} %pad_add_fusion.where_ref, bf16[16,2,128,128]{3,2,1,0:T(8,128)(2,1)S(1)} %all-to-all-done.1.force_ref, bf16[16,2,272,128]{3,2,1,0:T(8,128)(2,1)S(1)} %all-to-all-done.y_ref.lg_ref, ...), custom_call_target="tpu_custom_call" | custom-call | flops 1073741824 | bytes 10485760 | tf_op jit(solution)/shard_map/pallas_call | solution.py:395
  95.8 8.1 %all-gather.3 = bf16[256,128]{1,0:T(8,128)(2,1)S(1)} all-gather(bf16[128,128]{1,0:T(8,128)(2,1)S(1)} %get-tuple-element.8), channel_id=5, replica_groups=mesh['y'=4,'x'=4,'zh'=2,'zm'=2,'zq'=4,'c'=2] {'zm'}, dimensions={0}, use_global_device_ids=true | all-gather | bytes 98304 | tf_op jit(solution)/shard_map/all_gather | solution.py:416
  103.9 11.5 %all-gather.4 = bf16[8,128,128]{2,1,0:T(8,128)(2,1)S(1)} all-gather(bf16[2,128,128]{2,1,0:T(8,128)(2,1)S(1)} %bitcast.27), channel_id=6, replica_groups=mesh['y'=4,'x'=4,'zh'=2,'zm'=2,'zq'=4,'c'=2] {'zq'}, dimensions={0}, use_global_device_ids=true | all-gather | bytes 327680 | tf_op jit(solution)/shard_map/all_gather | solution.py:416
  115.4 7.7 %collective-permute-start.1 = (bf16[4,2,128,128]{3,2,1,0:T(8,128)(2,1)S(1)}, bf16[4,2,128,128]{3,2,1,0:T(8,128)(2,1)S(1)}, u32[]{:S(2)}, u32[]{:S(2)}) collective-permute-start(bf16[4,2,128,128]{3,2,1,0:T(8,128)(2,1)S(1)} %bitcast.19), channel_id=1, source_target_pairs={{0,1},{1,0},{2,3},{3,2},{4,5},{5,4},{6,7},{7,6},{8,9},{9,8},{10,11... | collective-permute-start | bytes 786440 | tf_op jit(solution)/shard_map/ppermute | solution.py:29
  123.1 1.1 collective-permute-done.1.other_ref
  124.3 1.5 %shard_map.50 = f32[2,64,128]{2,1,0:T(8,128)} custom-call(s32[3]{0:T(128)S(1)} %pad_add_fusion.where_ref, bf16[4,2,128,128]{3,2,1,0:T(8,128)(2,1)S(1)} %bitcast.20, bf16[4,2,128,128]{3,2,1,0:T(8,128)(2,1)S(1)} %collective-permute-done.1.other_ref, bf16[16,2,128,128]{3,2,1,0:T(8,128)(2,1)S(1)} %get-tuple-element.9.y_ref, ...), custom_call_target="tpu_custom_call" | custom-call | flops 134217728 | bytes 2097152 | tf_op jit(solution)/shard_map/pallas_call | solution.py:418
  (4 shorter events, 0.0 us)
Async XLA Ops:
  0.0 0.9 copy-start
  0.9 0.7 copy-start.1
  1.6 0.7 copy-start.3
  21.4 41.1 %all-to-all-start = ((bf16[16,2,272,128]{3,2,1,0:T(8,128)(2,1)}), bf16[16,2,272,128]{3,2,1,0:T(8,128)(2,1)S(1)}, u32[]{:S(2)}, u32[]{:S(2)}) async-start(bf16[16,2,272,128]{3,2,1,0:T(8,128)(2,1)} %broadcast_in_dim.2), calls=%async_computation | async-start | bytes 4456448 | tf_op jit(solution)/shard_map/all_to_all | solution.py:23
  55.2 7.4 %collective-permute-start = (bf16[4,2,2,128,128]{4,3,2,1,0:T(8,128)(2,1)S(1)}, bf16[4,2,2,128,128]{4,3,2,1,0:T(8,128)(2,1)S(1)}, u32[]{:S(2)}, u32[]{:S(2)}) collective-permute-start(bf16[4,2,2,128,128]{4,3,2,1,0:T(8,128)(2,1)S(1)} %bitcast.17), channel_id=1, source_target_pairs={{0,1},{1,0},{2,3},{3,2},{4,5},{5,4},{6,7},{7,6},{8,9},{9,8},{10,11... | collective-permute-start | bytes 1572872 | tf_op jit(solution)/shard_map/ppermute | solution.py:29
  64.6 22.8 %all-to-all-start.1 = ((bf16[16,2,128,128]{3,2,1,0:T(8,128)(2,1)}), bf16[16,2,128,128]{3,2,1,0:T(8,128)(2,1)S(1)}, u32[]{:S(2)}, u32[]{:S(2)}) async-start(bf16[16,2,128,128]{3,2,1,0:T(8,128)(2,1)} %shard_map.47), calls=%async_computation.1 | async-start | bytes 2097152 | tf_op jit(solution)/shard_map/all_to_all | solution.py:373
  71.9 15.5 %copy-start.2 = (f32[32]{0:T(128)S(1)}, f32[32]{0:T(128)}, u32[]{:S(2)}) copy-start(f32[32]{0:T(128)} %param.7) | copy-start | bytes 388
  115.4 8.9 %collective-permute-start.1 = (bf16[4,2,128,128]{3,2,1,0:T(8,128)(2,1)S(1)}, bf16[4,2,128,128]{3,2,1,0:T(8,128)(2,1)S(1)}, u32[]{:S(2)}, u32[]{:S(2)}) collective-permute-start(bf16[4,2,128,128]{3,2,1,0:T(8,128)(2,1)S(1)} %bitcast.19), channel_id=1, source_target_pairs={{0,1},{1,0},{2,3},{3,2},{4,5},{5,4},{6,7},{7,6},{8,9},{9,8},{10,11... | collective-permute-start | bytes 786440 | tf_op jit(solution)/shard_map/ppermute | solution.py:29

commit v5 on v4

--- a/solution.py
+++ b/solution.py
@@ -286,24 +286,34 @@
     for k in range(7):
         hom_ref[k + 1] = triple(rows_of(hom, k))
         carry_ref[k + 1] = triple(rows_of(carry, k))
-    factor = couplings(coupling_ref[...], 8)
-
-    def whole(k, _):
+    factor = couplings(coupling_ref[...], 2)
+
+    def piece(k, u):
+        n, row = 4 * k + u, u * 64
+
+        rows = jnp.concatenate(
+            [p_ref[k, pl.ds(row, 64), 0:608], p_ref[k, pl.ds(row + 256, 64), 0:608]], axis=0
+        )
+        source = jnp.concatenate([f_ref[k], f_ref[k], carry_ref[k]], axis=0)
+        real, imag = parts(dot(rows, source))
+        j_at, h_at = 2 * k + u // 2, u % 2
+        g = lg_ref[j_at, h_at, 128:256].astype(f32)
+        spectral_re, spectral_im = spectral(real, imag, g[:64], g[64:], factor)
+        s = jnp.concatenate([spectral_re, spectral_im], axis=1).astype(bf16)
+        s_ref[k, pl.ds(row, 64)] = s
+        y_ref[j_at, h_at, 0:64] = real.astype(bf16)
+        y_ref[j_at, h_at, 64:128] = imag.astype(bf16)
+        x_ref[n, 0:64], x_ref[n, 64:128] = real, imag
+
+    def block(k, _):
         fetch(k).wait()
-        source = jnp.concatenate([f_ref[k], f_ref[k], carry_ref[k]], axis=0)
-        real, imag = parts(dot(p_ref[k, :, 0:608], source))
-        x_ref[k, 0:256], x_ref[k, 256:512] = real, imag
-        g = block_of(lg_ref, k, 128).astype(f32)
-        spectral_re, spectral_im = spectral(real, imag, g[:, :128], g[:, 128:], factor)
-        s = jnp.concatenate([spectral_re, spectral_im], axis=1).astype(bf16)
-        s_ref[k] = s
-        for part, y in enumerate((real.astype(bf16), imag.astype(bf16))):
-            for u in range(4):
-                y_ref[2 * k + u // 2, u % 2, 64 * part : 64 * part + 64] = y[64 * u : 64 * u + 64]
-        put_end(k, s)
+        for u in range(4):
+            piece(k, u)
         return 0
 
-    lax.fori_loop(0, 8, whole, 0)
+    lax.fori_loop(0, 8, block, 0)
+    for k in range(8):
+        put_end(k, s_ref[k])
     carry = coarse()
     carry_ref[0] = jnp.zeros((96, 256), bf16)
     for k in range(7):
@@ -319,9 +329,24 @@
     real, imag = parts(dot(p_own[:, 0:608], source))
     t_ref[0:64], t_ref[64:128] = real.astype(bf16), imag.astype(bf16)
     real, imag = parts(dot(p_own[:, 512:608], hom_ref[own_block]))
-    base = own(x_ref)
+    base = x_ref[2 * j + h]
     base_ref[0:64] = 0.5 * (base[0:64] + real)
     base_ref[64:128] = 0.5 * (base[64:128] + imag)
+
+
+PRED_SCRATCH = [
+    pltpu.VMEM((8, 512, 640), bf16),
+    pltpu.VMEM((8, 64, 512), bf16),
+    pltpu.VMEM((8, 64, 896), bf16),
+    pltpu.VMEM((8, 256, 256), bf16),
+    pltpu.VMEM((8, 256, 256), bf16),
+    pltpu.VMEM((3, 8, 32, 256), bf16),
+    pltpu.VMEM((8, 96, 256), bf16),
+    pltpu.VMEM((8, 96, 256), bf16),
+    pltpu.VMEM((32, 128, 128), f32),
+    pltpu.SemaphoreType.DMA((10,)),
+]
+FIRST_SCRATCH = [pltpu.VMEM((256, 256), f32)]
 
 
 def call(kernel, outs, scratch, ins, flops, moved, grant=24, place=VMEM):
@@ -331,7 +356,7 @@
         in_specs=ins,
         out_specs=jax.tree.map(lambda _: place, outs),
         scratch_shapes=scratch,
-        compiler_params=pltpu.CompilerParams(vmem_limit_bytes=grant << 20),
+        compiler_params=pltpu.CompilerParams(vmem_limit_bytes=int(grant * (1 << 20))),
         cost_estimate=pl.CostEstimate(flops=flops, bytes_accessed=moved, transcendentals=0),
     )
 
@@ -354,6 +379,7 @@
         [VMEM, VMEM, VMEM],
         40 * 64 * 128,
         400 << 10,
+        63.9,
     )(window.reshape(2, 2, 64, 128), damping, strength)
     pair = lax.all_gather(message, "zh")
     lg = from_everyone(pair[:, :272], PLANE)
@@ -365,7 +391,7 @@
     c1 = call(
         functools.partial(first_collision, scale),
         shape(16, 2, 128, 128),
-        [pltpu.VMEM((256, 256), f32)],
+        FIRST_SCRATCH,
         [SMEM, VMEM, VMEM, VMEM],
         2 * 256 * 256 * 2048,
         4 << 20,
@@ -395,25 +421,14 @@
     y2, t2, base = call(
         predict,
         (shape(16, 2, 128, 128), shape(128, 128), shape(128, 128, kind=f32)),
-        [
-            pltpu.VMEM((8, 512, 640), bf16),
-            pltpu.VMEM((8, 64, 512), bf16),
-            pltpu.VMEM((8, 64, 896), bf16),
-            pltpu.VMEM((8, 256, 256), bf16),
-            pltpu.VMEM((8, 256, 256), bf16),
-            pltpu.VMEM((3, 8, 32, 256), bf16),
-            pltpu.VMEM((8, 96, 256), bf16),
-            pltpu.VMEM((8, 96, 256), bf16),
-            pltpu.VMEM((8, 512, 128), f32),
-            pltpu.SemaphoreType.DMA((10,)),
-        ],
+        PRED_SCRATCH,
         [SMEM] + [VMEM] * 3 + [HBM],
         2 * 8 * 512 * 512 * 128 * 2,
         10 << 20,
         44,
     )(where, force, lg, strength, plan)
 
-    t_rows = lax.all_gather(lax.all_gather(t2, "zm"), "zq")
+    t_rows = from_everyone(lax.all_gather(t2, "zm"), "zq")
     t_other = swapped(t_rows, "c")
     out = call(
         functools.partial(last_collision, scale),

time: 126 us -> 121 us (0.960)
  local copies, waits for them, and re-layouts: 4.63 us -> 2.43 us
  blocking collectives: 63.6 us -> 62 us
  starting transfers between devices: 27.1 us -> 25.7 us
    all_gather x2 -> x1, blocking collectives: 19.6 us -> 8.09 us  [shards(): t_rows = from_everyone(lax.all_gather(t2, 'zm'), 'zq')]
    all_to_all x0 -> x1, blocking collectives: none -> 8.88 us  [from_everyone(): lax.all_to_all(jnp.broadcast_to(shard[None], (peers, *shard.shape)), axis...]
    unnamed x8 -> x2, local copies, waits for them, and re-layouts: 2.24 us -> 0.01 us
    pallas_call x1, Pallas kernels: 0.16 us -> 1.72 us  [shards(): call(compose, shape(400, 128), [], [VMEM, VMEM, VMEM], 40 * 64 * 128, 400...]
    pallas_call x1, Pallas kernels: 8.36 us -> 7 us  [shards(): call(predict, (shape(16, 2, 128, 128), shape(128, 128), shape(128, 128, k...]
where the time goes in v5:
time: 121 us
  blocking collectives  62 us (51%)
  starting transfers between devices  25.7 us (21%)
  Pallas kernels  20.8 us (17%)
  waiting for transfers between devices  9.53 us (8%)
  local copies, waits for them, and re-layouts  2.43 us (2%)
    all_gather x1, blocking collectives, shards(): pair = lax.all_gather(message, 'zh')  17.6 us
    all_gather x1, blocking collectives, shards(): s_rows = lax.all_gather(s_rows, 'zq')  15.5 us
    ppermute x2, starting transfers between devices, swapped(): return lax.ppermute(shard, axis, [(0, 1), (1, 0)])  12.4 us
    all_gather x1, blocking collectives, shards(): s_rows = lax.all_gather(pair[:, 272:], 'zm')  12 us
    all_to_all x1, blocking collectives, from_everyone(): lax.all_to_all(jnp.broadcast_to(shard[None], (peers, *shard.shape)), axis...  8.88 us
    pallas_call x1, Pallas kernels, shards(): call(build_steps, shape(8, 640, 1024), [pltpu.VMEM((8, 512, 640), bf16),...  8.57 us
    all_gather x1, blocking collectives, shards(): t_rows = from_everyone(lax.all_gather(t2, 'zm'), 'zq')  8.09 us
    pallas_call x1, Pallas kernels, shards(): call(predict, (shape(16, 2, 128, 128), shape(128, 128), shape(128, 128, k...  7 us
  transfers between devices with their start and end apart: 4, of which 3 were waited for; matrix products, arithmetic and copies ran while one was open for 1% of the time, Pallas kernels for 7%

profile of v5, /device:TPU:1, one launch (start us, length us, event | category | flops | bytes accessed | tf_op | source)
XLA Modules:
  0.0 120.8 jit_solution(859440222943449875)
XLA Ops:
  0.0 1.7 %shard_map.46 = bf16[400,128]{1,0:T(8,128)(2,1)} custom-call(f32[2,2,64,128]{3,2,1,0:T(8,128)} %bitcast.25, f32[2,32]{1,0:T(2,128)} %damp_ref.1, f32[1,32]{1,0:T(1,128)} %bitcast.18), custom_call_target="tpu_custom_call" | custom-call | flops 327680 | bytes 409600 | tf_op jit(solution)/shard_map/pallas_call | solution.py:375
  1.7 17.6 %all-gather = bf16[800,128]{1,0:T(8,128)(2,1)S(1)} all-gather(bf16[400,128]{1,0:T(8,128)(2,1)} %shard_map.46), channel_id=2, replica_groups=mesh['y'=4,'x'=4,'zh'=2,'zm'=2,'zq'=4,'c'=2] {'zh'}, dimensions={0}, use_global_device_ids=true | all-gather | bytes 307200 | tf_op jit(solution)/shard_map/all_gather | solution.py:384
  19.4 1.7 %broadcast_in_dim.4 = bf16[16,2,272,128]{3,2,1,0:T(8,128)(2,1)} broadcast(bf16[2,272,128]{2,1,0:T(8,128)(2,1)S(1)} %slice.25), dimensions={1,2,3} | broadcast | bytes 2367488 | tf_op jit(solution)/shard_map/broadcast_in_dim | solution.py:24
  21.0 7.0 %all-to-all-start = ((bf16[16,2,272,128]{3,2,1,0:T(8,128)(2,1)}), bf16[16,2,272,128]{3,2,1,0:T(8,128)(2,1)S(1)}, u32[]{:S(2)}, u32[]{:S(2)}) async-start(bf16[16,2,272,128]{3,2,1,0:T(8,128)(2,1)} %broadcast_in_dim.4), calls=%async_computation | async-start | bytes 4456448 | tf_op jit(solution)/shard_map/all_to_all | solution.py:23
  28.0 12.0 %all-gather.1 = bf16[4,128,128]{2,1,0:T(8,128)(2,1)S(1)} all-gather(bf16[2,128,128]{2,1,0:T(8,128)(2,1)S(1)} %slice.24), channel_id=3, replica_groups=mesh['y'=4,'x'=4,'zh'=2,'zm'=2,'zq'=4,'c'=2] {'zm'}, dimensions={0}, use_global_device_ids=true | all-gather | bytes 196608 | tf_op jit(solution)/shard_map/all_gather | solution.py:387
  40.0 15.5 %all-gather.2 = bf16[8,2,128,128]{3,2,1,0:T(8,128)(2,1)S(1)} all-gather(bf16[2,2,128,128]{3,2,1,0:T(8,128)(2,1)S(1)} %bitcast.22), channel_id=4, replica_groups=mesh['y'=4,'x'=4,'zh'=2,'zm'=2,'zq'=4,'c'=2] {'zq'}, dimensions={0}, use_global_device_ids=true | all-gather | bytes 655360 | tf_op jit(solution)/shard_map/all_gather | solution.py:388
  55.5 5.2 %collective-permute-start = (bf16[4,2,2,128,128]{4,3,2,1,0:T(8,128)(2,1)S(1)}, bf16[4,2,2,128,128]{4,3,2,1,0:T(8,128)(2,1)S(1)}, u32[]{:S(2)}, u32[]{:S(2)}) collective-permute-start(bf16[4,2,2,128,128]{4,3,2,1,0:T(8,128)(2,1)S(1)} %bitcast.16), channel_id=1, source_target_pairs={{0,1},{1,0},{2,3},{3,2},{4,5},{5,4},{6,7},{7,6},{8,9},{9,8},{10,11... | collective-permute-start | bytes 1572872 | tf_op jit(solution)/shard_map/ppermute | solution.py:29
  60.7 0.1 pad_add_fusion.where_ref
  60.8 1.4 %collective-permute-done.other_ref = bf16[4,2,2,128,128]{4,3,2,1,0:T(8,128)(2,1)S(1)} collective-permute-done((bf16[4,2,2,128,128]{4,3,2,1,0:T(8,128)(2,1)S(1)}, bf16[4,2,2,128,128]{4,3,2,1,0:T(8,128)(2,1)S(1)}, u32[]{:S(2)}, u32[]{:S(2)}) %collective-permute-start) | collective-permute-done | bytes 524320 | tf_op jit(solution)/shard_map/ppermute | solution.py:29
  62.2 0.0 all-to-all-done.y_ref.lg_ref
  62.2 2.1 %shard_map.47 = bf16[16,2,128,128]{3,2,1,0:T(8,128)(2,1)} custom-call(s32[3]{0:T(128)S(1)} %pad_add_fusion.where_ref, bf16[4,2,2,128,128]{4,3,2,1,0:T(8,128)(2,1)S(1)} %bitcast.17, bf16[4,2,2,128,128]{4,3,2,1,0:T(8,128)(2,1)S(1)} %collective-permute-done.other_ref, bf16[16,2,272,128]{3,2,1,0:T(8,128)(2,1)S(1)} %all-to-all-done.y_ref.lg_ref), custom_call_target="tpu_custom_call" | custom-call | flops 268435456 | bytes 4194304 | tf_op jit(solution)/shard_map/pallas_call | solution.py:391
  64.2 6.3 %all-to-all-start.1 = ((bf16[16,2,128,128]{3,2,1,0:T(8,128)(2,1)}), bf16[16,2,128,128]{3,2,1,0:T(8,128)(2,1)S(1)}, u32[]{:S(2)}, u32[]{:S(2)}) async-start(bf16[16,2,128,128]{3,2,1,0:T(8,128)(2,1)} %shard_map.47), calls=%async_computation.1 | async-start | bytes 2097152 | tf_op jit(solution)/shard_map/all_to_all | solution.py:399
  70.6 0.1 fusion.1
  70.7 0.1 copy.6
  70.8 0.6 tile.4
  71.4 0.0 copy-start
  71.4 8.6 %shard_map.48.plan_hbm = bf16[8,640,1024]{2,1,0:T(8,128)(2,1)} custom-call(f32[64,64]{1,0:T(8,128)} %bitcast.24, f32[64,32]{1,0:T(8,128)} %bitcast.27), custom_call_target="tpu_custom_call" | custom-call | flops 536870912 | bytes 6291456 | tf_op jit(solution)/shard_map/pallas_call | solution.py:404
  80.0 7.0 %all-to-all-done.1.force_ref = bf16[16,2,128,128]{3,2,1,0:T(8,128)(2,1)S(1)} async-done(((bf16[16,2,128,128]{3,2,1,0:T(8,128)(2,1)}), bf16[16,2,128,128]{3,2,1,0:T(8,128)(2,1)S(1)}, u32[]{:S(2)}, u32[]{:S(2)}) %all-to-all-start.1) | async-done | bytes 1048608 | tf_op jit(solution)/shard_map/all_to_all | solution.py:399
  86.9 0.0 copy-done
  86.9 7.0 %shard_map.49 = (bf16[16,2,128,128]{3,2,1,0:T(8,128)(2,1)S(1)}, bf16[128,128]{1,0:T(8,128)(2,1)S(1)}, f32[128,128]{1,0:T(8,128)S(1)}) custom-call(s32[3]{0:T(128)S(1)} %pad_add_fusion.where_ref, bf16[16,2,128,128]{3,2,1,0:T(8,128)(2,1)S(1)} %all-to-all-done.1.force_ref, bf16[16,2,272,128]{3,2,1,0:T(8,128)(2,1)S(1)} %all-to-all-done.y_ref.lg_ref, ...), custom_call_target="tpu_custom_call" | custom-call | flops 1073741824 | bytes 10485760 | tf_op jit(solution)/shard_map/pallas_call | solution.py:421
  93.9 8.1 %all-gather.3 = bf16[256,128]{1,0:T(8,128)(2,1)S(1)} all-gather(bf16[128,128]{1,0:T(8,128)(2,1)S(1)} %get-tuple-element.8), channel_id=5, replica_groups=mesh['y'=4,'x'=4,'zh'=2,'zm'=2,'zq'=4,'c'=2] {'zm'}, dimensions={0}, use_global_device_ids=true | all-gather | bytes 98304 | tf_op jit(solution)/shard_map/all_gather | solution.py:431
  102.1 8.9 %all_to_all.15.own_ref = bf16[4,2,128,128]{3,2,1,0:T(8,128)(2,1)S(1)} all-to-all(bf16[4,2,128,128]{3,2,1,0:T(8,128)(2,1)S(1)} %broadcast_in_dim.5), channel_id=1, replica_groups=mesh['y'=4,'x'=4,'zh'=2,'zm'=2,'zq'=4,'c'=2] {'zq'}, dimensions={0} | all-to-all | bytes 524288 | tf_op jit(solution)/shard_map/all_to_all | solution.py:23
  111.0 7.2 %collective-permute-start.1 = (bf16[4,2,128,128]{3,2,1,0:T(8,128)(2,1)S(1)}, bf16[4,2,128,128]{3,2,1,0:T(8,128)(2,1)S(1)}, u32[]{:S(2)}, u32[]{:S(2)}) collective-permute-start(bf16[4,2,128,128]{3,2,1,0:T(8,128)(2,1)S(1)} %all_to_all.15.own_ref), channel_id=1, source_target_pairs={{0,1},{1,0},{2,3},{3,2},{4,5},{5,4},{6,7},{7,6},{8,9},{9,8},{10,11... | collective-permute-start | bytes 786440 | tf_op jit(solution)/shard_map/ppermute | solution.py:29
  118.2 1.1 collective-permute-done.1.other_ref
  119.3 1.5 %shard_map.50 = f32[2,64,128]{2,1,0:T(8,128)} custom-call(s32[3]{0:T(128)S(1)} %pad_add_fusion.where_ref, bf16[4,2,128,128]{3,2,1,0:T(8,128)(2,1)S(1)} %all_to_all.15.own_ref, bf16[4,2,128,128]{3,2,1,0:T(8,128)(2,1)S(1)} %collective-permute-done.1.other_ref, bf16[16,2,128,128]{3,2,1,0:T(8,128)(2,1)S(1)} %get-tuple-element.9.y_ref, ...), custom_call_target="tpu_custom_call" | custom-call | flops 134217728 | bytes 2097152 | tf_op jit(solution)/shard_map/pallas_call | solution.py:433
  (5 shorter events, 0.1 us)
Async XLA Ops:
  21.0 41.2 %all-to-all-start = ((bf16[16,2,272,128]{3,2,1,0:T(8,128)(2,1)}), bf16[16,2,272,128]{3,2,1,0:T(8,128)(2,1)S(1)}, u32[]{:S(2)}, u32[]{:S(2)}) async-start(bf16[16,2,272,128]{3,2,1,0:T(8,128)(2,1)} %broadcast_in_dim.4), calls=%async_computation | async-start | bytes 4456448 | tf_op jit(solution)/shard_map/all_to_all | solution.py:23
  55.5 6.7 %collective-permute-start = (bf16[4,2,2,128,128]{4,3,2,1,0:T(8,128)(2,1)S(1)}, bf16[4,2,2,128,128]{4,3,2,1,0:T(8,128)(2,1)S(1)}, u32[]{:S(2)}, u32[]{:S(2)}) collective-permute-start(bf16[4,2,2,128,128]{4,3,2,1,0:T(8,128)(2,1)S(1)} %bitcast.16), channel_id=1, source_target_pairs={{0,1},{1,0},{2,3},{3,2},{4,5},{5,4},{6,7},{7,6},{8,9},{9,8},{10,11... | collective-permute-start | bytes 1572872 | tf_op jit(solution)/shard_map/ppermute | solution.py:29
  64.2 22.7 %all-to-all-start.1 = ((bf16[16,2,128,128]{3,2,1,0:T(8,128)(2,1)}), bf16[16,2,128,128]{3,2,1,0:T(8,128)(2,1)S(1)}, u32[]{:S(2)}, u32[]{:S(2)}) async-start(bf16[16,2,128,128]{3,2,1,0:T(8,128)(2,1)} %shard_map.47), calls=%async_computation.1 | async-start | bytes 2097152 | tf_op jit(solution)/shard_map/all_to_all | solution.py:399
  71.4 15.5 %copy-start = (f32[32]{0:T(128)S(1)}, f32[32]{0:T(128)}, u32[]{:S(2)}) copy-start(f32[32]{0:T(128)} %param.7) | copy-start | bytes 388
  111.0 8.3 %collective-permute-start.1 = (bf16[4,2,128,128]{3,2,1,0:T(8,128)(2,1)S(1)}, bf16[4,2,128,128]{3,2,1,0:T(8,128)(2,1)S(1)}, u32[]{:S(2)}, u32[]{:S(2)}) collective-permute-start(bf16[4,2,128,128]{3,2,1,0:T(8,128)(2,1)S(1)} %all_to_all.15.own_ref), channel_id=1, source_target_pairs={{0,1},{1,0},{2,3},{3,2},{4,5},{5,4},{6,7},{7,6},{8,9},{9,8},{10,11... | collective-permute-start | bytes 786440 | tf_op jit(solution)/shard_map/ppermute | solution.py:29

commit v6 on v5

--- a/solution.py
+++ b/solution.py
@@ -72,6 +72,22 @@
     out_ref[272:336], out_ref[336:400] = real.astype(bf16), imag.astype(bf16)
 
 
+def compose(window_ref, damp_ref, coupling_ref, out_ref):
+    fields = [[window_ref[which, part] for part in range(2)] for which in range(2)]
+    for which in range(2):
+        for part in range(2):
+            start = 128 * which + 64 * part
+            out_ref[start : start + 64] = fields[which][part].astype(bf16)
+    damp = damp_ref[...]
+    high = damp.astype(bf16).astype(f32)
+    mid = (damp - high).astype(bf16).astype(f32)
+    low = damp - high - mid
+    rows = jnp.concatenate([high, mid, low, jnp.zeros_like(low)], axis=1)
+    out_ref[256:272] = jnp.concatenate([rows, jnp.zeros((14, 128), f32)], axis=0).astype(bf16)
+    real, imag = spectral(*fields[0], *fields[1], couplings(coupling_ref[...], 2))
+    out_ref[272:336], out_ref[336:400] = real.astype(bf16), imag.astype(bf16)
+
+
 def row_times_column(pieces, y_ref, acc_ref):
     for n, (left, blocks) in enumerate(pieces):
         right = [
@@ -88,34 +104,42 @@
             acc_ref[...] += part
 
 
-def first_collision(scale, where_ref, own_ref, other_ref, y_ref, out_ref, acc_ref):
-    core = where_ref[2]
-    pieces = [
-        (
-            [s_ref[q, m].reshape(256, 128) for m in range(2)],
-            [8 * m + 2 * q + side for m in range(2)],
-        )
-        for s_ref, side in ((own_ref, core), (other_ref, 1 - core))
-        for q in range(4)
-    ]
-    row_times_column(pieces, y_ref, acc_ref)
+def half_product(side, s_ref, y_ref, acc_ref):
+    for q in range(4):
+        left = jnp.concatenate([s_ref[q, m].reshape(-1, 128) for m in range(2)], axis=1)
+        right = []
+        for m in range(2):
+            j = 8 * m + 2 * q + side
+            right.append(
+                jnp.concatenate(
+                    [y_ref[j, :, 0:64].reshape(128, 128), y_ref[j, :, 64:128].reshape(128, 128)],
+                    axis=1,
+                )
+            )
+        part = dot(left, jnp.concatenate(right, axis=0))
+        if q == 0:
+            acc_ref[...] = part
+        else:
+            acc_ref[...] += part
+
+
+def own_half(where_ref, s_ref, y_ref, acc_ref):
+    half_product(where_ref[2], s_ref, y_ref, acc_ref)
+
+
+def first_collision(scale, where_ref, s_ref, y_ref, own_ref, out_ref, acc_ref):
+    half_product(1 - where_ref[2], s_ref, y_ref, acc_ref)
+    acc_ref[...] += own_ref[...]
     for h in range(2):
         top, low = acc_ref[h * 128 : h * 128 + 64], acc_ref[h * 128 + 64 : h * 128 + 128]
         real = (scale * (top[:, :128] - low[:, 128:])).astype(bf16)
         imag = (scale * (top[:, 128:] + low[:, :128])).astype(bf16)
-        for peer in range(16):
-            out_ref[peer, h, 0:64] = real
-            out_ref[peer, h, 64:128] = imag
-
-
-def last_collision(scale, where_ref, own_ref, other_ref, y_ref, base_ref, out_ref, acc_ref):
-    core = where_ref[2]
-    pieces = [
-        ([s_ref[q, m] for m in range(2)], [8 * m + 2 * q + side for m in range(2)])
-        for s_ref, side in ((own_ref, core), (other_ref, 1 - core))
-        for q in range(4)
-    ]
-    row_times_column(pieces, y_ref, acc_ref)
+        out_ref[h, 0:64], out_ref[h, 64:128] = real, imag
+
+
+def last_collision(scale, where_ref, s_ref, y_ref, own_ref, base_ref, out_ref, acc_ref):
+    half_product(1 - where_ref[2], s_ref, y_ref, acc_ref)
+    acc_ref[...] += own_ref[...]
     top, low = acc_ref[0:64], acc_ref[64:128]
     out_ref[0] = base_ref[0:64] + (0.5 * scale) * (top[:, :128] - low[:, 128:])
     out_ref[1] = base_ref[64:128] + (0.5 * scale) * (top[:, 128:] + low[:, :128])
@@ -158,8 +182,8 @@
         pltpu.make_async_copy(p_ref.at[k], out_hbm.at[k, 0:512, 0:640], sems.at[k])
         for k in range(8)
     ]
-    copies.append(pltpu.make_async_copy(last_ref, out_hbm.at[:, 512:576, 0:512], sems.at[8]))
-    copies.append(pltpu.make_async_copy(pc_ref, out_hbm.at[:, 576:640, 0:896], sems.at[9]))
+    copies.append(pltpu.make_async_copy(last_ref, out_hbm.at[:, 512:640, 0:256], sems.at[8]))
+    copies.append(pltpu.make_async_copy(pc_ref, out_hbm.at[:, 640:704, 0:896], sems.at[9]))
     left = halves(embedded(u_ref[...]))
 
     def store(k, i, z):
@@ -173,8 +197,8 @@
             p_ref[k, to, 256:512] = low[rows]
             p_ref[k, to, 512:608] = first[rows]
             if i == 7:
-                last_ref[k, rows, 0:256] = high[rows]
-                last_ref[k, rows, 256:512] = low[rows]
+                last_ref[k, rows] = high[rows]
+                last_ref[k, 64 + 32 * part : 96 + 32 * part] = low[rows]
 
     for k in range(8):
         start = jnp.concatenate([u_ref[...], jnp.zeros((64, 224), f32)], axis=1)
@@ -218,8 +242,8 @@
     p_ref, last_ref, pc_ref, f_ref, s_ref, ends_ref, carry_ref, hom_ref, x_ref, sems,
 ):
     copies = [
-        pltpu.make_async_copy(plan_hbm.at[:, 512:576, 0:512], last_ref, sems.at[8]),
-        pltpu.make_async_copy(plan_hbm.at[:, 576:640, 0:896], pc_ref, sems.at[9]),
+        pltpu.make_async_copy(plan_hbm.at[:, 512:640, 0:256], last_ref, sems.at[8]),
+        pltpu.make_async_copy(plan_hbm.at[:, 640:704, 0:896], pc_ref, sems.at[9]),
     ]
 
     def fetch(k):
@@ -258,7 +282,8 @@
         return jnp.concatenate([x, x], axis=0)
 
     def put_end(k, source):
-        real, imag = parts(dot(last_ref[k], twice(source)))
+        product = dot(last_ref[k], source)
+        real, imag = parts(product[:64] + product[64:])
         high, low = halves(jnp.concatenate([real, imag], axis=1))
         ends_ref[0, k], ends_ref[1, k], ends_ref[2, k] = high, low, high
 
@@ -336,7 +361,7 @@
 
 PRED_SCRATCH = [
     pltpu.VMEM((8, 512, 640), bf16),
-    pltpu.VMEM((8, 64, 512), bf16),
+    pltpu.VMEM((8, 128, 256), bf16),
     pltpu.VMEM((8, 64, 896), bf16),
     pltpu.VMEM((8, 256, 256), bf16),
     pltpu.VMEM((8, 256, 256), bf16),
@@ -346,7 +371,6 @@
     pltpu.VMEM((32, 128, 128), f32),
     pltpu.SemaphoreType.DMA((10,)),
 ]
-FIRST_SCRATCH = [pltpu.VMEM((256, 256), f32)]
 
 
 def call(kernel, outs, scratch, ins, flops, moved, grant=24, place=VMEM):
@@ -388,25 +412,33 @@
     s_rows = lax.all_gather(s_rows, "zq")
     s_other = swapped(s_rows, "c")
 
+    own = call(
+        own_half,
+        shape(256, 256, kind=f32),
+        [],
+        [SMEM, VMEM, VMEM],
+        256 * 256 * 2048,
+        2 << 20,
+    )(where, s_rows, lg)
     c1 = call(
         functools.partial(first_collision, scale),
-        shape(16, 2, 128, 128),
-        FIRST_SCRATCH,
+        shape(2, 128, 128),
+        [pltpu.VMEM((256, 256), f32)],
         [SMEM, VMEM, VMEM, VMEM],
-        2 * 256 * 256 * 2048,
-        4 << 20,
-    )(where, s_rows, s_other, lg)
-    force = lax.all_to_all(c1, PLANE, 0, 0, tiled=True)
+        256 * 256 * 2048,
+        3 << 20,
+    )(where, s_other, lg, own)
+    force = from_everyone(c1, PLANE)
 
     parts = lg[:, :, 256:258].reshape(64, 128).astype(f32)
     damp = parts[:, 0:32] + (parts[:, 32:64] + parts[:, 64:96])
     damp = jnp.tile(damp.T, (2, 1))
     plan = call(
         build_steps,
-        shape(8, 640, 1024),
+        shape(8, 704, 1024),
         [
             pltpu.VMEM((8, 512, 640), bf16),
-            pltpu.VMEM((8, 64, 512), bf16),
+            pltpu.VMEM((8, 128, 256), bf16),
             pltpu.VMEM((8, 64, 896), bf16),
             pltpu.VMEM((8, 64, 256), f32),
             pltpu.SemaphoreType.DMA((10,)),
@@ -430,14 +462,22 @@
 
     t_rows = from_everyone(lax.all_gather(t2, "zm"), "zq")
     t_other = swapped(t_rows, "c")
+    own = call(
+        own_half,
+        shape(128, 256, kind=f32),
+        [],
+        [SMEM, VMEM, VMEM],
+        128 * 256 * 2048,
+        1 << 20,
+    )(where, t_rows, y2)
     out = call(
         functools.partial(last_collision, scale),
         shape(2, 64, 128, kind=f32),
         [pltpu.VMEM((128, 256), f32)],
         [SMEM, VMEM, VMEM, VMEM, VMEM],
-        2 * 128 * 256 * 2048,
-        2 << 20,
-    )(where, t_rows, t_other, y2, base)
+        128 * 256 * 2048,
+        1 << 20,
+    )(where, t_other, y2, own, base)
     return out.reshape(2, 2, orbitals, 128)
 
 

time: 121 us -> 122 us (level)
  waiting for transfers between devices: 9.53 us -> 7.97 us
  local copies, waits for them, and re-layouts: 2.43 us -> 3.66 us
    all_to_all x1 -> x2, waiting for transfers between devices: 0.01 us -> 7.06 us  [from_everyone(): lax.all_to_all(jnp.broadcast_to(shard[None], (peers, *shard.shape)), axis...]
    all_to_all x1 -> x0, waiting for transfers between devices: 6.95 us -> none  [shards(): force = lax.all_to_all(c1, PLANE, 0, 0, tiled=True)]
    all_to_all x1 -> x0, starting transfers between devices: 6.33 us -> none  [shards(): force = lax.all_to_all(c1, PLANE, 0, 0, tiled=True)]
    all_to_all x1 -> x2, starting transfers between devices: 7 us -> 13.3 us  [from_everyone(): lax.all_to_all(jnp.broadcast_to(shard[None], (peers, *shard.shape)), axis...]
    ppermute x2, waiting for transfers between devices: 2.57 us -> 0.91 us  [swapped(): return lax.ppermute(shard, axis, [(0, 1), (1, 0)])]
    broadcast_in_dim x2 -> x3, local copies, waits for them, and re-layouts: 1.7 us -> 2.93 us  [from_everyone(): jnp.broadcast_to(shard[None], (peers, *shard.shape))]
    pallas_call x2 -> x4, Pallas kernels: 10.6 us -> 10.9 us  [the longest x1 8.46 us: shards(): call(build_steps, shape(8, 704, 1024), [pltpu.VMEM((8, 512, 640), bf16),...]
  transfers between devices with their start and end apart: 4 -> 4, of which waited for: 3 -> 3; matrix products, arithmetic and copies ran while one was open for 1% -> 1% of each run, Pallas kernels for 7% -> 8%
where the time goes in v6:
time: 122 us; the launch traced here: 121 us
  blocking collectives  62.9 us (52%)
  starting transfers between devices  25.7 us (21%)
  Pallas kernels  20.8 us (17%)
  waiting for transfers between devices  7.97 us (7%)
  local copies, waits for them, and re-layouts  3.66 us (3%)
    all_gather x1, blocking collectives, shards(): pair = lax.all_gather(message, 'zh')  17.6 us
    all_gather x1, blocking collectives, shards(): s_rows = lax.all_gather(s_rows, 'zq')  15.5 us
    all_to_all x2, starting transfers between devices, from_everyone(): lax.all_to_all(jnp.broadcast_to(shard[None], (peers, *shard.shape)), axis...  13.3 us
    ppermute x2, starting transfers between devices, swapped(): return lax.ppermute(shard, axis, [(0, 1), (1, 0)])  12.4 us
    all_gather x1, blocking collectives, shards(): s_rows = lax.all_gather(pair[:, 272:], 'zm')  12 us
    all_to_all x1, blocking collectives, from_everyone(): lax.all_to_all(jnp.broadcast_to(shard[None], (peers, *shard.shape)), axis...  9.75 us
    pallas_call x1, Pallas kernels, shards(): call(build_steps, shape(8, 704, 1024), [pltpu.VMEM((8, 512, 640), bf16),...  8.46 us
    all_gather x1, blocking collectives, shards(): t_rows = from_everyone(lax.all_gather(t2, 'zm'), 'zq')  8.09 us
  transfers between devices with their start and end apart: 4, of which 3 were waited for; matrix products, arithmetic and copies ran while one was open for 1% of the time, Pallas kernels for 8%

profile of v6, /device:TPU:1, one launch (start us, length us, event | category | flops | bytes accessed | tf_op | source)
XLA Modules:
  0.0 121.3 jit_solution(12947936521217936665)
XLA Ops:
  0.0 1.7 %shard_map.46 = bf16[400,128]{1,0:T(8,128)(2,1)} custom-call(f32[2,2,64,128]{3,2,1,0:T(8,128)} %bitcast.25, f32[2,32]{1,0:T(2,128)} %damp_ref.1, f32[1,32]{1,0:T(1,128)} %bitcast.18), custom_call_target="tpu_custom_call" | custom-call | flops 327680 | bytes 409600 | tf_op jit(solution)/shard_map/pallas_call | solution.py:399
  1.7 17.6 %all-gather = bf16[800,128]{1,0:T(8,128)(2,1)S(1)} all-gather(bf16[400,128]{1,0:T(8,128)(2,1)} %shard_map.46), channel_id=2, replica_groups=mesh['y'=4,'x'=4,'zh'=2,'zm'=2,'zq'=4,'c'=2] {'zh'}, dimensions={0}, use_global_device_ids=true | all-gather | bytes 307200 | tf_op jit(solution)/shard_map/all_gather | solution.py:408
  19.4 1.7 %broadcast_in_dim.6 = bf16[16,2,272,128]{3,2,1,0:T(8,128)(2,1)} broadcast(bf16[2,272,128]{2,1,0:T(8,128)(2,1)S(1)} %slice.25), dimensions={1,2,3} | broadcast | bytes 2367488 | tf_op jit(solution)/shard_map/broadcast_in_dim | solution.py:24
  21.0 7.0 %all-to-all-start = ((bf16[16,2,272,128]{3,2,1,0:T(8,128)(2,1)}), bf16[16,2,272,128]{3,2,1,0:T(8,128)(2,1)S(1)}, u32[]{:S(2)}, u32[]{:S(2)}) async-start(bf16[16,2,272,128]{3,2,1,0:T(8,128)(2,1)} %broadcast_in_dim.6), calls=%async_computation | async-start | bytes 4456448 | tf_op jit(solution)/shard_map/all_to_all | solution.py:23
  28.0 12.0 %all-gather.1 = bf16[4,128,128]{2,1,0:T(8,128)(2,1)S(1)} all-gather(bf16[2,128,128]{2,1,0:T(8,128)(2,1)S(1)} %slice.24), channel_id=3, replica_groups=mesh['y'=4,'x'=4,'zh'=2,'zm'=2,'zq'=4,'c'=2] {'zm'}, dimensions={0}, use_global_device_ids=true | all-gather | bytes 196608 | tf_op jit(solution)/shard_map/all_gather | solution.py:411
  40.0 15.5 %all-gather.2 = bf16[8,2,128,128]{3,2,1,0:T(8,128)(2,1)S(1)} all-gather(bf16[2,2,128,128]{3,2,1,0:T(8,128)(2,1)S(1)} %bitcast.22), channel_id=4, replica_groups=mesh['y'=4,'x'=4,'zh'=2,'zm'=2,'zq'=4,'c'=2] {'zq'}, dimensions={0}, use_global_device_ids=true | all-gather | bytes 655360 | tf_op jit(solution)/shard_map/all_gather | solution.py:412
  55.5 5.2 %collective-permute-start = (bf16[4,2,2,128,128]{4,3,2,1,0:T(8,128)(2,1)S(1)}, bf16[4,2,2,128,128]{4,3,2,1,0:T(8,128)(2,1)S(1)}, u32[]{:S(2)}, u32[]{:S(2)}) collective-permute-start(bf16[4,2,2,128,128]{4,3,2,1,0:T(8,128)(2,1)S(1)} %bitcast.16), channel_id=1, source_target_pairs={{0,1},{1,0},{2,3},{3,2},{4,5},{5,4},{6,7},{7,6},{8,9},{9,8},{10,11... | collective-permute-start | bytes 1572872 | tf_op jit(solution)/shard_map/ppermute | solution.py:29
  60.7 0.1 pad_add_fusion.where_ref
  60.8 0.0 all-to-all-done.y_ref.lg_ref
  60.8 0.9 shard_map.47.own_ref
  61.6 0.6 collective-permute-done.s_ref
  62.2 0.8 shard_map.48
  63.0 1.2 %broadcast_in_dim.7 = bf16[16,2,128,128]{3,2,1,0:T(8,128)(2,1)} broadcast(bf16[2,128,128]{2,1,0:T(8,128)(2,1)S(1)} %shard_map.48), dimensions={1,2,3} | broadcast | bytes 1114112 | tf_op jit(solution)/shard_map/broadcast_in_dim | solution.py:24
  64.3 6.3 %all-to-all-start.1 = ((bf16[16,2,128,128]{3,2,1,0:T(8,128)(2,1)}), bf16[16,2,128,128]{3,2,1,0:T(8,128)(2,1)S(1)}, u32[]{:S(2)}, u32[]{:S(2)}) async-start(bf16[16,2,128,128]{3,2,1,0:T(8,128)(2,1)} %broadcast_in_dim.7), calls=%async_computation.1 | async-start | bytes 2097152 | tf_op jit(solution)/shard_map/all_to_all | solution.py:23
  70.7 0.1 fusion.1
  70.7 0.1 copy.6
  70.8 0.6 tile.4
  71.4 0.0 copy-start
  71.4 8.5 %shard_map.49.plan_hbm = bf16[8,704,1024]{2,1,0:T(8,128)(2,1)} custom-call(f32[64,64]{1,0:T(8,128)} %bitcast.24, f32[64,32]{1,0:T(8,128)} %bitcast.27), custom_call_target="tpu_custom_call" | custom-call | flops 536870912 | bytes 6291456 | tf_op jit(solution)/shard_map/pallas_call | solution.py:436
  79.9 7.1 %all-to-all-done.1.force_ref = bf16[16,2,128,128]{3,2,1,0:T(8,128)(2,1)S(1)} async-done(((bf16[16,2,128,128]{3,2,1,0:T(8,128)(2,1)}), bf16[16,2,128,128]{3,2,1,0:T(8,128)(2,1)S(1)}, u32[]{:S(2)}, u32[]{:S(2)}) %all-to-all-start.1) | async-done | bytes 1048608 | tf_op jit(solution)/shard_map/all_to_all | solution.py:23
  87.0 0.0 copy-done
  87.0 6.7 %shard_map.50 = (bf16[16,2,128,128]{3,2,1,0:T(8,128)(2,1)S(1)}, bf16[128,128]{1,0:T(8,128)(2,1)S(1)}, f32[128,128]{1,0:T(8,128)S(1)}) custom-call(s32[3]{0:T(128)S(1)} %pad_add_fusion.where_ref, bf16[16,2,128,128]{3,2,1,0:T(8,128)(2,1)S(1)} %all-to-all-done.1.force_ref, bf16[16,2,272,128]{3,2,1,0:T(8,128)(2,1)S(1)} %all-to-all-done.y_ref.lg_ref, ...), custom_call_target="tpu_custom_call" | custom-call | flops 1073741824 | bytes 10485760 | tf_op jit(solution)/shard_map/pallas_call | solution.py:453
  93.7 8.1 %all-gather.3 = bf16[256,128]{1,0:T(8,128)(2,1)S(1)} all-gather(bf16[128,128]{1,0:T(8,128)(2,1)S(1)} %get-tuple-element.8), channel_id=5, replica_groups=mesh['y'=4,'x'=4,'zh'=2,'zm'=2,'zq'=4,'c'=2] {'zm'}, dimensions={0}, use_global_device_ids=true | all-gather | bytes 98304 | tf_op jit(solution)/shard_map/all_gather | solution.py:463
  101.8 9.8 %all_to_all.15.s_ref = bf16[4,2,128,128]{3,2,1,0:T(8,128)(2,1)S(1)} all-to-all(bf16[4,2,128,128]{3,2,1,0:T(8,128)(2,1)S(1)} %broadcast_in_dim.8), channel_id=1, replica_groups=mesh['y'=4,'x'=4,'zh'=2,'zm'=2,'zq'=4,'c'=2] {'zq'}, dimensions={0} | all-to-all | bytes 524288 | tf_op jit(solution)/shard_map/all_to_all | solution.py:23
  111.5 7.2 %collective-permute-start.1 = (bf16[4,2,128,128]{3,2,1,0:T(8,128)(2,1)S(1)}, bf16[4,2,128,128]{3,2,1,0:T(8,128)(2,1)S(1)}, u32[]{:S(2)}, u32[]{:S(2)}) collective-permute-start(bf16[4,2,128,128]{3,2,1,0:T(8,128)(2,1)S(1)} %all_to_all.15.s_ref), channel_id=1, source_target_pairs={{0,1},{1,0},{2,3},{3,2},{4,5},{5,4},{6,7},{7,6},{8,9},{9,8},{10,11... | collective-permute-start | bytes 786440 | tf_op jit(solution)/shard_map/ppermute | solution.py:29
  118.8 0.8 shard_map.51.own_ref
  119.5 0.3 collective-permute-done.1.s_ref
  119.9 1.4 %shard_map.52 = f32[2,64,128]{2,1,0:T(8,128)} custom-call(s32[3]{0:T(128)S(1)} %pad_add_fusion.where_ref, bf16[4,2,128,128]{3,2,1,0:T(8,128)(2,1)S(1)} %collective-permute-done.1.s_ref, bf16[16,2,128,128]{3,2,1,0:T(8,128)(2,1)S(1)} %get-tuple-element.9.y_ref, f32[128,256]{1,0:T(8,128)S(1)} %shard_map.51.own_ref, f32[128,128]{1,0:T(8,128)S(1)} %get-tuple-element.10.base_ref), custom_call_target="tpu_custom_call" | custom-call | flops 67108864 | bytes 1048576 | tf_op jit(solution)/shard_map/pallas_call | solution.py:473
  (5 shorter events, 0.1 us)
Async XLA Ops:
  21.0 39.7 %all-to-all-start = ((bf16[16,2,272,128]{3,2,1,0:T(8,128)(2,1)}), bf16[16,2,272,128]{3,2,1,0:T(8,128)(2,1)S(1)}, u32[]{:S(2)}, u32[]{:S(2)}) async-start(bf16[16,2,272,128]{3,2,1,0:T(8,128)(2,1)} %broadcast_in_dim.6), calls=%async_computation | async-start | bytes 4456448 | tf_op jit(solution)/shard_map/all_to_all | solution.py:23
  55.5 6.7 %collective-permute-start = (bf16[4,2,2,128,128]{4,3,2,1,0:T(8,128)(2,1)S(1)}, bf16[4,2,2,128,128]{4,3,2,1,0:T(8,128)(2,1)S(1)}, u32[]{:S(2)}, u32[]{:S(2)}) collective-permute-start(bf16[4,2,2,128,128]{4,3,2,1,0:T(8,128)(2,1)S(1)} %bitcast.16), channel_id=1, source_target_pairs={{0,1},{1,0},{2,3},{3,2},{4,5},{5,4},{6,7},{7,6},{8,9},{9,8},{10,11... | collective-permute-start | bytes 1572872 | tf_op jit(solution)/shard_map/ppermute | solution.py:29
  64.3 22.7 %all-to-all-start.1 = ((bf16[16,2,128,128]{3,2,1,0:T(8,128)(2,1)}), bf16[16,2,128,128]{3,2,1,0:T(8,128)(2,1)S(1)}, u32[]{:S(2)}, u32[]{:S(2)}) async-start(bf16[16,2,128,128]{3,2,1,0:T(8,128)(2,1)} %broadcast_in_dim.7), calls=%async_computation.1 | async-start | bytes 2097152 | tf_op jit(solution)/shard_map/all_to_all | solution.py:23
  71.4 15.5 %copy-start = (f32[32]{0:T(128)S(1)}, f32[32]{0:T(128)}, u32[]{:S(2)}) copy-start(f32[32]{0:T(128)} %param.7) | copy-start | bytes 388
  111.5 8.4 %collective-permute-start.1 = (bf16[4,2,128,128]{3,2,1,0:T(8,128)(2,1)S(1)}, bf16[4,2,128,128]{3,2,1,0:T(8,128)(2,1)S(1)}, u32[]{:S(2)}, u32[]{:S(2)}) collective-permute-start(bf16[4,2,128,128]{3,2,1,0:T(8,128)(2,1)S(1)} %all_to_all.15.s_ref), channel_id=1, source_target_pairs={{0,1},{1,0},{2,3},{3,2},{4,5},{5,4},{6,7},{7,6},{8,9},{9,8},{10,11... | collective-permute-start | bytes 786440 | tf_op jit(solution)/shard_map/ppermute | solution.py:29

commit v7 on v5

--- a/solution.py
+++ b/solution.py
@@ -67,9 +67,9 @@
     mid = (damp - high).astype(bf16).astype(f32)
     low = damp - high - mid
     rows = jnp.concatenate([high, mid, low, jnp.zeros_like(low)], axis=1)
-    out_ref[256:272] = jnp.concatenate([rows, jnp.zeros((14, 128), f32)], axis=0).astype(bf16)
+    out_ref[256:264] = jnp.concatenate([rows, jnp.zeros((6, 128), f32)], axis=0).astype(bf16)
     real, imag = spectral(*fields[0], *fields[1], couplings(coupling_ref[...], 2))
-    out_ref[272:336], out_ref[336:400] = real.astype(bf16), imag.astype(bf16)
+    out_ref[264:328], out_ref[328:392] = real.astype(bf16), imag.astype(bf16)
 
 
 def row_times_column(pieces, y_ref, acc_ref):
@@ -158,8 +158,8 @@
         pltpu.make_async_copy(p_ref.at[k], out_hbm.at[k, 0:512, 0:640], sems.at[k])
         for k in range(8)
     ]
-    copies.append(pltpu.make_async_copy(last_ref, out_hbm.at[:, 512:576, 0:512], sems.at[8]))
-    copies.append(pltpu.make_async_copy(pc_ref, out_hbm.at[:, 576:640, 0:896], sems.at[9]))
+    copies.append(pltpu.make_async_copy(last_ref, out_hbm.at[:, 512:640, 0:256], sems.at[8]))
+    copies.append(pltpu.make_async_copy(pc_ref, out_hbm.at[:, 640:704, 0:896], sems.at[9]))
     left = halves(embedded(u_ref[...]))
 
     def store(k, i, z):
@@ -173,8 +173,8 @@
             p_ref[k, to, 256:512] = low[rows]
             p_ref[k, to, 512:608] = first[rows]
             if i == 7:
-                last_ref[k, rows, 0:256] = high[rows]
-                last_ref[k, rows, 256:512] = low[rows]
+                last_ref[k, rows] = high[rows]
+                last_ref[k, 64 + 32 * part : 96 + 32 * part] = low[rows]
 
     for k in range(8):
         start = jnp.concatenate([u_ref[...], jnp.zeros((64, 224), f32)], axis=1)
@@ -218,8 +218,8 @@
     p_ref, last_ref, pc_ref, f_ref, s_ref, ends_ref, carry_ref, hom_ref, x_ref, sems,
 ):
     copies = [
-        pltpu.make_async_copy(plan_hbm.at[:, 512:576, 0:512], last_ref, sems.at[8]),
-        pltpu.make_async_copy(plan_hbm.at[:, 576:640, 0:896], pc_ref, sems.at[9]),
+        pltpu.make_async_copy(plan_hbm.at[:, 512:640, 0:256], last_ref, sems.at[8]),
+        pltpu.make_async_copy(plan_hbm.at[:, 640:704, 0:896], pc_ref, sems.at[9]),
     ]
 
     def fetch(k):
@@ -258,7 +258,8 @@
         return jnp.concatenate([x, x], axis=0)
 
     def put_end(k, source):
-        real, imag = parts(dot(last_ref[k], twice(source)))
+        product = dot(last_ref[k], source)
+        real, imag = parts(product[:64] + product[64:])
         high, low = halves(jnp.concatenate([real, imag], axis=1))
         ends_ref[0, k], ends_ref[1, k], ends_ref[2, k] = high, low, high
 
@@ -291,10 +292,20 @@
     def piece(k, u):
         n, row = 4 * k + u, u * 64
 
+        width = 128 if u < 2 else 256
         rows = jnp.concatenate(
-            [p_ref[k, pl.ds(row, 64), 0:608], p_ref[k, pl.ds(row + 256, 64), 0:608]], axis=0
+            [
+                jnp.concatenate(
+                    [p_ref[k, at : at + 64, lane : lane + width] for lane in (0, 256)]
+                    + [p_ref[k, at : at + 64, 512:608]],
+                    axis=1,
+                )
+                for at in (row, row + 256)
+            ],
+            axis=0,
         )
-        source = jnp.concatenate([f_ref[k], f_ref[k], carry_ref[k]], axis=0)
+        force = f_ref[k, 0:width]
+        source = jnp.concatenate([force, force, carry_ref[k]], axis=0)
         real, imag = parts(dot(rows, source))
         j_at, h_at = 2 * k + u // 2, u % 2
         g = lg_ref[j_at, h_at, 128:256].astype(f32)
@@ -336,7 +347,7 @@
 
 PRED_SCRATCH = [
     pltpu.VMEM((8, 512, 640), bf16),
-    pltpu.VMEM((8, 64, 512), bf16),
+    pltpu.VMEM((8, 128, 256), bf16),
     pltpu.VMEM((8, 64, 896), bf16),
     pltpu.VMEM((8, 256, 256), bf16),
     pltpu.VMEM((8, 256, 256), bf16),
@@ -346,7 +357,6 @@
     pltpu.VMEM((32, 128, 128), f32),
     pltpu.SemaphoreType.DMA((10,)),
 ]
-FIRST_SCRATCH = [pltpu.VMEM((256, 256), f32)]
 
 
 def call(kernel, outs, scratch, ins, flops, moved, grant=24, place=VMEM):
@@ -374,7 +384,7 @@
     strength = coupling.reshape(1, 32)
     message = call(
         compose,
-        shape(400, 128),
+        shape(392, 128),
         [],
         [VMEM, VMEM, VMEM],
         40 * 64 * 128,
@@ -382,16 +392,16 @@
         63.9,
     )(window.reshape(2, 2, 64, 128), damping, strength)
     pair = lax.all_gather(message, "zh")
-    lg = from_everyone(pair[:, :272], PLANE)
-
-    s_rows = lax.all_gather(pair[:, 272:], "zm")
+    lg = from_everyone(pair[:, :264], PLANE)
+
+    s_rows = lax.all_gather(pair[:, 264:], "zm")
     s_rows = lax.all_gather(s_rows, "zq")
     s_other = swapped(s_rows, "c")
 
     c1 = call(
         functools.partial(first_collision, scale),
         shape(16, 2, 128, 128),
-        FIRST_SCRATCH,
+        [pltpu.VMEM((256, 256), f32)],
         [SMEM, VMEM, VMEM, VMEM],
         2 * 256 * 256 * 2048,
         4 << 20,
@@ -403,10 +413,10 @@
     damp = jnp.tile(damp.T, (2, 1))
     plan = call(
         build_steps,
-        shape(8, 640, 1024),
+        shape(8, 704, 1024),
         [
             pltpu.VMEM((8, 512, 640), bf16),
-            pltpu.VMEM((8, 64, 512), bf16),
+            pltpu.VMEM((8, 128, 256), bf16),
             pltpu.VMEM((8, 64, 896), bf16),
             pltpu.VMEM((8, 64, 256), f32),
             pltpu.SemaphoreType.DMA((10,)),

time: 121 us -> 120 us (level)
  no operation moved by 1% of the time
where the time goes in v7:
time: 120 us; the launch traced here: 119 us
  blocking collectives  61.3 us (51%)
  starting transfers between devices  25.3 us (21%)
  Pallas kernels  20.2 us (17%)
  waiting for transfers between devices  9.64 us (8%)
  local copies, waits for them, and re-layouts  2.39 us (2%)
    all_gather x1, blocking collectives, shards(): pair = lax.all_gather(message, 'zh')  17.6 us
    all_gather x1, blocking collectives, shards(): s_rows = lax.all_gather(s_rows, 'zq')  16.2 us
    ppermute x2, starting transfers between devices, swapped(): return lax.ppermute(shard, axis, [(0, 1), (1, 0)])  11.9 us
    all_gather x1, blocking collectives, shards(): s_rows = lax.all_gather(pair[:, 264:], 'zm')  11.1 us
    pallas_call x1, Pallas kernels, shards(): call(build_steps, shape(8, 704, 1024), [pltpu.VMEM((8, 512, 640), bf16),...  8.46 us
    all_to_all x1, blocking collectives, from_everyone(): lax.all_to_all(jnp.broadcast_to(shard[None], (peers, *shard.shape)), axis...  8.36 us
    all_gather x1, blocking collectives, shards(): t_rows = from_everyone(lax.all_gather(t2, 'zm'), 'zq')  8.04 us
    all_to_all x1, waiting for transfers between devices, shards(): force = lax.all_to_all(c1, PLANE, 0, 0, tiled=True)  7.06 us
  transfers between devices with their start and end apart: 4, of which 3 were waited for; matrix products, arithmetic and copies ran while one was open for 1% of the time, Pallas kernels for 7%

profile of v7, /device:TPU:1, one launch (start us, length us, event | category | flops | bytes accessed | tf_op | source)
XLA Modules:
  0.0 119.1 jit_solution(7890427303275559151)
XLA Ops:
  0.0 1.7 %shard_map.46 = bf16[392,128]{1,0:T(8,128)(2,1)} custom-call(f32[2,2,64,128]{3,2,1,0:T(8,128)} %bitcast.25, f32[2,32]{1,0:T(2,128)} %damp_ref.1, f32[1,32]{1,0:T(1,128)} %bitcast.18), custom_call_target="tpu_custom_call" | custom-call | flops 327680 | bytes 409600 | tf_op jit(solution)/shard_map/pallas_call | solution.py:385
  1.7 17.6 %all-gather = bf16[784,128]{1,0:T(8,128)(2,1)S(1)} all-gather(bf16[392,128]{1,0:T(8,128)(2,1)} %shard_map.46), channel_id=2, replica_groups=mesh['y'=4,'x'=4,'zh'=2,'zm'=2,'zq'=4,'c'=2] {'zh'}, dimensions={0}, use_global_device_ids=true | all-gather | bytes 301056 | tf_op jit(solution)/shard_map/all_gather | solution.py:394
  19.3 1.6 %broadcast_in_dim.4 = bf16[16,2,264,128]{3,2,1,0:T(8,128)(2,1)} broadcast(bf16[2,264,128]{2,1,0:T(8,128)(2,1)S(1)} %slice.25), dimensions={1,2,3} | broadcast | bytes 2297856 | tf_op jit(solution)/shard_map/broadcast_in_dim | solution.py:24
  21.0 7.0 %all-to-all-start = ((bf16[16,2,264,128]{3,2,1,0:T(8,128)(2,1)}), bf16[16,2,264,128]{3,2,1,0:T(8,128)(2,1)S(1)}, u32[]{:S(2)}, u32[]{:S(2)}) async-start(bf16[16,2,264,128]{3,2,1,0:T(8,128)(2,1)} %broadcast_in_dim.4), calls=%async_computation | async-start | bytes 4325376 | tf_op jit(solution)/shard_map/all_to_all | solution.py:23
  28.0 11.1 %all-gather.1 = bf16[4,128,128]{2,1,0:T(8,128)(2,1)S(1)} all-gather(bf16[2,128,128]{2,1,0:T(8,128)(2,1)S(1)} %slice.24), channel_id=3, replica_groups=mesh['y'=4,'x'=4,'zh'=2,'zm'=2,'zq'=4,'c'=2] {'zm'}, dimensions={0}, use_global_device_ids=true | all-gather | bytes 196608 | tf_op jit(solution)/shard_map/all_gather | solution.py:397
  39.1 16.2 %all-gather.2 = bf16[8,2,128,128]{3,2,1,0:T(8,128)(2,1)S(1)} all-gather(bf16[2,2,128,128]{3,2,1,0:T(8,128)(2,1)S(1)} %bitcast.22), channel_id=4, replica_groups=mesh['y'=4,'x'=4,'zh'=2,'zm'=2,'zq'=4,'c'=2] {'zq'}, dimensions={0}, use_global_device_ids=true | all-gather | bytes 655360 | tf_op jit(solution)/shard_map/all_gather | solution.py:398
  55.3 5.2 %collective-permute-start = (bf16[4,2,2,128,128]{4,3,2,1,0:T(8,128)(2,1)S(1)}, bf16[4,2,2,128,128]{4,3,2,1,0:T(8,128)(2,1)S(1)}, u32[]{:S(2)}, u32[]{:S(2)}) collective-permute-start(bf16[4,2,2,128,128]{4,3,2,1,0:T(8,128)(2,1)S(1)} %bitcast.16), channel_id=1, source_target_pairs={{0,1},{1,0},{2,3},{3,2},{4,5},{5,4},{6,7},{7,6},{8,9},{9,8},{10,11... | collective-permute-start | bytes 1572872 | tf_op jit(solution)/shard_map/ppermute | solution.py:29
  60.5 0.1 pad_add_fusion.where_ref
  60.6 1.4 %collective-permute-done.other_ref = bf16[4,2,2,128,128]{4,3,2,1,0:T(8,128)(2,1)S(1)} collective-permute-done((bf16[4,2,2,128,128]{4,3,2,1,0:T(8,128)(2,1)S(1)}, bf16[4,2,2,128,128]{4,3,2,1,0:T(8,128)(2,1)S(1)}, u32[]{:S(2)}, u32[]{:S(2)}) %collective-permute-start) | collective-permute-done | bytes 524320 | tf_op jit(solution)/shard_map/ppermute | solution.py:29
  62.0 0.0 all-to-all-done.y_ref.lg_ref
  62.0 2.1 %shard_map.47 = bf16[16,2,128,128]{3,2,1,0:T(8,128)(2,1)} custom-call(s32[3]{0:T(128)S(1)} %pad_add_fusion.where_ref, bf16[4,2,2,128,128]{4,3,2,1,0:T(8,128)(2,1)S(1)} %bitcast.17, bf16[4,2,2,128,128]{4,3,2,1,0:T(8,128)(2,1)S(1)} %collective-permute-done.other_ref, bf16[16,2,264,128]{3,2,1,0:T(8,128)(2,1)S(1)} %all-to-all-done.y_ref.lg_ref), custom_call_target="tpu_custom_call" | custom-call | flops 268435456 | bytes 4194304 | tf_op jit(solution)/shard_map/pallas_call | solution.py:401
  64.1 6.4 %all-to-all-start.1 = ((bf16[16,2,128,128]{3,2,1,0:T(8,128)(2,1)}), bf16[16,2,128,128]{3,2,1,0:T(8,128)(2,1)S(1)}, u32[]{:S(2)}, u32[]{:S(2)}) async-start(bf16[16,2,128,128]{3,2,1,0:T(8,128)(2,1)} %shard_map.47), calls=%async_computation.1 | async-start | bytes 2097152 | tf_op jit(solution)/shard_map/all_to_all | solution.py:409
  70.5 0.1 fusion.1
  70.6 0.1 copy.6
  70.6 0.6 tile.4
  71.3 0.0 copy-start
  71.3 8.5 %shard_map.48.plan_hbm = bf16[8,704,1024]{2,1,0:T(8,128)(2,1)} custom-call(f32[64,64]{1,0:T(8,128)} %bitcast.24, f32[64,32]{1,0:T(8,128)} %bitcast.27), custom_call_target="tpu_custom_call" | custom-call | flops 536870912 | bytes 6291456 | tf_op jit(solution)/shard_map/pallas_call | solution.py:414
  79.7 7.1 %all-to-all-done.1.force_ref = bf16[16,2,128,128]{3,2,1,0:T(8,128)(2,1)S(1)} async-done(((bf16[16,2,128,128]{3,2,1,0:T(8,128)(2,1)}), bf16[16,2,128,128]{3,2,1,0:T(8,128)(2,1)S(1)}, u32[]{:S(2)}, u32[]{:S(2)}) %all-to-all-start.1) | async-done | bytes 1048608 | tf_op jit(solution)/shard_map/all_to_all | solution.py:409
  86.8 0.0 copy-done
  86.8 6.4 %shard_map.49 = (bf16[16,2,128,128]{3,2,1,0:T(8,128)(2,1)S(1)}, bf16[128,128]{1,0:T(8,128)(2,1)S(1)}, f32[128,128]{1,0:T(8,128)S(1)}) custom-call(s32[3]{0:T(128)S(1)} %pad_add_fusion.where_ref, bf16[16,2,128,128]{3,2,1,0:T(8,128)(2,1)S(1)} %all-to-all-done.1.force_ref, bf16[16,2,264,128]{3,2,1,0:T(8,128)(2,1)S(1)} %all-to-all-done.y_ref.lg_ref, ...), custom_call_target="tpu_custom_call" | custom-call | flops 1073741824 | bytes 10485760 | tf_op jit(solution)/shard_map/pallas_call | solution.py:431
  93.2 8.0 %all-gather.3 = bf16[256,128]{1,0:T(8,128)(2,1)S(1)} all-gather(bf16[128,128]{1,0:T(8,128)(2,1)S(1)} %get-tuple-element.8), channel_id=5, replica_groups=mesh['y'=4,'x'=4,'zh'=2,'zm'=2,'zq'=4,'c'=2] {'zm'}, dimensions={0}, use_global_device_ids=true | all-gather | bytes 98304 | tf_op jit(solution)/shard_map/all_gather | solution.py:441
  101.3 8.4 %all_to_all.15.own_ref = bf16[4,2,128,128]{3,2,1,0:T(8,128)(2,1)S(1)} all-to-all(bf16[4,2,128,128]{3,2,1,0:T(8,128)(2,1)S(1)} %broadcast_in_dim.5), channel_id=1, replica_groups=mesh['y'=4,'x'=4,'zh'=2,'zm'=2,'zq'=4,'c'=2] {'zq'}, dimensions={0} | all-to-all | bytes 524288 | tf_op jit(solution)/shard_map/all_to_all | solution.py:23
  109.7 6.7 %collective-permute-start.1 = (bf16[4,2,128,128]{3,2,1,0:T(8,128)(2,1)S(1)}, bf16[4,2,128,128]{3,2,1,0:T(8,128)(2,1)S(1)}, u32[]{:S(2)}, u32[]{:S(2)}) collective-permute-start(bf16[4,2,128,128]{3,2,1,0:T(8,128)(2,1)S(1)} %all_to_all.15.own_ref), channel_id=1, source_target_pairs={{0,1},{1,0},{2,3},{3,2},{4,5},{5,4},{6,7},{7,6},{8,9},{9,8},{10,11... | collective-permute-start | bytes 786440 | tf_op jit(solution)/shard_map/ppermute | solution.py:29
  116.4 1.1 collective-permute-done.1.other_ref
  117.6 1.5 %shard_map.50 = f32[2,64,128]{2,1,0:T(8,128)} custom-call(s32[3]{0:T(128)S(1)} %pad_add_fusion.where_ref, bf16[4,2,128,128]{3,2,1,0:T(8,128)(2,1)S(1)} %all_to_all.15.own_ref, bf16[4,2,128,128]{3,2,1,0:T(8,128)(2,1)S(1)} %collective-permute-done.1.other_ref, bf16[16,2,128,128]{3,2,1,0:T(8,128)(2,1)S(1)} %get-tuple-element.9.y_ref, ...), custom_call_target="tpu_custom_call" | custom-call | flops 134217728 | bytes 2097152 | tf_op jit(solution)/shard_map/pallas_call | solution.py:443
  (5 shorter events, 0.1 us)
Async XLA Ops:
  21.0 41.0 %all-to-all-start = ((bf16[16,2,264,128]{3,2,1,0:T(8,128)(2,1)}), bf16[16,2,264,128]{3,2,1,0:T(8,128)(2,1)S(1)}, u32[]{:S(2)}, u32[]{:S(2)}) async-start(bf16[16,2,264,128]{3,2,1,0:T(8,128)(2,1)} %broadcast_in_dim.4), calls=%async_computation | async-start | bytes 4325376 | tf_op jit(solution)/shard_map/all_to_all | solution.py:23
  55.3 6.7 %collective-permute-start = (bf16[4,2,2,128,128]{4,3,2,1,0:T(8,128)(2,1)S(1)}, bf16[4,2,2,128,128]{4,3,2,1,0:T(8,128)(2,1)S(1)}, u32[]{:S(2)}, u32[]{:S(2)}) collective-permute-start(bf16[4,2,2,128,128]{4,3,2,1,0:T(8,128)(2,1)S(1)} %bitcast.16), channel_id=1, source_target_pairs={{0,1},{1,0},{2,3},{3,2},{4,5},{5,4},{6,7},{7,6},{8,9},{9,8},{10,11... | collective-permute-start | bytes 1572872 | tf_op jit(solution)/shard_map/ppermute | solution.py:29
  64.1 22.7 %all-to-all-start.1 = ((bf16[16,2,128,128]{3,2,1,0:T(8,128)(2,1)}), bf16[16,2,128,128]{3,2,1,0:T(8,128)(2,1)S(1)}, u32[]{:S(2)}, u32[]{:S(2)}) async-start(bf16[16,2,128,128]{3,2,1,0:T(8,128)(2,1)} %shard_map.47), calls=%async_computation.1 | async-start | bytes 2097152 | tf_op jit(solution)/shard_map/all_to_all | solution.py:409
  71.3 15.5 %copy-start = (f32[32]{0:T(128)S(1)}, f32[32]{0:T(128)}, u32[]{:S(2)}) copy-start(f32[32]{0:T(128)} %param.7) | copy-start | bytes 388
  109.7 7.9 %collective-permute-start.1 = (bf16[4,2,128,128]{3,2,1,0:T(8,128)(2,1)S(1)}, bf16[4,2,128,128]{3,2,1,0:T(8,128)(2,1)S(1)}, u32[]{:S(2)}, u32[]{:S(2)}) collective-permute-start(bf16[4,2,128,128]{3,2,1,0:T(8,128)(2,1)S(1)} %all_to_all.15.own_ref), channel_id=1, source_target_pairs={{0,1},{1,0},{2,3},{3,2},{4,5},{5,4},{6,7},{7,6},{8,9},{9,8},{10,11... | collective-permute-start | bytes 786440 | tf_op jit(solution)/shard_map/ppermute | solution.py:29

commit v8 on v7

--- a/solution.py
+++ b/solution.py
@@ -108,11 +108,10 @@
             out_ref[peer, h, 64:128] = imag
 
 
-def last_collision(scale, where_ref, own_ref, other_ref, y_ref, base_ref, out_ref, acc_ref):
-    core = where_ref[2]
+def last_collision(scale, s_ref, y_ref, base_ref, out_ref, acc_ref):
     pieces = [
-        ([s_ref[q, m] for m in range(2)], [8 * m + 2 * q + side for m in range(2)])
-        for s_ref, side in ((own_ref, core), (other_ref, 1 - core))
+        ([s_ref[side, q, m] for m in range(2)], [8 * m + 2 * q + side for m in range(2)])
+        for side in range(2)
         for q in range(4)
     ]
     row_times_column(pieces, y_ref, acc_ref)
@@ -439,15 +438,15 @@
     )(where, force, lg, strength, plan)
 
     t_rows = from_everyone(lax.all_gather(t2, "zm"), "zq")
-    t_other = swapped(t_rows, "c")
+    t_rows = lax.all_gather(t_rows, "c")
     out = call(
         functools.partial(last_collision, scale),
         shape(2, 64, 128, kind=f32),
         [pltpu.VMEM((128, 256), f32)],
-        [SMEM, VMEM, VMEM, VMEM, VMEM],
+        [VMEM, VMEM, VMEM],
         2 * 128 * 256 * 2048,
         2 << 20,
-    )(where, t_rows, t_other, y2, base)
+    )(t_rows, y2, base)
     return out.reshape(2, 2, orbitals, 128)
 
 

time: 120 us -> 118 us (0.983)
  starting transfers between devices: 25.3 us -> 18.5 us
  blocking collectives: 61.3 us -> 68 us
    ppermute x2 -> x1, starting transfers between devices: 11.9 us -> 5.19 us  [swapped(): return lax.ppermute(shard, axis, [(0, 1), (1, 0)])]
    all_gather x0 -> x1, blocking collectives: none -> 6.62 us  [shards(): t_rows = lax.all_gather(t_rows, 'c')]
    ppermute x2 -> x1, waiting for transfers between devices: 2.57 us -> 1.43 us  [swapped(): return lax.ppermute(shard, axis, [(0, 1), (1, 0)])]
  transfers between devices with their start and end apart: 4 -> 3, of which waited for: 3 -> 2; matrix products, arithmetic and copies ran while one was open for 1% -> 1% of each run, Pallas kernels for 7% -> 7%
where the time goes in v8:
time: 118 us; the launch traced here: 117 us
  blocking collectives  68 us (58%)
  Pallas kernels  19.6 us (17%)
  starting transfers between devices  18.5 us (16%)
  waiting for transfers between devices  8.48 us (7%)
  local copies, waits for them, and re-layouts  2.4 us (2%)
    all_gather x1, blocking collectives, shards(): pair = lax.all_gather(message, 'zh')  17.6 us
    all_gather x1, blocking collectives, shards(): s_rows = lax.all_gather(s_rows, 'zq')  16.2 us
    all_gather x1, blocking collectives, shards(): s_rows = lax.all_gather(pair[:, 264:], 'zm')  11.1 us
    pallas_call x1, Pallas kernels, shards(): call(build_steps, shape(8, 704, 1024), [pltpu.VMEM((8, 512, 640), bf16),...  8.47 us
    all_to_all x1, blocking collectives, from_everyone(): lax.all_to_all(jnp.broadcast_to(shard[None], (peers, *shard.shape)), axis...  8.36 us
    all_gather x1, blocking collectives, shards(): t_rows = from_everyone(lax.all_gather(t2, 'zm'), 'zq')  8.09 us
    all_to_all x1, waiting for transfers between devices, shards(): force = lax.all_to_all(c1, PLANE, 0, 0, tiled=True)  7.05 us
    all_to_all x1, starting transfers between devices, from_everyone(): lax.all_to_all(jnp.broadcast_to(shard[None], (peers, *shard.shape)), axis...  6.97 us
  transfers between devices with their start and end apart: 3, of which 2 were waited for; matrix products, arithmetic and copies ran while one was open for 1% of the time, Pallas kernels for 7%

profile of v8, /device:TPU:1, one launch (start us, length us, event | category | flops | bytes accessed | tf_op | source)
XLA Modules:
  0.0 117.3 jit_solution(1969467979863279450)
XLA Ops:
  0.0 1.7 %shard_map.46 = bf16[392,128]{1,0:T(8,128)(2,1)} custom-call(f32[2,2,64,128]{3,2,1,0:T(8,128)} %bitcast.27, f32[2,32]{1,0:T(2,128)} %damp_ref.1, f32[1,32]{1,0:T(1,128)} %bitcast.20), custom_call_target="tpu_custom_call" | custom-call | flops 327680 | bytes 409600 | tf_op jit(solution)/shard_map/pallas_call | solution.py:384
  1.7 17.6 %all-gather = bf16[784,128]{1,0:T(8,128)(2,1)S(1)} all-gather(bf16[392,128]{1,0:T(8,128)(2,1)} %shard_map.46), channel_id=2, replica_groups=mesh['y'=4,'x'=4,'zh'=2,'zm'=2,'zq'=4,'c'=2] {'zh'}, dimensions={0}, use_global_device_ids=true | all-gather | bytes 301056 | tf_op jit(solution)/shard_map/all_gather | solution.py:393
  19.3 1.6 %broadcast_in_dim.4 = bf16[16,2,264,128]{3,2,1,0:T(8,128)(2,1)} broadcast(bf16[2,264,128]{2,1,0:T(8,128)(2,1)S(1)} %slice.25), dimensions={1,2,3} | broadcast | bytes 2297856 | tf_op jit(solution)/shard_map/broadcast_in_dim | solution.py:24
  21.0 7.0 %all-to-all-start = ((bf16[16,2,264,128]{3,2,1,0:T(8,128)(2,1)}), bf16[16,2,264,128]{3,2,1,0:T(8,128)(2,1)S(1)}, u32[]{:S(2)}, u32[]{:S(2)}) async-start(bf16[16,2,264,128]{3,2,1,0:T(8,128)(2,1)} %broadcast_in_dim.4), calls=%async_computation | async-start | bytes 4325376 | tf_op jit(solution)/shard_map/all_to_all | solution.py:23
  28.0 11.1 %all-gather.1 = bf16[4,128,128]{2,1,0:T(8,128)(2,1)S(1)} all-gather(bf16[2,128,128]{2,1,0:T(8,128)(2,1)S(1)} %slice.24), channel_id=3, replica_groups=mesh['y'=4,'x'=4,'zh'=2,'zm'=2,'zq'=4,'c'=2] {'zm'}, dimensions={0}, use_global_device_ids=true | all-gather | bytes 196608 | tf_op jit(solution)/shard_map/all_gather | solution.py:396
  39.1 16.2 %all-gather.2 = bf16[8,2,128,128]{3,2,1,0:T(8,128)(2,1)S(1)} all-gather(bf16[2,2,128,128]{3,2,1,0:T(8,128)(2,1)S(1)} %bitcast.24), channel_id=4, replica_groups=mesh['y'=4,'x'=4,'zh'=2,'zm'=2,'zq'=4,'c'=2] {'zq'}, dimensions={0}, use_global_device_ids=true | all-gather | bytes 655360 | tf_op jit(solution)/shard_map/all_gather | solution.py:397
  55.3 5.2 %collective-permute-start = (bf16[4,2,2,128,128]{4,3,2,1,0:T(8,128)(2,1)S(1)}, bf16[4,2,2,128,128]{4,3,2,1,0:T(8,128)(2,1)S(1)}, u32[]{:S(2)}, u32[]{:S(2)}) collective-permute-start(bf16[4,2,2,128,128]{4,3,2,1,0:T(8,128)(2,1)S(1)} %bitcast.17), channel_id=1, source_target_pairs={{0,1},{1,0},{2,3},{3,2},{4,5},{5,4},{6,7},{7,6},{8,9},{9,8},{10,11... | collective-permute-start | bytes 1572872 | tf_op jit(solution)/shard_map/ppermute | solution.py:29
  60.5 0.1 pad_add_fusion.where_ref
  60.6 1.4 %collective-permute-done.other_ref = bf16[4,2,2,128,128]{4,3,2,1,0:T(8,128)(2,1)S(1)} collective-permute-done((bf16[4,2,2,128,128]{4,3,2,1,0:T(8,128)(2,1)S(1)}, bf16[4,2,2,128,128]{4,3,2,1,0:T(8,128)(2,1)S(1)}, u32[]{:S(2)}, u32[]{:S(2)}) %collective-permute-start) | collective-permute-done | bytes 524320 | tf_op jit(solution)/shard_map/ppermute | solution.py:29
  62.0 0.0 all-to-all-done.y_ref.lg_ref
  62.0 2.1 %shard_map.47 = bf16[16,2,128,128]{3,2,1,0:T(8,128)(2,1)} custom-call(s32[3]{0:T(128)S(1)} %pad_add_fusion.where_ref, bf16[4,2,2,128,128]{4,3,2,1,0:T(8,128)(2,1)S(1)} %bitcast.18, bf16[4,2,2,128,128]{4,3,2,1,0:T(8,128)(2,1)S(1)} %collective-permute-done.other_ref, bf16[16,2,264,128]{3,2,1,0:T(8,128)(2,1)S(1)} %all-to-all-done.y_ref.lg_ref), custom_call_target="tpu_custom_call" | custom-call | flops 268435456 | bytes 4194304 | tf_op jit(solution)/shard_map/pallas_call | solution.py:400
  64.1 6.4 %all-to-all-start.1 = ((bf16[16,2,128,128]{3,2,1,0:T(8,128)(2,1)}), bf16[16,2,128,128]{3,2,1,0:T(8,128)(2,1)S(1)}, u32[]{:S(2)}, u32[]{:S(2)}) async-start(bf16[16,2,128,128]{3,2,1,0:T(8,128)(2,1)} %shard_map.47), calls=%async_computation.1 | async-start | bytes 2097152 | tf_op jit(solution)/shard_map/all_to_all | solution.py:408
  70.5 0.1 fusion.1
  70.6 0.1 copy.6
  70.6 0.6 tile.4
  71.3 0.0 copy-start
  71.3 8.5 %shard_map.48.plan_hbm = bf16[8,704,1024]{2,1,0:T(8,128)(2,1)} custom-call(f32[64,64]{1,0:T(8,128)} %bitcast.26, f32[64,32]{1,0:T(8,128)} %bitcast.29), custom_call_target="tpu_custom_call" | custom-call | flops 536870912 | bytes 6291456 | tf_op jit(solution)/shard_map/pallas_call | solution.py:413
  79.8 7.1 %all-to-all-done.1.force_ref = bf16[16,2,128,128]{3,2,1,0:T(8,128)(2,1)S(1)} async-done(((bf16[16,2,128,128]{3,2,1,0:T(8,128)(2,1)}), bf16[16,2,128,128]{3,2,1,0:T(8,128)(2,1)S(1)}, u32[]{:S(2)}, u32[]{:S(2)}) %all-to-all-start.1) | async-done | bytes 1048608 | tf_op jit(solution)/shard_map/all_to_all | solution.py:408
  86.8 0.0 copy-done
  86.8 6.4 %shard_map.49 = (bf16[16,2,128,128]{3,2,1,0:T(8,128)(2,1)S(1)}, bf16[128,128]{1,0:T(8,128)(2,1)S(1)}, f32[128,128]{1,0:T(8,128)S(1)}) custom-call(s32[3]{0:T(128)S(1)} %pad_add_fusion.where_ref, bf16[16,2,128,128]{3,2,1,0:T(8,128)(2,1)S(1)} %all-to-all-done.1.force_ref, bf16[16,2,264,128]{3,2,1,0:T(8,128)(2,1)S(1)} %all-to-all-done.y_ref.lg_ref, ...), custom_call_target="tpu_custom_call" | custom-call | flops 1073741824 | bytes 10485760 | tf_op jit(solution)/shard_map/pallas_call | solution.py:430
  93.2 8.1 %all-gather.3 = bf16[256,128]{1,0:T(8,128)(2,1)S(1)} all-gather(bf16[128,128]{1,0:T(8,128)(2,1)S(1)} %get-tuple-element.8), channel_id=5, replica_groups=mesh['y'=4,'x'=4,'zh'=2,'zm'=2,'zq'=4,'c'=2] {'zm'}, dimensions={0}, use_global_device_ids=true | all-gather | bytes 98304 | tf_op jit(solution)/shard_map/all_gather | solution.py:440
  101.3 8.4 %all_to_all.15 = bf16[4,2,128,128]{3,2,1,0:T(8,128)(2,1)S(1)} all-to-all(bf16[4,2,128,128]{3,2,1,0:T(8,128)(2,1)S(1)} %broadcast_in_dim.5), channel_id=1, replica_groups=mesh['y'=4,'x'=4,'zh'=2,'zm'=2,'zq'=4,'c'=2] {'zq'}, dimensions={0} | all-to-all | bytes 524288 | tf_op jit(solution)/shard_map/all_to_all | solution.py:23
  109.7 6.6 %all-gather.4 = bf16[8,2,128,128]{3,2,1,0:T(8,128)(2,1)S(1)} all-gather(bf16[4,2,128,128]{3,2,1,0:T(8,128)(2,1)S(1)} %all_to_all.15), channel_id=6, replica_groups=mesh['y'=4,'x'=4,'zh'=2,'zm'=2,'zq'=4,'c'=2] {'c'}, dimensions={0}, use_global_device_ids=true | all-gather | bytes 786432 | tf_op jit(solution)/shard_map/all_gather | solution.py:441
  116.3 1.0 shard_map.50
  (5 shorter events, 0.1 us)
Async XLA Ops:
  21.0 41.0 %all-to-all-start = ((bf16[16,2,264,128]{3,2,1,0:T(8,128)(2,1)}), bf16[16,2,264,128]{3,2,1,0:T(8,128)(2,1)S(1)}, u32[]{:S(2)}, u32[]{:S(2)}) async-start(bf16[16,2,264,128]{3,2,1,0:T(8,128)(2,1)} %broadcast_in_dim.4), calls=%async_computation | async-start | bytes 4325376 | tf_op jit(solution)/shard_map/all_to_all | solution.py:23
  55.3 6.7 %collective-permute-start = (bf16[4,2,2,128,128]{4,3,2,1,0:T(8,128)(2,1)S(1)}, bf16[4,2,2,128,128]{4,3,2,1,0:T(8,128)(2,1)S(1)}, u32[]{:S(2)}, u32[]{:S(2)}) collective-permute-start(bf16[4,2,2,128,128]{4,3,2,1,0:T(8,128)(2,1)S(1)} %bitcast.17), channel_id=1, source_target_pairs={{0,1},{1,0},{2,3},{3,2},{4,5},{5,4},{6,7},{7,6},{8,9},{9,8},{10,11... | collective-permute-start | bytes 1572872 | tf_op jit(solution)/shard_map/ppermute | solution.py:29
  64.1 22.7 %all-to-all-start.1 = ((bf16[16,2,128,128]{3,2,1,0:T(8,128)(2,1)}), bf16[16,2,128,128]{3,2,1,0:T(8,128)(2,1)S(1)}, u32[]{:S(2)}, u32[]{:S(2)}) async-start(bf16[16,2,128,128]{3,2,1,0:T(8,128)(2,1)} %shard_map.47), calls=%async_computation.1 | async-start | bytes 2097152 | tf_op jit(solution)/shard_map/all_to_all | solution.py:408
  71.3 15.5 %copy-start = (f32[32]{0:T(128)S(1)}, f32[32]{0:T(128)}, u32[]{:S(2)}) copy-start(f32[32]{0:T(128)} %param.7) | copy-start | bytes 388

commit v9 on v8

--- a/solution.py
+++ b/solution.py
@@ -14,7 +14,6 @@
 PLANE = ("y", "x")
 f32, bf16 = jnp.float32, jnp.bfloat16
 VMEM = pl.BlockSpec(memory_space=pltpu.VMEM)
-SMEM = pl.BlockSpec(memory_space=pltpu.SMEM)
 HBM = pl.BlockSpec(memory_space=pltpu.HBM)
 
 
@@ -88,8 +87,8 @@
             acc_ref[...] += part
 
 
-def first_collision(scale, where_ref, own_ref, other_ref, y_ref, out_ref, acc_ref):
-    core = where_ref[2]
+def first_collision(scale, own_ref, other_ref, y_ref, out_ref, acc_ref):
+    core = lax.axis_index("c")
     pieces = [
         (
             [s_ref[q, m].reshape(256, 128) for m in range(2)],
@@ -212,7 +211,7 @@
 
 
 def predict(
-    where_ref, force_ref, lg_ref, coupling_ref, plan_hbm,
+    force_ref, lg_ref, coupling_ref, plan_hbm,
     y_ref, t_ref, base_ref,
     p_ref, last_ref, pc_ref, f_ref, s_ref, ends_ref, carry_ref, hom_ref, x_ref, sems,
 ):
@@ -229,7 +228,8 @@
     for copy in copies + [fetch(k) for k in range(8)]:
         copy.start()
 
-    j, h = where_ref[0], where_ref[1]
+    j = lax.axis_index("y") * lax.axis_size("x") + lax.axis_index("x")
+    h = lax.axis_index("zh")
     own_block, own_start = j // 2, pl.multiple_of((j % 2) * 128 + h * 64, 64)
     own_low = pl.multiple_of(own_start + 256, 64)
 
@@ -378,8 +378,6 @@
     orbitals = coupling.shape[0]
     horizon = damping.shape[0] * lax.axis_size(FIRST)
     scale = 1.0 / (horizon * math.sqrt(orbitals))
-    where = jnp.stack([lax.axis_index(axis) for axis in (PLANE, "zh", "c")]).astype(jnp.int32)
-
     strength = coupling.reshape(1, 32)
     message = call(
         compose,
@@ -401,10 +399,10 @@
         functools.partial(first_collision, scale),
         shape(16, 2, 128, 128),
         [pltpu.VMEM((256, 256), f32)],
-        [SMEM, VMEM, VMEM, VMEM],
+        [VMEM, VMEM, VMEM],
         2 * 256 * 256 * 2048,
         4 << 20,
-    )(where, s_rows, s_other, lg)
+    )(s_rows, s_other, lg)
     force = lax.all_to_all(c1, PLANE, 0, 0, tiled=True)
 
     parts = lg[:, :, 256:258].reshape(64, 128).astype(f32)
@@ -431,11 +429,11 @@
         predict,
         (shape(16, 2, 128, 128), shape(128, 128), shape(128, 128, kind=f32)),
         PRED_SCRATCH,
-        [SMEM] + [VMEM] * 3 + [HBM],
+        [VMEM] * 3 + [HBM],
         2 * 8 * 512 * 512 * 128 * 2,
         10 << 20,
         44,
-    )(where, force, lg, strength, plan)
+    )(force, lg, strength, plan)
 
     t_rows = from_everyone(lax.all_gather(t2, "zm"), "zq")
     t_rows = lax.all_gather(t_rows, "c")

time: 118 us -> 117 us (level)
  Pallas kernels: 19.6 us -> 17.5 us
    pallas_call x1, Pallas kernels: 2.08 us -> 0.52 us  [shards(): call(functools.partial(first_collision, scale), shape(16, 2, 128, 128), [...]
where the time goes in v9:
time: 117 us; the launch traced here: 116 us
  blocking collectives  68 us (58%)
  starting transfers between devices  18.5 us (16%)
  Pallas kernels  17.5 us (15%)
  waiting for transfers between devices  8.58 us (7%)
  local copies, waits for them, and re-layouts  3.39 us (3%)
    all_gather x1, blocking collectives, shards(): pair = lax.all_gather(message, 'zh')  17.6 us
    all_gather x1, blocking collectives, shards(): s_rows = lax.all_gather(s_rows, 'zq')  16.2 us
    all_gather x1, blocking collectives, shards(): s_rows = lax.all_gather(pair[:, 264:], 'zm')  11.1 us
    pallas_call x1, Pallas kernels, shards(): call(build_steps, shape(8, 704, 1024), [pltpu.VMEM((8, 512, 640), bf16),...  8.46 us
    all_to_all x1, blocking collectives, from_everyone(): lax.all_to_all(jnp.broadcast_to(shard[None], (peers, *shard.shape)), axis...  8.36 us
    all_gather x1, blocking collectives, shards(): t_rows = from_everyone(lax.all_gather(t2, 'zm'), 'zq')  8.09 us
    all_to_all x1, waiting for transfers between devices, shards(): force = lax.all_to_all(c1, PLANE, 0, 0, tiled=True)  7.06 us
    all_to_all x1, starting transfers between devices, from_everyone(): lax.all_to_all(jnp.broadcast_to(shard[None], (peers, *shard.shape)), axis...  6.97 us
  transfers between devices with their start and end apart: 3, of which 2 were waited for; matrix products, arithmetic and copies ran while one was open for 1% of the time, Pallas kernels for 7%

profile of v9, /device:TPU:1, one launch (start us, length us, event | category | flops | bytes accessed | tf_op | source)
XLA Modules:
  0.0 116.2 jit_solution(6347797297211546702)
XLA Ops:
  0.0 1.7 %shard_map.46 = bf16[392,128]{1,0:T(8,128)(2,1)} custom-call(f32[2,2,64,128]{3,2,1,0:T(8,128)} %bitcast.24, f32[2,32]{1,0:T(2,128)} %damp_ref.1, f32[1,32]{1,0:T(1,128)} %bitcast.17), custom_call_target="tpu_custom_call" | custom-call | flops 327680 | bytes 409600 | tf_op jit(solution)/shard_map/pallas_call | solution.py:382
  1.7 17.6 %all-gather = bf16[784,128]{1,0:T(8,128)(2,1)S(1)} all-gather(bf16[392,128]{1,0:T(8,128)(2,1)} %shard_map.46), channel_id=2, replica_groups=mesh['y'=4,'x'=4,'zh'=2,'zm'=2,'zq'=4,'c'=2] {'zh'}, dimensions={0}, use_global_device_ids=true | all-gather | bytes 301056 | tf_op jit(solution)/shard_map/all_gather | solution.py:391
  19.3 1.6 %broadcast_in_dim.4 = bf16[16,2,264,128]{3,2,1,0:T(8,128)(2,1)} broadcast(bf16[2,264,128]{2,1,0:T(8,128)(2,1)S(1)} %slice.25), dimensions={1,2,3} | broadcast | bytes 2297856 | tf_op jit(solution)/shard_map/broadcast_in_dim | solution.py:23
  21.0 7.0 %all-to-all-start = ((bf16[16,2,264,128]{3,2,1,0:T(8,128)(2,1)}), bf16[16,2,264,128]{3,2,1,0:T(8,128)(2,1)S(1)}, u32[]{:S(2)}, u32[]{:S(2)}) async-start(bf16[16,2,264,128]{3,2,1,0:T(8,128)(2,1)} %broadcast_in_dim.4), calls=%async_computation | async-start | bytes 4325376 | tf_op jit(solution)/shard_map/all_to_all | solution.py:22
  28.0 11.1 %all-gather.1 = bf16[4,128,128]{2,1,0:T(8,128)(2,1)S(1)} all-gather(bf16[2,128,128]{2,1,0:T(8,128)(2,1)S(1)} %slice.24), channel_id=3, replica_groups=mesh['y'=4,'x'=4,'zh'=2,'zm'=2,'zq'=4,'c'=2] {'zm'}, dimensions={0}, use_global_device_ids=true | all-gather | bytes 196608 | tf_op jit(solution)/shard_map/all_gather | solution.py:394
  39.1 16.2 %all-gather.2 = bf16[8,2,128,128]{3,2,1,0:T(8,128)(2,1)S(1)} all-gather(bf16[2,2,128,128]{3,2,1,0:T(8,128)(2,1)S(1)} %bitcast.21), channel_id=4, replica_groups=mesh['y'=4,'x'=4,'zh'=2,'zm'=2,'zq'=4,'c'=2] {'zq'}, dimensions={0}, use_global_device_ids=true | all-gather | bytes 655360 | tf_op jit(solution)/shard_map/all_gather | solution.py:395
  55.3 5.2 %collective-permute-start = (bf16[4,2,2,128,128]{4,3,2,1,0:T(8,128)(2,1)S(1)}, bf16[4,2,2,128,128]{4,3,2,1,0:T(8,128)(2,1)S(1)}, u32[]{:S(2)}, u32[]{:S(2)}) collective-permute-start(bf16[4,2,2,128,128]{4,3,2,1,0:T(8,128)(2,1)S(1)} %bitcast.15), channel_id=1, source_target_pairs={{0,1},{1,0},{2,3},{3,2},{4,5},{5,4},{6,7},{7,6},{8,9},{9,8},{10,11... | collective-permute-start | bytes 1572872 | tf_op jit(solution)/shard_map/ppermute | solution.py:28
  60.5 1.5 %collective-permute-done.other_ref = bf16[4,2,2,128,128]{4,3,2,1,0:T(8,128)(2,1)S(1)} collective-permute-done((bf16[4,2,2,128,128]{4,3,2,1,0:T(8,128)(2,1)S(1)}, bf16[4,2,2,128,128]{4,3,2,1,0:T(8,128)(2,1)S(1)}, u32[]{:S(2)}, u32[]{:S(2)}) %collective-permute-start) | collective-permute-done | bytes 524320 | tf_op jit(solution)/shard_map/ppermute | solution.py:28
  62.0 0.0 all-to-all-done.y_ref.lg_ref
  62.0 0.5 shard_map.47
  62.5 0.0 copy-start
  62.5 1.0 copy-done
  63.5 6.4 %all-to-all-start.1 = ((bf16[16,2,128,128]{3,2,1,0:T(8,128)(2,1)}), bf16[16,2,128,128]{3,2,1,0:T(8,128)(2,1)S(1)}, u32[]{:S(2)}, u32[]{:S(2)}) async-start(bf16[16,2,128,128]{3,2,1,0:T(8,128)(2,1)} %copy-done), calls=%async_computation.1 | async-start | bytes 2097152 | tf_op jit(solution)/shard_map/all_to_all | solution.py:406
  69.9 0.1 fusion.1
  70.0 0.1 copy.6
  70.1 0.6 tile.4
  70.7 0.0 copy-start.1
  70.7 8.5 %shard_map.48.plan_hbm = bf16[8,704,1024]{2,1,0:T(8,128)(2,1)} custom-call(f32[64,64]{1,0:T(8,128)} %bitcast.23, f32[64,32]{1,0:T(8,128)} %bitcast.26), custom_call_target="tpu_custom_call" | custom-call | flops 536870912 | bytes 6291456 | tf_op jit(solution)/shard_map/pallas_call | solution.py:411
  79.2 7.1 %all-to-all-done.1.force_ref = bf16[16,2,128,128]{3,2,1,0:T(8,128)(2,1)S(1)} async-done(((bf16[16,2,128,128]{3,2,1,0:T(8,128)(2,1)}), bf16[16,2,128,128]{3,2,1,0:T(8,128)(2,1)S(1)}, u32[]{:S(2)}, u32[]{:S(2)}) %all-to-all-start.1) | async-done | bytes 1048608 | tf_op jit(solution)/shard_map/all_to_all | solution.py:406
  86.3 0.0 copy-done.1
  86.3 5.8 %shard_map.49 = (bf16[16,2,128,128]{3,2,1,0:T(8,128)(2,1)S(1)}, bf16[128,128]{1,0:T(8,128)(2,1)S(1)}, f32[128,128]{1,0:T(8,128)S(1)}) custom-call(bf16[16,2,128,128]{3,2,1,0:T(8,128)(2,1)S(1)} %all-to-all-done.1.force_ref, bf16[16,2,264,128]{3,2,1,0:T(8,128)(2,1)S(1)} %all-to-all-done.y_ref.lg_ref, f32[1,32]{1,0:T(1,128)S(1)} %bitcast.18, ...), custom_call_target="tpu_custom_call" | custom-call | flops 1073741824 | bytes 10485760 | tf_op jit(solution)/shard_map/pallas_call | solution.py:428
  92.1 8.1 %all-gather.3 = bf16[256,128]{1,0:T(8,128)(2,1)S(1)} all-gather(bf16[128,128]{1,0:T(8,128)(2,1)S(1)} %get-tuple-element.8), channel_id=5, replica_groups=mesh['y'=4,'x'=4,'zh'=2,'zm'=2,'zq'=4,'c'=2] {'zm'}, dimensions={0}, use_global_device_ids=true | all-gather | bytes 98304 | tf_op jit(solution)/shard_map/all_gather | solution.py:438
  100.2 8.4 %all_to_all.15 = bf16[4,2,128,128]{3,2,1,0:T(8,128)(2,1)S(1)} all-to-all(bf16[4,2,128,128]{3,2,1,0:T(8,128)(2,1)S(1)} %broadcast_in_dim.5), channel_id=1, replica_groups=mesh['y'=4,'x'=4,'zh'=2,'zm'=2,'zq'=4,'c'=2] {'zq'}, dimensions={0} | all-to-all | bytes 524288 | tf_op jit(solution)/shard_map/all_to_all | solution.py:22
  108.6 6.6 %all-gather.4 = bf16[8,2,128,128]{3,2,1,0:T(8,128)(2,1)S(1)} all-gather(bf16[4,2,128,128]{3,2,1,0:T(8,128)(2,1)S(1)} %all_to_all.15), channel_id=6, replica_groups=mesh['y'=4,'x'=4,'zh'=2,'zm'=2,'zq'=4,'c'=2] {'c'}, dimensions={0}, use_global_device_ids=true | all-gather | bytes 786432 | tf_op jit(solution)/shard_map/all_gather | solution.py:439
  115.2 1.0 shard_map.50
  (5 shorter events, 0.1 us)
Async XLA Ops:
  21.0 41.0 %all-to-all-start = ((bf16[16,2,264,128]{3,2,1,0:T(8,128)(2,1)}), bf16[16,2,264,128]{3,2,1,0:T(8,128)(2,1)S(1)}, u32[]{:S(2)}, u32[]{:S(2)}) async-start(bf16[16,2,264,128]{3,2,1,0:T(8,128)(2,1)} %broadcast_in_dim.4), calls=%async_computation | async-start | bytes 4325376 | tf_op jit(solution)/shard_map/all_to_all | solution.py:22
  55.3 6.7 %collective-permute-start = (bf16[4,2,2,128,128]{4,3,2,1,0:T(8,128)(2,1)S(1)}, bf16[4,2,2,128,128]{4,3,2,1,0:T(8,128)(2,1)S(1)}, u32[]{:S(2)}, u32[]{:S(2)}) collective-permute-start(bf16[4,2,2,128,128]{4,3,2,1,0:T(8,128)(2,1)S(1)} %bitcast.15), channel_id=1, source_target_pairs={{0,1},{1,0},{2,3},{3,2},{4,5},{5,4},{6,7},{7,6},{8,9},{9,8},{10,11... | collective-permute-start | bytes 1572872 | tf_op jit(solution)/shard_map/ppermute | solution.py:28
  62.5 1.0 copy-start
  63.5 22.7 %all-to-all-start.1 = ((bf16[16,2,128,128]{3,2,1,0:T(8,128)(2,1)}), bf16[16,2,128,128]{3,2,1,0:T(8,128)(2,1)S(1)}, u32[]{:S(2)}, u32[]{:S(2)}) async-start(bf16[16,2,128,128]{3,2,1,0:T(8,128)(2,1)} %copy-done), calls=%async_computation.1 | async-start | bytes 2097152 | tf_op jit(solution)/shard_map/all_to_all | solution.py:406
  70.7 15.5 %copy-start.1 = (f32[32]{0:T(128)S(1)}, f32[32]{0:T(128)}, u32[]{:S(2)}) copy-start(f32[32]{0:T(128)} %param.7) | copy-start | bytes 388
